TPU v7x, 256 devices: a whole 4x4x8 slice. The times are simulated.
256 devices in a mesh: narrow: 8 (over x, z_lo), wide: 32 (over y, z_hi, core).
Axes of the slice: x: 4, y: 4, z: 8 (z_hi: 4, z_lo: 2; z = z_hi * 2 + z_lo), core: 2. Of those that a mesh axis runs over, the one named last changes fastest.
Arguments:
- basis: bfloat16 [128, 32, 512, 128], P(None, 'narrow', 'wide'), may hold values from -6 to 6
- rhs: bfloat16 [32, 512, 128], P('narrow', 'wide'), may hold values from -48 to 48
- coeffs: float32 [4, 32, 512, 128], P(None, 'narrow', 'wide'), may hold values from 0.25 to 4
- rows: int32 [4, 32, 512, 128], P(None, 'narrow', 'wide'), may hold values from 0 to 255
- signs: int32 [4, 32, 512, 128], P(None, 'narrow', 'wide'), may hold values from 0 to 1
- params: float32 [256, 4], P(('narrow', 'wide')), may hold values from 0.25 to 4
- order: int32 [256], replicated, may hold values from 0 to 255, each once
Outputs:
- fields: bfloat16 [256, 32, 512, 128], P(None, 'narrow', 'wide')
Inputs may be any that keep to these rules, and one draw needn't show every extreme that they name: `order`: each point number appears exactly once.
All inputs are finite; a program needn't handle non-finite values.
Results may differ from a plain program's by a relative error of at most 0.0056.
Values may be sent and summed in bfloat16 or wider, within the bound.
No kernel may reach another device: no remote copies, remote signals or barrier semaphores. Data moves between devices by JAX's collectives and lax.ppermute only.
A program may use at most 64 MiB of HBM per device.

v0:
```python
import jax
import jax.numpy as jnp
from jax import lax
from jax.sharding import PartitionSpec as P

K = 128
M = 1024
TERMS = 4
NNZ = 4


def extended(cells, sides, width):
    for axis, dim in sides:
        count = lax.axis_size(axis)
        ends = count - 1
        head = lax.slice_in_dim(cells, 0, width, axis=dim)
        tail = lax.slice_in_dim(cells, cells.shape[dim] - width, cells.shape[dim], axis=dim)
        cells = jnp.concatenate(
            [
                lax.ppermute(tail, axis, [(i, (i + 1) % count) for i in range(ends)]),
                cells,
                lax.ppermute(head, axis, [((i + 1) % count, i) for i in range(ends)]),
            ],
            axis=dim,
        )
    return cells


def column_products(sketched, sketched_rhs):
    dims = (((0,), (0,)), ((), ()))
    gram_matrix = lax.dot_general(
        sketched,
        sketched,
        dims,
        precision=lax.Precision.HIGHEST,
        preferred_element_type=jnp.float32,
    )
    projected = lax.dot_general(
        sketched,
        sketched_rhs,
        dims,
        precision=lax.Precision.HIGHEST,
        preferred_element_type=jnp.float32,
    )
    return (gram_matrix, projected)


def solve_points(point_params, gram_matrix, projected):
    gram_blocks = gram_matrix.reshape(TERMS, K, TERMS, K)
    proj_blocks = projected.reshape(TERMS, K)
    pair_weight = point_params[:, :, None] * point_params[:, None, :]
    normal = jnp.einsum("pqr,qirj->pij", pair_weight, gram_blocks, precision=lax.Precision.HIGHEST)
    right_side = jnp.einsum("pq,qi->pi", point_params, proj_blocks, precision=lax.Precision.HIGHEST)
    lower_factor = jnp.linalg.cholesky(normal)
    forward = lax.linalg.triangular_solve(
        lower_factor, right_side[:, :, None], left_side=True, lower=True
    )
    solved = lax.linalg.triangular_solve(
        lower_factor, forward, left_side=True, lower=True, transpose_a=True
    )
    return solved[:, :, 0]


def per_device(basis, rhs, coeffs, rows, signs, params, order):
    cell_count = basis.shape[1] * basis.shape[2] * basis.shape[3]
    padded = extended(basis, (("narrow", 1), ("wide", 2)), 1).astype(jnp.float32)
    centre = padded[:, 1:-1, 1:-1, :]
    along_x = 2.0 * centre - padded[:, :-2, 1:-1, :] - padded[:, 2:, 1:-1, :]
    along_y = 2.0 * centre - padded[:, 1:-1, :-2, :] - padded[:, 1:-1, 2:, :]
    z_padded = jnp.pad(centre, ((0, 0), (0, 0), (0, 0), (1, 1)))
    along_z = 2.0 * centre - z_padded[..., :-2] - z_padded[..., 2:]
    terms = jnp.stack(
        [coeffs[0] * centre, coeffs[1] * along_x, coeffs[2] * along_y, coeffs[3] * along_z]
    )
    terms = terms.astype(jnp.bfloat16).reshape(TERMS * K, cell_count)
    row_block = M // NNZ
    flat_rows = rows.reshape(NNZ, cell_count)
    sign_values = ((2 * signs - 1).astype(jnp.float32) * 0.5).reshape(NNZ, cell_count)
    flat_rhs = rhs.reshape(cell_count)
    block_cells = max(min(1024, cell_count), cell_count // 16)
    block_count = cell_count // block_cells
    row_slots = lax.broadcasted_iota(jnp.int32, (1, row_block, 1), 1)

    def accumulate(turn_index, carry):
        sketch_sum, rhs_sum = carry
        offset = turn_index * block_cells
        hashed_rows = lax.dynamic_slice_in_dim(flat_rows, offset, block_cells, 1)
        hashed_signs = lax.dynamic_slice_in_dim(sign_values, offset, block_cells, 1)
        hashed = jnp.where(row_slots == hashed_rows[:, None, :], hashed_signs[:, None, :], 0.0)
        hashed = hashed.astype(jnp.bfloat16).reshape(M, block_cells)
        columns = lax.dynamic_slice_in_dim(terms, offset, block_cells, 1)
        sketch_sum = sketch_sum + lax.dot_general(
            hashed, columns, (((1,), (1,)), ((), ())), preferred_element_type=jnp.float32
        )
        source = lax.dynamic_slice_in_dim(flat_rhs, offset, block_cells, 0)
        rhs_sum = rhs_sum + jnp.dot(hashed, source, preferred_element_type=jnp.float32)
        return (sketch_sum, rhs_sum)

    start = (jnp.zeros((M, TERMS * K), jnp.float32), jnp.zeros((M,), jnp.float32))
    sketched, sketched_rhs = lax.fori_loop(0, block_count, accumulate, start)
    sketched, sketched_rhs = lax.psum((sketched, sketched_rhs), ("narrow", "wide"))
    gram_matrix, projected = column_products(sketched, sketched_rhs)
    own_coef = solve_points(params, gram_matrix, projected).astype(jnp.bfloat16)
    all_coef = lax.all_gather(own_coef, ("narrow", "wide"), axis=0, tiled=True)
    point_total = all_coef.shape[0]
    picker = (order[:, None] == lax.broadcasted_iota(jnp.int32, (1, point_total), 1)).astype(
        jnp.bfloat16
    )
    picked = jnp.dot(picker, all_coef, preferred_element_type=jnp.float32).astype(jnp.bfloat16)
    fields = jnp.dot(picked, basis.reshape(K, cell_count), preferred_element_type=jnp.float32)
    return fields.astype(jnp.bfloat16).reshape(
        point_total, basis.shape[1], basis.shape[2], basis.shape[3]
    )


def solution(mesh):
    in_specs = (
        P(None, "narrow", "wide", None),
        P("narrow", "wide", None),
        P(None, "narrow", "wide", None),
        P(None, "narrow", "wide", None),
        P(None, "narrow", "wide", None),
        P(("narrow", "wide"), None),
        P(),
    )
    out_specs = P(None, "narrow", "wide", None)
    return jax.shard_map(
        per_device, mesh=mesh, in_specs=in_specs, out_specs=out_specs, check_vma=False
    )
```

profile of v0, /device:TPU:1, one launch (start us, length us, event | category | flops | bytes accessed | tf_op | source)
XLA Modules:
  0.0 799.9 jit_solution(9524437281529108941)
XLA Ops:
  6.5 1.6 fusion.34
  8.1 0.9 copy.40
  9.0 5.1 collective-permute-start
  14.3 1.3 collective-permute-start.1
  15.8 8.4 %collective-permute-done = bf16[128,1,16,128]{3,0,2,1:T(8,128)(2,1)} collective-permute-done((bf16[128,1,16,128]{3,0,2,1:T(8,128)(2,1)}, bf16[128,1,16,128]{3,0,2,1:T(8,128)(2,1)}, u32[]{:S(2)}, u32[]{:S(2)}) %collective-permute-start) | collective-permute-done | bytes 524320 | tf_op jit(solution)/shard_map/ppermute | solution.py:20
  24.3 1.1 constant_dynamic-update-slice_fusion.2
  25.4 1.5 constant_dynamic-update-slice_fusion.1
  26.9 10.0 %collective-permute-done.1 = bf16[128,1,16,128]{3,0,2,1:T(8,128)(2,1)S(1)} collective-permute-done((bf16[128,1,16,128]{3,0,2,1:T(8,128)(2,1)S(1)}, bf16[128,1,16,128]{3,0,2,1:T(8,128)(2,1)S(1)}, u32[]{:S(2)}, u32[]{:S(2)}) %collective-permute-start.1) | collective-permute-done | bytes 524320 | tf_op jit(solution)/shard_map/ppermute | solution.py:22
  37.0 6.3 collective-permute-start.2
  43.3 1.9 collective-permute-start.3
  45.3 0.6 collective-permute-done.2
  46.0 7.4 collective-permute-done.3
  53.3 0.6 maximum_convert_fusion
  53.9 3.1 fusion.14
  57.0 2.2 fusion.19
  59.2 3.8 pad_maximum_fusion
  63.0 12.0 %copy.17 = bf16[4,128,4,16,128]{4,3,2,1,0:T(8,128)(2,1)} copy(bf16[4,128,4,16,128]{4,1,3,2,0:T(8,128)(2,1)} %pad_maximum_fusion) | data formatting | bytes 16777216 | tf_op jit(solution)/shard_map/stack | solution.py:72
  75.1 13.3 %convert_element_type.36 = bf16[512,8192]{1,0:T(8,128)(2,1)} reshape(bf16[4,128,4,16,128]{4,3,2,1,0:T(8,128)(2,1)} %copy.17) | data formatting | bytes 16777216 | tf_op jit(solution)/shard_map/convert_element_type | solution.py:75
  88.4 50.1 %while.16 = (s32[]{:T(128)}, f32[1024,512]{1,0:T(8,128)}, f32[1024]{0:T(1024)S(1)}, s32[4,8192]{1,0:T(4,128)S(1)}, bf16[4,8192]{1,0:T(4,128)(2,1)S(1)}, /*index=...) while((s32[]{:T(128)}, f32[1024,512]{1,0:T(8,128)}, ...), condition=%wide.region_1.2_spmd.clone, body=%wide.region_0.1_spmd.clone.sunk | while | flops 1078986752 | bytes 11651254 | solution.py:100
  88.4 0.4 fusion.60
  88.8 3.8 select_add_fusion.4
  92.7 0.7 dynamic_slice.43
  93.4 0.6 fusion.61
  94.1 0.4 fusion.60
  94.5 4.5 select_add_fusion.4
  99.0 0.7 dynamic_slice.43
  99.7 0.6 fusion.61
  100.4 0.4 fusion.60
  100.8 4.5 select_add_fusion.4
  105.4 0.7 dynamic_slice.43
  106.1 0.6 fusion.61
  106.8 0.4 fusion.60
  107.2 4.5 select_add_fusion.4
  111.7 0.7 dynamic_slice.43
  112.4 0.6 fusion.61
  113.1 0.4 fusion.60
  113.5 4.5 select_add_fusion.4
  118.1 0.7 dynamic_slice.43
  118.8 0.6 fusion.61
  119.5 0.4 fusion.60
  119.9 4.5 select_add_fusion.4
  124.4 0.7 dynamic_slice.43
  125.1 0.6 fusion.61
  125.8 0.4 fusion.60
  126.2 4.5 select_add_fusion.4
  130.8 0.7 dynamic_slice.43
  131.5 0.6 fusion.61
  132.2 0.4 fusion.60
  132.6 4.5 select_add_fusion.4
  137.1 0.7 dynamic_slice.43
  137.8 0.6 fusion.61
  138.6 78.1 %psum.15 = f32[1024]{0:T(1024)S(1)} all-reduce(f32[1024]{0:T(1024)S(1)} %get-tuple-element.146), channel_id=1, replica_groups=mesh['narrow'=8,'wide'=32] {'narrow','wide'}, use_global_device_ids=true, to_apply=%region_5.6 | all-reduce | flops 1024 | bytes 8192 | tf_op jit(solution)/shard_map/psum | solution.py:101
  216.7 186.0 %all-reduce.3.cloned.1.call-done = f32[1024,512]{1,0:T(8,128)} async-done(((f32[1024,512]{1,0:T(8,128)}), f32[1024,512]{1,0:T(8,128)}) %all-reduce.3.cloned.1.call-update) | async-done | bytes 2097168 | tf_op jit(solution)/shard_map/psum | solution.py:101
  402.7 5.7 fusion.36
  408.4 1.3 reshape.187
  409.7 2.7 convolution_bitcast_fusion
  412.7 11.7 %custom-call.9 = f32[1,128,128]{2,1,0:T(8,128)S(1)} custom-call(f32[1,128,128]{2,1,0:T(8,128)S(1)} %fusion.29), custom_call_target="Cholesky" | custom-call | tf_op jit(solution)/shard_map/jit(cholesky)/cholesky | solution.py:54
  424.4 0.6 compare_reduce_fusion
  425.1 0.7 fusion.24
  425.7 9.8 %custom-call.10 = f32[1,1,128,128]{2,3,1,0:T(8,128)S(1)} custom-call(f32[1,1,128,128]{3,2,1,0:T(8,128)S(1)} %fusion.24), custom_call_target="InvertDiagBlocksLowerTriangular" | custom-call | tf_op jit(solution)/shard_map/triangular_solve | solution.py:58
  435.5 1.5 fusion.37
  437.5 344.6 %all-gather.1 = bf16[256,1,128]{2,1,0:T(2,128)(2,1)S(1)} all-gather(bf16[1,1,128]{2,1,0:T(2,128)(2,1)S(1)} %fusion.21), channel_id=2, replica_groups=mesh['narrow'=8,'wide'=32] {'narrow','wide'}, dimensions={0}, use_global_device_ids=true | all-gather | bytes 65792 | tf_op jit(solution)/shard_map/all_gather | solution.py:104
  782.1 5.6 fusion.13
  787.7 5.4 copy.27
  (81 shorter events, 1.6 us)
Async XLA Ops:
  6.5 18.8 %copy-start.1 = (bf16[128,4,16,128]{3,2,1,0:T(8,128)(2,1)S(1)}, bf16[128,4,16,128]{3,2,1,0:T(8,128)(2,1)}, u32[]{:S(2)}) copy-start(bf16[128,4,16,128]{3,2,1,0:T(8,128)(2,1)} %param.9) | copy-start | bytes 6291460
  6.5 9.1 %copy-start.2 = (s32[4,4,16,128]{3,2,1,0:T(8,128)S(1)}, s32[4,4,16,128]{3,2,1,0:T(8,128)}, u32[]{:S(2)}) copy-start(s32[4,4,16,128]{3,2,1,0:T(8,128)} %param.13) | copy-start | bytes 393220
  6.5 9.2 %copy-start.3 = (s32[4,4,16,128]{3,2,1,0:T(8,128)S(1)}, s32[4,4,16,128]{3,2,1,0:T(8,128)}, u32[]{:S(2)}) copy-start(s32[4,4,16,128]{3,2,1,0:T(8,128)} %param.12) | copy-start | bytes 393220
  6.5 396.1 %all-reduce.3.cloned.1.call-start = ((), (), s32[]{:S(2)}) async-start(), calls=%async_computation | async-start | bytes 4194304 | tf_op jit(solution)/shard_map/psum | solution.py:101
  9.0 15.3 %collective-permute-start = (bf16[128,1,16,128]{3,0,2,1:T(8,128)(2,1)}, bf16[128,1,16,128]{3,0,2,1:T(8,128)(2,1)}, u32[]{:S(2)}, u32[]{:S(2)}) collective-permute-start(bf16[128,1,16,128]{3,0,2,1:T(8,128)(2,1)} %copy.40), channel_id=1, source_target_pairs={{0,32},{32,64},{64,96},{96,128},{128,160},{160,192},{192,224},{1,3... | collective-permute-start | bytes 1572872 | tf_op jit(solution)/shard_map/ppermute | solution.py:20
  14.3 22.6 %collective-permute-start.1 = (bf16[128,1,16,128]{3,0,2,1:T(8,128)(2,1)S(1)}, bf16[128,1,16,128]{3,0,2,1:T(8,128)(2,1)S(1)}, u32[]{:S(2)}, u32[]{:S(2)}) collective-permute-start(bf16[128,1,16,128]{3,0,2,1:T(8,128)(2,1)S(1)} %copy.41), channel_id=1, source_target_pairs={{32,0},{64,32},{96,64},{128,96},{160,128},{192,160},{224,192},{33,... | collective-permute-start | bytes 1572872 | tf_op jit(solution)/shard_map/ppermute | solution.py:22
  25.4 19.9 %copy-start.4 = (f32[4,4,16,128]{3,2,1,0:T(8,128)S(1)}, f32[4,4,16,128]{3,2,1,0:T(8,128)}, u32[]{:S(2)}) copy-start(f32[4,4,16,128]{3,2,1,0:T(8,128)} %param.11) | copy-start | bytes 393220
  37.0 8.9 %collective-permute-start.2 = (bf16[128,6,1,128]{3,0,2,1:T(8,128)(2,1)S(1)}, bf16[128,6,1,128]{3,0,2,1:T(8,128)(2,1)S(1)}, u32[]{:S(2)}, u32[]{:S(2)}) collective-permute-start(bf16[128,6,1,128]{3,0,2,1:T(8,128)(2,1)S(1)} %get-tuple-element.191), channel_id=1, source_target_pairs={{0,1},{1,2},{2,3},{3,4},{4,5},{5,6},{6,7},{7,8},{8,9},{9,10},{10,1... | collective-permute-start | bytes 589832 | tf_op jit(solution)/shard_map/ppermute | solution.py:20
  43.3 10.0 %collective-permute-start.3 = (bf16[128,6,1,128]{3,0,2,1:T(8,128)(2,1)S(1)}, bf16[128,6,1,128]{3,0,2,1:T(8,128)(2,1)S(1)}, u32[]{:S(2)}, u32[]{:S(2)}) collective-permute-start(bf16[128,6,1,128]{3,0,2,1:T(8,128)(2,1)S(1)} %get-tuple-element.192), channel_id=1, source_target_pairs={{1,0},{2,1},{3,2},{4,3},{5,4},{6,5},{7,6},{8,7},{9,8},{10,9},{11,1... | collective-permute-start | bytes 589832 | tf_op jit(solution)/shard_map/ppermute | solution.py:22
  88.4 50.1 %copy-start.5 = (f32[1,4]{1,0:T(1,128)S(1)}, f32[1,4]{1,0:T(1,128)}, u32[]{:S(2)}) copy-start(f32[1,4]{1,0:T(1,128)} %param.14) | copy-start | bytes 52
  408.4 27.2 %copy-start = (f32[1024,512]{1,0:T(8,128)S(1)}, f32[1024,512]{1,0:T(8,128)}, u32[]{:S(2)}) copy-start(f32[1024,512]{1,0:T(8,128)} %all-reduce.3.cloned.1.call-done) | copy-start | bytes 6291460
  408.4 373.7 %copy-start.6 = (s32[256]{0:T(256)S(1)}, s32[256]{0:T(256)}, u32[]{:S(2)}) copy-start(s32[256]{0:T(256)} %param.15) | copy-start | bytes 3076
Sparse Core Ops, SparseCore 0:
  138.6 263.9 all-reduce.2
where the time goes:
time: 801 us; the launch traced here: 800 us
  blocking collectives  423 us (53%)
  waiting for transfers between devices  213 us (27%)
  matrix products  56.7 us (7%)
  local copies, waits for them, and re-layouts  43.4 us (5%)
  other arithmetic  36 us (4%)
  starting transfers between devices  14.7 us (2%)
  between operations  13.6 us (2%)
    all_gather x1, blocking collectives, per_device(): all_coef = lax.all_gather(own_coef, ('narrow', 'wide'), axis=0, tiled=True)  345 us
    psum x1, waiting for transfers between devices, per_device(): lax.psum((sketched, sketched_rhs), ('narrow', 'wide'))  186 us
    psum x1, blocking collectives, per_device(): lax.psum((sketched, sketched_rhs), ('narrow', 'wide'))  78.1 us
    dot_general x8, matrix products, accumulate(): lax.dot_general(hashed, columns, (((1,), (1,)), ((), ())), preferred_elem...  35.6 us
    ppermute x2, waiting for transfers between devices, extended(): lax.ppermute(head, axis, [((i + 1) % count, i) for i in range(ends)])  17.4 us
  transfers between devices with their start and end apart: 5, of which 5 were waited for; matrix products, arithmetic and copies ran while one was open for 0% of the time, Pallas kernels for 0%

commit v1 on v0

v1 whole, which is shorter than its diff:
```python
import jax
import jax.numpy as jnp
from jax import lax
from jax.experimental import pallas as pl
from jax.experimental.pallas import tpu as pltpu
from jax.sharding import Mesh
from jax.sharding import PartitionSpec as P

K = 128
M = 1024
TERMS = 4
NNZ = 4
ROWS = M // NNZ
NX = 4
NY = 16
NZ = 128
CELLS = NY * NZ
TALL = TERMS * K + 16
CHIPS = 128
CHUNK = 24
POINTS = 256
TOL2 = 1e-10
MAX_ROUNDS = 256

f32 = jnp.float32
bf16 = jnp.bfloat16


def put_hash(hash_ref, lane, row_of, sign_of):
    slots = lax.broadcasted_iota(jnp.int32, (ROWS, NZ), 0)
    for j in range(NNZ):
        chosen = jnp.where(slots == row_of(j), sign_of(j), 0.0)
        hash_ref[j * ROWS:(j + 1) * ROWS, pl.ds(lane, NZ)] = chosen.astype(bf16)


def nt(a, b):
    return lax.dot_general(a, b, (((1,), (1,)), ((), ())), preferred_element_type=f32)


def in_two(source):
    high = source.astype(bf16).astype(f32)
    return (high + pltpu.roll(source - high, 2, 0)).astype(bf16)


def sketch_body(basis_ref, rhs_ref, co_ref, rows_ref, signs_ref, acc_ref, bt_ref, flat, pad, terms, hashes, source_ref):
    def widen(i, _):
        k = pl.multiple_of(i * 8, 8)
        flat[pl.ds(pl.multiple_of(k * NX * NY, 512), 512), :] = (
            basis_ref[pl.ds(k, 8)].astype(f32).reshape(8 * NX * NY, NZ)
        )
        return 0

    lax.fori_loop(0, K // 8, widen, 0)
    pad[0] = jnp.zeros((K, (NY + 2) * NZ), f32)
    pad[NX + 1] = jnp.zeros((K, (NY + 2) * NZ), f32)
    for x in range(NX):
        pad[x + 1, :, 0:NZ] = jnp.zeros((K, NZ), f32)
        pad[x + 1, :, (NY + 1) * NZ:] = jnp.zeros((K, NZ), f32)

    def turn(i, _):
        x = i // NY
        y = i % NY
        tile = flat[pl.ds(i, K, stride=NX * NY), :]
        pad[x + 1, :, pl.ds(pl.multiple_of((y + 1) * NZ, NZ), NZ)] = tile
        bt_ref[x, :, pl.ds(pl.multiple_of(y * NZ, NZ), NZ)] = tile.astype(bf16)
        return 0

    lax.fori_loop(0, NX * NY, turn, 0)
    lane = lax.broadcasted_iota(jnp.int32, (K, NZ), 1)

    def plane(x, _):
        source_ref[...] = rhs_ref[x].astype(f32)

        def group(y, _):
            here = pl.multiple_of(y * NZ, NZ)
            above = pl.multiple_of(y * NZ + NZ, NZ)
            v = pad[x + 1, :, pl.ds(above, NZ)]
            v2 = v + v
            along_x = v2 - pad[x, :, pl.ds(above, NZ)] - pad[x + 2, :, pl.ds(above, NZ)]
            along_y = v2 - pad[x + 1, :, pl.ds(here, NZ)] - pad[x + 1, :, pl.ds(pl.multiple_of(y * NZ + 2 * NZ, NZ), NZ)]
            lower = jnp.where(lane == 0, 0.0, pltpu.roll(v, 1, 1))
            upper = jnp.where(lane == NZ - 1, 0.0, pltpu.roll(v, NZ - 1, 1))
            along_z = v2 - lower - upper
            for q, t in enumerate((v, along_x, along_y, along_z)):
                terms[q * K:(q + 1) * K, pl.ds(here, NZ)] = (co_ref[q, x, pl.ds(y, 1), :] * t).astype(bf16)
            source = source_ref[pl.ds(y, 1), :]
            top = lax.broadcasted_iota(jnp.int32, (16, NZ), 0) == 0
            terms[TERMS * K:TALL, pl.ds(here, NZ)] = jnp.where(top, source, 0.0).astype(bf16)
            put_hash(
                hashes,
                here,
                lambda j: rows_ref[j, x, pl.ds(y, 1), :],
                lambda j: signs_ref[j, x, pl.ds(y, 1), :].astype(f32) - 0.5,
            )
            return 0

        lax.fori_loop(0, NY, group, 0)
        got = nt(terms[...], hashes[...])

        @pl.when(x == 0)
        def _():
            acc_ref[...] = got

        @pl.when(x > 0)
        def _():
            acc_ref[...] += got

        return 0

    lax.fori_loop(0, NX, plane, 0)


def sketch(basis, rhs, coeffs, rows, signs):
    return pl.pallas_call(
        sketch_body,
        out_shape=(
            jax.ShapeDtypeStruct((TALL, M), f32),
            jax.ShapeDtypeStruct((NX, K, CELLS), bf16),
        ),
        scratch_shapes=[
            pltpu.VMEM((K * NX * NY, NZ), f32),
            pltpu.VMEM((NX + 2, K, (NY + 2) * NZ), f32),
            pltpu.VMEM((TALL, CELLS), bf16),
            pltpu.VMEM((M, CELLS), bf16),
            pltpu.VMEM((NY, NZ), f32),
        ],
        compiler_params=pltpu.CompilerParams(vmem_limit_bytes=56 << 20),
        name="sketch",
    )(basis, rhs, coeffs, rows, signs)


def edge_body(core_ref, acc_in, bt_ref, xl_ref, xu_ref, yl_ref, yu_ref, own_ref, other_ref, acc, terms, hashes):
    acc[...] = acc_in[...]

    def one(info, plane_x, lane_in, y_info, place):
        v = bt_ref[plane_x, :, pl.ds(lane_in, NZ)].astype(f32)
        terms[:, pl.ds(place, NZ)] = (-info[2 * NNZ, pl.ds(y_info, 1), :] * v).astype(bf16)
        put_hash(
            hashes,
            place,
            lambda j: info[j, pl.ds(y_info, 1), :].astype(jnp.int32),
            lambda j: info[NNZ + j, pl.ds(y_info, 1), :] - 0.5,
        )

    for info, plane_x in ((xl_ref, 0), (xu_ref, NX - 1)):
        def group(y, _):
            here = pl.multiple_of(y * NZ, NZ)
            one(info, plane_x, here, y, here)
            return 0

        lax.fori_loop(0, NY, group, 0)
        acc[K:2 * K, :] += nt(terms[...], hashes[...])
    for x in range(NX):
        one(yl_ref, x, 0, x, x * NZ)
        one(yu_ref, x, (NY - 1) * NZ, x, (NX + x) * NZ)
    acc[2 * K:3 * K, :] += nt(terms[:, :2 * NX * NZ], hashes[:, :2 * NX * NZ])

    c = core_ref[0]
    row = lax.broadcasted_iota(jnp.int32, (8, NZ), 0)

    def split(g, _):
        mine = pl.multiple_of(c * 2 * K + g * 16, 16)
        theirs = pl.multiple_of((1 - c) * 2 * K + g * 16, 16)
        for l in range(M // NZ):
            own_ref[g * 8 + l, 0:16, :] = acc[pl.ds(mine, 16), l * NZ:(l + 1) * NZ]
            other_ref[g * 8 + l, 0:16, :] = acc[pl.ds(theirs, 16), l * NZ:(l + 1) * NZ].astype(bf16)
            own_ref[g * 8 + l, 16:24, :] = jnp.zeros((8, NZ), f32)
            other_ref[g * 8 + l, 16:24, :] = jnp.zeros((8, NZ), bf16)
        return 0

    lax.fori_loop(0, 2 * K // 16, split, 0)
    for l in range(M // NZ):
        source = jnp.where(row == 0, acc[TERMS * K:TERMS * K + 8, l * NZ:(l + 1) * NZ], 0.0)
        own_ref[l, 16:24, :] = source
        other_ref[l, 16:24, :] = in_two(source)


def edges(core, acc, bt, infos):
    vm = pl.BlockSpec(memory_space=pltpu.VMEM)
    return pl.pallas_call(
        edge_body,
        in_specs=[pl.BlockSpec(memory_space=pltpu.SMEM)] + [vm] * 6,
        out_shape=(
            jax.ShapeDtypeStruct((CHIPS, CHUNK, NZ), f32),
            jax.ShapeDtypeStruct((CHIPS, CHUNK, NZ), bf16),
        ),
        scratch_shapes=[
            pltpu.VMEM((TALL, M), f32),
            pltpu.VMEM((K, CELLS), bf16),
            pltpu.VMEM((M, CELLS), bf16),
        ],
        compiler_params=pltpu.CompilerParams(vmem_limit_bytes=56 << 20),
        name="edges",
    )(core, acc, bt, *infos)


def merge_body(own_ref, got_ref, out_ref):
    def add(i, _):
        at = pl.ds(pl.multiple_of(i * 8, 8), 8)
        out_ref[at, 0:16, :] = (own_ref[at, 0:16, :] + got_ref[at, 0:16, :].astype(f32)).astype(bf16)
        out_ref[at, 16:24, :] = jnp.zeros((8, 8, NZ), bf16)
        return 0

    lax.fori_loop(0, CHIPS // 8, add, 0)
    row = lax.broadcasted_iota(jnp.int32, (8, NZ), 0)
    for l in range(M // NZ):
        got = got_ref[l, 16:24, :].astype(f32)
        source = own_ref[l, 16:24, :] + (got + pltpu.roll(got, 6, 0))
        out_ref[l, 16:24, :] = in_two(jnp.where(row == 0, source, 0.0))


def merge(own, got):
    return pl.pallas_call(
        merge_body,
        out_shape=jax.ShapeDtypeStruct((CHIPS, CHUNK, NZ), bf16),
        name="merge",
    )(own, got)


def total_body(params_ref, parts_ref, out_ref):
    def add(i, carry):
        a, b = carry
        m = i * 8
        for s in range(8):
            a = a + parts_ref[m + s, 0:16, :].astype(f32)
            b = b + parts_ref[m + s, 16:24, :].astype(f32)
        return (a, b)

    a, b = lax.fori_loop(0, CHIPS // 8, add, (jnp.zeros((16, NZ), f32), jnp.zeros((8, NZ), f32)))
    lane = lax.broadcasted_iota(jnp.int32, (8, NZ), 1)
    row = lax.broadcasted_iota(jnp.int32, (8, NZ), 0)
    weights = jnp.zeros((8, NZ), f32)
    for q in range(TERMS):
        weights = jnp.where((row == 1) & (lane == q), params_ref[0, q], weights)
    high = weights.astype(bf16).astype(f32)
    rest = weights - high
    mid = rest.astype(bf16).astype(f32)
    low = (rest - mid).astype(bf16).astype(f32)
    b = jnp.where(row == 0, b + pltpu.roll(b, 6, 0), 0.0)
    b = in_two(b).astype(f32) + (high + pltpu.roll(mid, TERMS, 1) + pltpu.roll(low, 2 * TERMS, 1))
    a = a.astype(bf16)
    b = b.astype(bf16)

    def spread(m, _):
        out_ref[m, 0:16, :] = a
        out_ref[m, 16:24, :] = b
        return 0

    lax.fori_loop(0, CHIPS, spread, 0, unroll=8)


def total(params, parts):
    vm = pl.BlockSpec(memory_space=pltpu.VMEM)
    return pl.pallas_call(
        total_body,
        in_specs=[pl.BlockSpec(memory_space=pltpu.SMEM), vm],
        out_shape=jax.ShapeDtypeStruct((CHIPS, CHUNK, NZ), bf16),
        name="total",
    )(params, parts)


def solve_body(core_ref, own_ref, other_ref, order_ref, out_ref, st, high, low, extra, weight, wide, scale, xs, rs, ps):
    c = core_ref[0]
    half = TERMS * K // 2

    def place(g, _):
        mine = pl.multiple_of(c * half + g * 16, 16)
        theirs = pl.multiple_of((1 - c) * half + g * 16, 16)
        for l in range(M // NZ):
            st[pl.ds(mine, 16), l * NZ:(l + 1) * NZ] = own_ref[g * 8 + l, 0:16, :]
            st[pl.ds(theirs, 16), l * NZ:(l + 1) * NZ] = other_ref[g * 8 + l, 0:16, :]
        return 0

    lax.fori_loop(0, half // 16, place, 0)

    for ref, h in ((own_ref, c), (other_ref, 1 - c)):
        def lift(m, _):
            extra[pl.ds(pl.multiple_of(m * 8, 8), 8), :] = ref[m, 16:24, :].astype(f32)
            return 0

        lax.fori_loop(0, CHIPS, lift, 0, unroll=8)
        e = extra[pl.ds(1, CHIPS, stride=8), :]
        e = e + (pltpu.roll(e, NZ - TERMS, 1) + pltpu.roll(e, NZ - 2 * TERMS, 1))
        for q in range(TERMS):
            weight[q, pl.ds(pl.multiple_of(h * CHIPS, CHIPS), CHIPS), :] = jnp.broadcast_to(e[:, q:q + 1], (CHIPS, K))
    source = jnp.concatenate([own_ref[l, 16:24, :] for l in range(M // NZ)], axis=1)
    row = lax.broadcasted_iota(jnp.int32, (8, M), 0)
    source = jnp.where((row == 0) | (row == 2), source.astype(f32), 0.0).astype(bf16)
    gram = nt(st[...], st[...])
    projected = nt(source, st[...])
    projected = projected[0:1, :] + projected[2:3, :]
    top = gram.astype(bf16)
    high[...] = top
    low[...] = (gram - top.astype(f32)).astype(bf16)
    diagonal = lax.broadcasted_iota(jnp.int32, (K, K), 0) == lax.broadcasted_iota(jnp.int32, (K, K), 1)
    sizes = jnp.zeros((POINTS, K), f32)
    right = jnp.zeros((POINTS, K), f32)
    for q in range(TERMS):
        right = right + weight[q] * projected[:, q * K:(q + 1) * K]
        for r in range(TERMS):
            block = gram[q * K:(q + 1) * K, r * K:(r + 1) * K]
            entries = jnp.sum(jnp.where(diagonal, block, 0.0), axis=0, keepdims=True)
            sizes = sizes + (weight[q] * weight[r]) * entries
    scale[...] = 1.0 / sizes
    z0 = right * scale[...]
    xs[...] = jnp.zeros((POINTS, K), f32)
    rs[...] = right
    ps[...] = z0
    start = jnp.sum(right * z0, axis=1, keepdims=True)
    goal = start * TOL2

    def step(rz):
        p = ps[...]
        for q in range(TERMS):
            t = weight[q] * p
            t_high = t.astype(bf16)
            wide[0:POINTS, q * K:(q + 1) * K] = t_high
            wide[POINTS:2 * POINTS, q * K:(q + 1) * K] = (t - t_high.astype(f32)).astype(bf16)
        both = jnp.dot(wide[...], high[...], preferred_element_type=f32)
        image = both[:POINTS] + both[POINTS:] + jnp.dot(wide[0:POINTS, :], low[...], preferred_element_type=f32)
        ap = weight[0] * image[:, 0:K]
        for q in range(1, TERMS):
            ap = ap + weight[q] * image[:, q * K:(q + 1) * K]
        pap = jnp.sum(p * ap, axis=1, keepdims=True)
        alpha = jnp.where(pap > 0.0, rz / pap, 0.0)
        xs[...] += alpha * p
        r = rs[...] - alpha * ap
        rs[...] = r
        z = r * scale[...]
        new = jnp.sum(r * z, axis=1, keepdims=True)
        beta = jnp.where(rz > 0.0, new / rz, 0.0)
        ps[...] = z + beta * p
        return new

    def rounds(carry):
        n, rz, _ = carry
        rz = step(step(rz))
        return (n + 1, rz, jnp.max(jnp.where(rz > goal, 1.0, 0.0)))

    lax.while_loop(lambda s: (s[0] < MAX_ROUNDS) & (s[2] > 0.5), rounds, (jnp.int32(0), start, f32(1.0)))
    wanted = order_ref[...]
    wanted = (wanted & 1) * CHIPS + (wanted >> 1)
    pick = jnp.where(lax.broadcasted_iota(jnp.int32, (POINTS, POINTS), 0) == wanted, 1.0, 0.0).astype(bf16)
    coef = xs[...].astype(bf16)
    picked = lax.dot_general(pick, coef, (((0,), (0,)), ((), ())), preferred_element_type=f32)
    out_ref[...] = picked.astype(bf16)


def solve(core, own, other, order):
    vm = pl.BlockSpec(memory_space=pltpu.VMEM)
    wide = (POINTS, K)
    return pl.pallas_call(
        solve_body,
        in_specs=[pl.BlockSpec(memory_space=pltpu.SMEM), vm, vm, vm],
        out_shape=jax.ShapeDtypeStruct((POINTS, K), bf16),
        scratch_shapes=[
            pltpu.VMEM((TERMS * K, M), bf16),
            pltpu.VMEM((TERMS * K, TERMS * K), bf16),
            pltpu.VMEM((TERMS * K, TERMS * K), bf16),
            pltpu.VMEM((CHIPS * 8, NZ), f32),
            pltpu.VMEM((TERMS, POINTS, K), f32),
            pltpu.VMEM((2 * POINTS, TERMS * K), bf16),
            pltpu.VMEM(wide, f32),
            pltpu.VMEM(wide, f32),
            pltpu.VMEM(wide, f32),
            pltpu.VMEM(wide, f32),
        ],
        compiler_params=pltpu.CompilerParams(vmem_limit_bytes=56 << 20),
        name="solve",
    )(core, own, other, order)


def fields_body(picked_ref, bt_ref, out_ref, turned):
    got = jnp.dot(picked_ref[...], bt_ref[0], preferred_element_type=f32)
    for y in range(NY):
        turned[pl.ds(y, POINTS, stride=NY), :] = got[:, y * NZ:(y + 1) * NZ]
    out_ref[...] = turned[...].reshape(POINTS, 1, NY, NZ).astype(bf16)


def fields_of(picked, bt):
    return pl.pallas_call(
        fields_body,
        grid=(NX,),
        in_specs=[
            pl.BlockSpec((POINTS, K), lambda x: (0, 0)),
            pl.BlockSpec((1, K, CELLS), lambda x: (x, 0, 0)),
        ],
        out_specs=pl.BlockSpec((POINTS, 1, NY, NZ), lambda x: (0, x, 0, 0)),
        out_shape=jax.ShapeDtypeStruct((POINTS, NX, NY, NZ), bf16),
        scratch_shapes=[pltpu.VMEM((POINTS * NY, NZ), f32)],
        compiler_params=pltpu.CompilerParams(
            dimension_semantics=("arbitrary",), vmem_limit_bytes=48 << 20
        ),
        name="fields",
    )(picked, bt)


NARROW = ("x", "zl")
WIDE = ("y", "zh", "core")
CHIP = ("x", "zl", "y", "zh")


def halo_infos(rows, signs, coeffs):
    out = []
    for axes, count, dim, term in ((NARROW, 8, 1, 1), (WIDE, 32, 2, 2)):
        last = rows.shape[dim] - 1

        def info(at):
            take = lambda a: lax.index_in_dim(a, at, dim, keepdims=False).astype(f32)
            return jnp.concatenate([take(rows), take(signs), take(coeffs)[term:term + 1]], axis=0)

        up = [(i, i + 1) for i in range(count - 1)]
        down = [(i + 1, i) for i in range(count - 1)]
        out.append(lax.ppermute(info(last), axes, up))
        out.append(lax.ppermute(info(0), axes, down))
    return out


def per_device(basis, rhs, coeffs, rows, signs, params, order):
    infos = halo_infos(rows, signs, coeffs)
    core = lax.axis_index("core").astype(jnp.int32).reshape(1)
    acc, bt = sketch(basis, rhs, coeffs, rows, signs)
    own, other = edges(core, acc, bt, infos)
    swap = [(0, 1), (1, 0)]
    got = lax.ppermute(other, "core", swap)
    parts = lax.all_to_all(merge(own, got), CHIP, 0, 0, tiled=True)
    mine = lax.all_to_all(total(params, parts), CHIP, 0, 0, tiled=True)
    theirs = lax.ppermute(mine, "core", swap)
    picked = solve(core, mine, theirs, order.reshape(1, POINTS))
    return fields_of(picked, bt)


def solution(mesh):
    fine = Mesh(mesh.devices.reshape(4, 2, 4, 4, 2), ("x", "zl", "y", "zh", "core"))
    cells = P(None, NARROW, WIDE, None)
    in_specs = (
        cells,
        P(NARROW, WIDE, None),
        cells,
        cells,
        cells,
        P(NARROW + WIDE, None),
        P(),
    )
    return jax.shard_map(per_device, mesh=fine, in_specs=in_specs, out_specs=cells, check_vma=False)
```

time: 801 us -> 166 us (0.21)
  blocking collectives: 423 us -> 70.8 us
  waiting for transfers between devices: 213 us -> 4.42 us
  Pallas kernels: 0 us -> 65.1 us
  matrix products: 56.7 us -> 0 us
  local copies, waits for them, and re-layouts: 43.4 us -> 6.48 us
  other arithmetic: 36 us -> 0.86 us
  between operations: 13.6 us -> 0.15 us
    all_gather x1 -> x0, blocking collectives: 345 us -> none  [per_device(): all_coef = lax.all_gather(own_coef, ('narrow', 'wide'), axis=0, tiled=True)]
    psum x1 -> x0, waiting for transfers between devices: 186 us -> none  [per_device(): lax.psum((sketched, sketched_rhs), ('narrow', 'wide'))]
    psum x1 -> x0, blocking collectives: 78.1 us -> none  [per_device(): lax.psum((sketched, sketched_rhs), ('narrow', 'wide'))]
    all_to_all x0 -> x2, blocking collectives: none -> 70.8 us  [the longest x1 41.7 us: per_device(): parts = lax.all_to_all(merge(own, got), CHIP, 0, 0, tiled=True)]
    pallas_call x0 -> x6, Pallas kernels: none -> 65.1 us  [the longest x1 31.5 us: sketch(): pl.pallas_call(sketch_body, out_shape=(jax.ShapeDtypeStruct((TALL, M), f3...]
    dot_general x21 -> x0, matrix products: 56.3 us -> none  [the longest x8 35.6 us: accumulate(): lax.dot_general(hashed, columns, (((1,), (1,)), ((), ())), preferred_elem...]
    another operation x8 -> x0, other arithmetic: 32 us -> none  [the longest x3 12.4 us: solve_points(): lower_factor = jnp.linalg.cholesky(normal)]
    ppermute x4 -> x6, waiting for transfers between devices: 26.5 us -> 4.42 us  [the longest x1 2.49 us: per_device(): got = lax.ppermute(other, 'core', swap)]
  transfers between devices with their start and end apart: 5 -> 6, of which waited for: 5 -> 2; matrix products, arithmetic and copies ran while one was open for 0% -> 1% of each run, Pallas kernels for 0% -> 19%
where the time goes in v1:
time: 166 us; the launch traced here: 165 us
  blocking collectives  70.8 us (43%)
  Pallas kernels  65.1 us (39%)
  starting transfers between devices  17.5 us (11%)
  local copies, waits for them, and re-layouts  6.48 us (4%)
  waiting for transfers between devices  4.42 us (3%)
    all_to_all x1, blocking collectives, per_device(): parts = lax.all_to_all(merge(own, got), CHIP, 0, 0, tiled=True)  41.7 us
    pallas_call x1, Pallas kernels, sketch(): pl.pallas_call(sketch_body, out_shape=(jax.ShapeDtypeStruct((TALL, M), f3...  31.5 us
    all_to_all x1, blocking collectives, per_device(): mine = lax.all_to_all(total(params, parts), CHIP, 0, 0, tiled=True)  29.1 us
    pallas_call x1, Pallas kernels, solve(): pl.pallas_call(solve_body, in_specs=[pl.BlockSpec(memory_space=pltpu.SMEM...  13.2 us
    pallas_call x1, Pallas kernels, edges(): pl.pallas_call(edge_body, in_specs=[pl.BlockSpec(memory_space=pltpu.SMEM)...  10.7 us
    ppermute x2, starting transfers between devices, halo_infos(): out.append(lax.ppermute(info(last), axes, up))  6.91 us
    ppermute x2, starting transfers between devices, halo_infos(): out.append(lax.ppermute(info(0), axes, down))  6.4 us
    pallas_call x1, Pallas kernels, fields_of(): pl.pallas_call(fields_body, grid=(NX,), in_specs=[pl.BlockSpec((POINTS, K...  4.46 us
  transfers between devices with their start and end apart: 6, of which 2 were waited for; matrix products, arithmetic and copies ran while one was open for 1% of the time, Pallas kernels for 19%

profile of v1, /device:TPU:1, one launch (start us, length us, event | category | flops | bytes accessed | tf_op | source)
XLA Modules:
  0.0 165.3 jit_solution(1652774216079927772)
XLA Ops:
  0.0 0.7 fusion.6
  0.7 0.9 fusion.4
  1.6 0.9 fusion.5
  2.5 5.1 %collective-permute-start.3 = (f32[9,4,128]{2,1,0:T(4,128)S(1)}, f32[9,4,128]{2,1,0:T(4,128)S(1)}, u32[]{:S(2)}, u32[]{:S(2)}) collective-permute-start(f32[9,4,128]{2,1,0:T(4,128)S(1)} %pad_maximum_fusion.3), channel_id=1, source_target_pairs={{1,0},{2,1},{3,2},{4,3},{5,4},{6,5},{7,6},{8,7},{9,8},{10,9},{11,1... | collective-permute-start | bytes 55304 | tf_op jit(solution)/shard_map/ppermute | solution.py:415
  7.7 0.7 slice_bitcast_fusion
  8.4 0.8 fusion
  9.2 1.8 %collective-permute-start = (f32[9,16,128]{2,1,0:T(8,128)S(1)}, f32[9,16,128]{2,1,0:T(8,128)S(1)}, u32[]{:S(2)}, u32[]{:S(2)}) collective-permute-start(f32[9,16,128]{2,1,0:T(8,128)S(1)} %pad_maximum_fusion), channel_id=1, source_target_pairs={{0,32},{32,64},{64,96},{96,128},{128,160},{160,192},{192,224},{1,3... | collective-permute-start | bytes 221192 | tf_op jit(solution)/shard_map/ppermute | solution.py:414
  11.1 1.3 collective-permute-start.1
  12.4 5.1 %collective-permute-start.2 = (f32[9,4,128]{2,1,0:T(4,128)S(1)}, f32[9,4,128]{2,1,0:T(4,128)S(1)}, u32[]{:S(2)}, u32[]{:S(2)}) collective-permute-start(f32[9,4,128]{2,1,0:T(4,128)S(1)} %pad_maximum_fusion.2), channel_id=1, source_target_pairs={{0,1},{1,2},{2,3},{3,4},{4,5},{5,6},{6,7},{7,8},{8,9},{9,10},{10,1... | collective-permute-start | bytes 55304 | tf_op jit(solution)/shard_map/ppermute | solution.py:414
  17.5 31.5 %sketch.1 = (f32[528,1024]{1,0:T(8,128)}, bf16[4,128,2048]{2,1,0:T(8,128)(2,1)}) custom-call(bf16[128,4,16,128]{3,2,1,0:T(8,128)(2,1)} %basis_ref.1, bf16[4,16,128]{2,1,0:T(8,128)(2,1)} %rhs_ref.1, f32[4,4,16,128]{3,2,1,0:T(8,128)} %co_ref.1, s32[4,4,16,128]{3,2,1,0:T(8,128)} %rows_ref.1, s32[4,4,16,128]{3,2,1,0:T(8,128)} %signs_ref.1), custom_call_target="tpu_custom_call" | custom-call | tf_op jit(solution)/shard_map/sketch/pallas_call | solution.py:114
  49.0 0.0 collective-permute-done.3.yu_ref
  49.0 0.0 copy-start.7
  49.0 0.0 collective-permute-done.2.yl_ref
  49.0 0.0 copy-start.8
  49.0 0.0 collective-permute-done.xl_ref
  49.0 0.0 copy-start.5
  49.0 0.0 collective-permute-done.1.xu_ref
  49.0 0.0 copy-start.6
  49.0 0.5 copy-done.7
  49.6 0.0 copy-done.8
  49.6 0.0 copy-done.5
  49.6 0.0 copy-done.6
  49.7 10.7 %edges.1 = (f32[128,24,128]{2,1,0:T(8,128)}, bf16[128,24,128]{2,1,0:T(8,128)(2,1)}) custom-call(s32[1]{0:T(128)} %bitcast.core_ref, f32[528,1024]{1,0:T(8,128)} %get-tuple-element.9.acc_in, bf16[4,128,2048]{2,1,0:T(8,128)(2,1)} %get-tuple-element.10.bt_ref, f32[9,16,128]{2,1,0:T(8,128)} %copy-done.5, f32[9,16,128]{2,1,0:T(8,128)} %copy-done.6, ...), custom_call_target="tpu_custom_call" | custom-call | tf_op jit(solution)/shard_map/edges/pallas_call | solution.py:180
  60.4 0.0 collective-permute-start.4
  60.4 2.5 %collective-permute-done.4.got_ref = bf16[128,24,128]{2,1,0:T(8,128)(2,1)S(1)} collective-permute-done((bf16[128,24,128]{2,1,0:T(8,128)(2,1)}, bf16[128,24,128]{2,1,0:T(8,128)(2,1)S(1)}, u32[]{:S(2)}, u32[]{:S(2)}) %collective-permute-start.4) | collective-permute-done | bytes 786464 | tf_op jit(solution)/shard_map/ppermute | solution.py:425
  62.9 0.0 copy-start.3
  62.9 0.9 copy-done.3
  63.7 2.7 %merge.1 = bf16[128,24,128]{2,1,0:T(8,128)(2,1)} custom-call(f32[128,24,128]{2,1,0:T(8,128)} %get-tuple-element.11.own_ref, bf16[128,24,128]{2,1,0:T(8,128)(2,1)} %copy-done.3), custom_call_target="tpu_custom_call" | custom-call | tf_op jit(solution)/shard_map/merge/pallas_call | solution.py:213
  66.4 41.7 %all_to_all.10.parts_ref = bf16[128,24,128]{2,1,0:T(8,128)(2,1)} all-to-all(bf16[128,24,128]{2,1,0:T(8,128)(2,1)} %merge.1), channel_id=1, replica_groups=mesh['x'=4,'zl'=2,'y'=4,'zh'=4,'core'=2] {'x','zl','y','zh'}, dimensions={0} | all-to-all | bytes 1572864 | tf_op jit(solution)/shard_map/all_to_all | solution.py:426
  108.2 0.0 copy-start
  108.2 2.6 %total.1 = bf16[128,24,128]{2,1,0:T(8,128)(2,1)} custom-call(f32[1,4]{1,0:T(1,128)} %params_ref.1, bf16[128,24,128]{2,1,0:T(8,128)(2,1)} %all_to_all.10.parts_ref), custom_call_target="tpu_custom_call" | custom-call | tf_op jit(solution)/shard_map/total/pallas_call | solution.py:254
  110.7 29.1 %all_to_all.11.own_ref = bf16[128,24,128]{2,1,0:T(8,128)(2,1)S(1)} all-to-all(bf16[128,24,128]{2,1,0:T(8,128)(2,1)} %total.1), channel_id=1, replica_groups=mesh['x'=4,'zl'=2,'y'=4,'zh'=4,'core'=2] {'x','zl','y','zh'}, dimensions={0} | all-to-all | bytes 1572864 | tf_op jit(solution)/shard_map/all_to_all | solution.py:427
  139.8 0.0 copy-start.2
  139.8 4.2 %collective-permute-start.5 = (bf16[128,24,128]{2,1,0:T(8,128)(2,1)S(1)}, bf16[128,24,128]{2,1,0:T(8,128)(2,1)S(1)}, u32[]{:S(2)}, u32[]{:S(2)}) collective-permute-start(bf16[128,24,128]{2,1,0:T(8,128)(2,1)S(1)} %all_to_all.11.own_ref), channel_id=1, source_target_pairs={{0,1},{1,0},{2,3},{3,2},{4,5},{5,4},{6,7},{7,6},{8,9},{9,8},{10,11... | collective-permute-start | bytes 2359304 | tf_op jit(solution)/shard_map/ppermute | solution.py:428
  144.0 1.9 %collective-permute-done.5.other_ref = bf16[128,24,128]{2,1,0:T(8,128)(2,1)S(1)} collective-permute-done((bf16[128,24,128]{2,1,0:T(8,128)(2,1)S(1)}, bf16[128,24,128]{2,1,0:T(8,128)(2,1)S(1)}, u32[]{:S(2)}, u32[]{:S(2)}) %collective-permute-start.5) | collective-permute-done | bytes 786464 | tf_op jit(solution)/shard_map/ppermute | solution.py:428
  145.9 0.0 copy-start.4
  145.9 0.0 copy-done.2
  145.9 0.9 copy-done.4
  146.8 13.2 %solve.1.picked_ref = bf16[256,128]{1,0:T(8,128)(2,1)} custom-call(s32[1]{0:T(128)} %bitcast.core_ref, bf16[128,24,128]{2,1,0:T(8,128)(2,1)} %copy-done.2, bf16[128,24,128]{2,1,0:T(8,128)(2,1)} %copy-done.4, s32[1,256]{1,0:T(1,128)} %bitcast.54), custom_call_target="tpu_custom_call" | custom-call | tf_op jit(solution)/shard_map/solve/pallas_call | solution.py:352
  160.0 0.0 copy-done
  160.0 0.0 copy-start.1
  160.0 0.8 copy-done.1
  160.8 4.5 %fields.1 = bf16[256,4,16,128]{3,2,1,0:T(8,128)(2,1)} custom-call(bf16[256,128]{1,0:T(8,128)(2,1)S(1)} %copy-done.1, bf16[4,128,2048]{2,1,0:T(8,128)(2,1)S(1)} %copy-done), custom_call_target="tpu_custom_call" | custom-call | tf_op jit(solution)/shard_map/fields/pallas_call | solution.py:381
  (6 shorter events, 0.0 us)
Async XLA Ops:
  2.5 46.4 %collective-permute-start.3 = (f32[9,4,128]{2,1,0:T(4,128)S(1)}, f32[9,4,128]{2,1,0:T(4,128)S(1)}, u32[]{:S(2)}, u32[]{:S(2)}) collective-permute-start(f32[9,4,128]{2,1,0:T(4,128)S(1)} %pad_maximum_fusion.3), channel_id=1, source_target_pairs={{1,0},{2,1},{3,2},{4,3},{5,4},{6,5},{7,6},{8,7},{9,8},{10,9},{11,1... | collective-permute-start | bytes 55304 | tf_op jit(solution)/shard_map/ppermute | solution.py:415
  9.2 39.8 %collective-permute-start = (f32[9,16,128]{2,1,0:T(8,128)S(1)}, f32[9,16,128]{2,1,0:T(8,128)S(1)}, u32[]{:S(2)}, u32[]{:S(2)}) collective-permute-start(f32[9,16,128]{2,1,0:T(8,128)S(1)} %pad_maximum_fusion), channel_id=1, source_target_pairs={{0,32},{32,64},{64,96},{96,128},{128,160},{160,192},{192,224},{1,3... | collective-permute-start | bytes 221192 | tf_op jit(solution)/shard_map/ppermute | solution.py:414
  11.1 37.9 %collective-permute-start.1 = (f32[9,16,128]{2,1,0:T(8,128)S(1)}, f32[9,16,128]{2,1,0:T(8,128)S(1)}, u32[]{:S(2)}, u32[]{:S(2)}) collective-permute-start(f32[9,16,128]{2,1,0:T(8,128)S(1)} %pad_maximum_fusion.1), channel_id=1, source_target_pairs={{32,0},{64,32},{96,64},{128,96},{160,128},{192,160},{224,192},{33,... | collective-permute-start | bytes 221192 | tf_op jit(solution)/shard_map/ppermute | solution.py:415
  12.4 36.6 %collective-permute-start.2 = (f32[9,4,128]{2,1,0:T(4,128)S(1)}, f32[9,4,128]{2,1,0:T(4,128)S(1)}, u32[]{:S(2)}, u32[]{:S(2)}) collective-permute-start(f32[9,4,128]{2,1,0:T(4,128)S(1)} %pad_maximum_fusion.2), channel_id=1, source_target_pairs={{0,1},{1,2},{2,3},{3,4},{4,5},{5,6},{6,7},{7,8},{8,9},{9,10},{10,1... | collective-permute-start | bytes 55304 | tf_op jit(solution)/shard_map/ppermute | solution.py:414
  49.0 0.6 copy-start.7
  49.0 0.6 copy-start.8
  49.0 0.6 copy-start.5
  49.0 0.6 copy-start.6
  60.4 2.5 %collective-permute-start.4 = (bf16[128,24,128]{2,1,0:T(8,128)(2,1)}, bf16[128,24,128]{2,1,0:T(8,128)(2,1)S(1)}, u32[]{:S(2)}, u32[]{:S(2)}) collective-permute-start(bf16[128,24,128]{2,1,0:T(8,128)(2,1)} %get-tuple-element.12), channel_id=1, source_target_pairs={{0,1},{1,0},{2,3},{3,2},{4,5},{5,4},{6,7},{7,6},{8,9},{9,8},{10,11... | collective-permute-start | bytes 2359304 | tf_op jit(solution)/shard_map/ppermute | solution.py:425
  62.9 0.9 copy-start.3
  108.2 51.8 %copy-start = (bf16[4,128,2048]{2,1,0:T(8,128)(2,1)S(1)}, bf16[4,128,2048]{2,1,0:T(8,128)(2,1)}, u32[]{:S(2)}) copy-start(bf16[4,128,2048]{2,1,0:T(8,128)(2,1)} %get-tuple-element.10.bt_ref) | copy-start | bytes 6291460
  139.8 6.1 %copy-start.2 = (bf16[128,24,128]{2,1,0:T(8,128)(2,1)}, bf16[128,24,128]{2,1,0:T(8,128)(2,1)S(1)}, u32[]{:S(2)}) copy-start(bf16[128,24,128]{2,1,0:T(8,128)(2,1)S(1)} %all_to_all.11.own_ref) | copy-start | bytes 2359300
  139.8 6.1 %collective-permute-start.5 = (bf16[128,24,128]{2,1,0:T(8,128)(2,1)S(1)}, bf16[128,24,128]{2,1,0:T(8,128)(2,1)S(1)}, u32[]{:S(2)}, u32[]{:S(2)}) collective-permute-start(bf16[128,24,128]{2,1,0:T(8,128)(2,1)S(1)} %all_to_all.11.own_ref), channel_id=1, source_target_pairs={{0,1},{1,0},{2,3},{3,2},{4,5},{5,4},{6,7},{7,6},{8,9},{9,8},{10,11... | collective-permute-start | bytes 2359304 | tf_op jit(solution)/shard_map/ppermute | solution.py:428
  145.9 0.9 copy-start.4
  160.0 0.8 copy-start.1

commit v2 on v1

v2 whole, which is shorter than its diff:
```python
import jax
import jax.numpy as jnp
from jax import lax
from jax.experimental import pallas as pl
from jax.experimental.pallas import tpu as pltpu
from jax.sharding import Mesh
from jax.sharding import PartitionSpec as P

K = 128
M = 1024
TERMS = 4
NNZ = 4
ROWS = M // NNZ
NX = 4
NY = 16
NZ = 128
CELLS = NY * NZ
TALL = TERMS * K + 16
CHIPS = 128
SIDE = 16
DEEP = 8
BODY = 128
CHUNK = BODY + 8
POINTS = 256
TOL2 = 1e-10
MAX_ROUNDS = 256

f32 = jnp.float32
bf16 = jnp.bfloat16


def put_hash(hash_ref, slot_ref, y, row_of, sign_of):
    for j in range(NNZ):
        row = jnp.broadcast_to(row_of(j), (16, NZ)).astype(bf16)
        sign = jnp.broadcast_to(sign_of(j), (16, NZ)).astype(bf16)
        for s in range(0, ROWS, 16):
            hash_ref[y, j * ROWS + s:j * ROWS + s + 16, :] = jnp.where(
                slot_ref[s:s + 16, :] == row, sign, jnp.zeros((16, NZ), bf16)
            )


def put_slots(slot_ref):
    slot_ref[...] = lax.broadcasted_iota(jnp.int32, (ROWS, NZ), 0).astype(f32).astype(bf16)


def nt(a, b):
    return lax.dot_general(a, b, (((1,), (1,)), ((), ())), preferred_element_type=f32)


def side_by_side(ref, count):
    return jnp.concatenate([ref[y] for y in range(count)], axis=1)


def in_three(extra):
    high = extra.astype(bf16).astype(f32)
    rest = extra - high
    mid = rest.astype(bf16).astype(f32)
    return (high + pltpu.roll(mid, 2, 0) + pltpu.roll(rest - mid, 4, 0)).astype(bf16)


def from_three(coded):
    coded = coded.astype(f32)
    row = lax.broadcasted_iota(jnp.int32, (8, NZ), 0)
    return jnp.where(row < 2, coded + (pltpu.roll(coded, 6, 0) + pltpu.roll(coded, 4, 0)), 0.0)


def sketch_body(basis_ref, rhs_ref, co_ref, rows_ref, signs_ref, acc_ref, bt_ref, pad, terms, hashes, source_ref, slots):
    put_slots(slots)
    none = jnp.zeros((NY + 2, K, NZ), f32)
    pad[0] = none
    pad[NX + 1] = none
    for x in range(NX):
        pad[x + 1, 0] = jnp.zeros((K, NZ), f32)
        pad[x + 1, NY + 1] = jnp.zeros((K, NZ), f32)
    out = lax.broadcasted_iota(jnp.int32, (16 * NY, 16 * NY), 0)
    src = lax.broadcasted_iota(jnp.int32, (16 * NY, 16 * NY), 1)
    turn = jnp.where((out // 16 == src % 16) & (out % 16 == src // 16), 1.0, 0.0).astype(bf16)

    def turned(i, _):
        k = pl.multiple_of(i * 16, 16)
        for x in range(0, NX, 2):
            both = jnp.concatenate(
                [basis_ref[pl.ds(k, 16), x + d].reshape(16 * NY, NZ) for d in range(2)], axis=1
            )
            got = jnp.dot(turn, both, preferred_element_type=f32)
            for d in range(2):
                for y in range(NY):
                    tile = got[y * 16:(y + 1) * 16, d * NZ:(d + 1) * NZ]
                    pad[x + d + 1, y + 1, pl.ds(k, 16), :] = tile
                    bt_ref[x + d, y, pl.ds(k, 16), :] = tile.astype(bf16)
        return 0

    lax.fori_loop(0, K // 16, turned, 0)
    lane = lax.broadcasted_iota(jnp.int32, (1, NZ), 1)

    def plane(x, _):
        source_ref[...] = rhs_ref[x].astype(f32)

        def group(y, _):
            c0, c1, c2, c3 = (co_ref[q, x, pl.ds(y, 1), :] for q in range(TERMS))
            low3 = jnp.where(lane == 0, 0.0, c3)
            up3 = jnp.where(lane == NZ - 1, 0.0, c3)
            for k in range(0, K, 16):
                at = slice(k, k + 16)
                v = pad[x + 1, y + 1, at, :]
                v2 = v + v
                along_x = v2 - pad[x, y + 1, at, :] - pad[x + 2, y + 1, at, :]
                along_y = v2 - pad[x + 1, y, at, :] - pad[x + 1, y + 2, at, :]
                t3 = c3 * v2 - low3 * pltpu.roll(v, 1, 1) - up3 * pltpu.roll(v, NZ - 1, 1)
                for q, t in enumerate((c0 * v, c1 * along_x, c2 * along_y, t3)):
                    terms[y, q * K + k:q * K + k + 16, :] = t.astype(bf16)
            top = lax.broadcasted_iota(jnp.int32, (16, NZ), 0) == 0
            source = source_ref[pl.ds(y, 1), :]
            terms[y, TERMS * K:TALL, :] = jnp.where(top, source, 0.0).astype(bf16)
            put_hash(
                hashes,
                slots,
                y,
                lambda j: rows_ref[j, x, pl.ds(y, 1), :].astype(f32),
                lambda j: signs_ref[j, x, pl.ds(y, 1), :].astype(f32) - 0.5,
            )
            return 0

        lax.fori_loop(0, NY, group, 0, unroll=2)
        got = nt(side_by_side(terms, NY), side_by_side(hashes, NY))

        @pl.when(x == 0)
        def _():
            acc_ref[...] = got

        @pl.when(x > 0)
        def _():
            acc_ref[...] += got

        return 0

    lax.fori_loop(0, NX, plane, 0)


def sketch(basis, rhs, coeffs, rows, signs):
    return pl.pallas_call(
        sketch_body,
        out_shape=(
            jax.ShapeDtypeStruct((TALL, M), f32),
            jax.ShapeDtypeStruct((NX, NY, K, NZ), bf16),
        ),
        scratch_shapes=[
            pltpu.VMEM((NX + 2, NY + 2, K, NZ), f32),
            pltpu.VMEM((NY, TALL, NZ), bf16),
            pltpu.VMEM((NY, M, NZ), bf16),
            pltpu.VMEM((NY, NZ), f32),
            pltpu.VMEM((ROWS, NZ), bf16),
        ],
        compiler_params=pltpu.CompilerParams(vmem_limit_bytes=56 << 20),
        name="sketch",
    )(basis, rhs, coeffs, rows, signs)


def planes_body(rows_ref, signs_ref, co_ref, x_low, x_high, y_low, y_high):
    for out, x in ((x_low, 0), (x_high, NX - 1)):
        out[0:NNZ] = rows_ref[:, x].astype(f32)
        out[NNZ:2 * NNZ] = signs_ref[:, x].astype(f32)
        out[2 * NNZ] = co_ref[1, x]
    for out, y in ((y_low, 0), (y_high, NY - 1)):
        for x in range(NX):
            for j in range(NNZ):
                out[j, x:x + 1, :] = rows_ref[j, x, y:y + 1, :].astype(f32)
                out[NNZ + j, x:x + 1, :] = signs_ref[j, x, y:y + 1, :].astype(f32)
            out[2 * NNZ, x:x + 1, :] = co_ref[2, x, y:y + 1, :]


def planes(rows, signs, coeffs):
    along_x = jax.ShapeDtypeStruct((2 * NNZ + 1, NY, NZ), f32)
    along_y = jax.ShapeDtypeStruct((2 * NNZ + 1, NX, NZ), f32)
    return pl.pallas_call(
        planes_body, out_shape=(along_x, along_x, along_y, along_y), name="planes"
    )(rows, signs, coeffs)


def edge_body(ids_ref, acc_in, bxl_ref, bxu_ref, byl_ref, byu_ref, xl_ref, xu_ref, yl_ref, yu_ref, own_ref, other_ref, acc, terms, hashes, slots):
    put_slots(slots)
    acc[...] = acc_in[...]

    def one(info, v, y_info, place):
        terms[place] = (-info[2 * NNZ, pl.ds(y_info, 1), :] * v.astype(f32)).astype(bf16)
        put_hash(
            hashes,
            slots,
            place,
            lambda j: info[j, pl.ds(y_info, 1), :],
            lambda j: info[NNZ + j, pl.ds(y_info, 1), :] - 0.5,
        )

    for info, values in ((xl_ref, bxl_ref), (xu_ref, bxu_ref)):
        def group(y, _):
            one(info, values[0, y], y, y)
            return 0

        lax.fori_loop(0, NY, group, 0, unroll=2)
        acc[K:2 * K, :] += nt(side_by_side(terms, NY), side_by_side(hashes, NY))

    def group(x, _):
        one(yl_ref, byl_ref[x, 0], x, x)
        one(yu_ref, byu_ref[x, 0], x, NX + x)
        return 0

    lax.fori_loop(0, NX, group, 0)
    acc[2 * K:3 * K, :] += nt(side_by_side(terms, 2 * NX), side_by_side(hashes, 2 * NX))
    c = ids_ref[0]
    row = lax.broadcasted_iota(jnp.int32, (8, NZ), 0)

    def split(i, _):
        mine = pl.multiple_of(c * 2 * K + i * 16, 16)
        theirs = pl.multiple_of((1 - c) * 2 * K + i * 16, 16)
        for l in range(M // NZ):
            own_ref[i, l * 16:l * 16 + 16, :] = acc[pl.ds(mine, 16), l * NZ:(l + 1) * NZ]
            other_ref[i, l * 16:l * 16 + 16, :] = acc[pl.ds(theirs, 16), l * NZ:(l + 1) * NZ].astype(bf16)
        lane = pl.multiple_of(jnp.minimum(i, M // NZ - 1) * NZ, NZ)
        source = acc[TERMS * K:TERMS * K + 8, pl.ds(lane, NZ)]
        source = jnp.where((row == 0) & (i < M // NZ), source, 0.0)
        own_ref[i, BODY:CHUNK, :] = source
        other_ref[i, BODY:CHUNK, :] = in_three(source)
        return 0

    lax.fori_loop(0, SIDE, split, 0)


def edges(ids, acc, bt, infos):
    vm = pl.BlockSpec(memory_space=pltpu.VMEM)
    return pl.pallas_call(
        edge_body,
        grid=(1,),
        in_specs=[
            pl.BlockSpec(memory_space=pltpu.SMEM),
            vm,
            pl.BlockSpec((1, NY, K, NZ), lambda i: (0, 0, 0, 0)),
            pl.BlockSpec((1, NY, K, NZ), lambda i: (NX - 1, 0, 0, 0)),
            pl.BlockSpec((NX, 1, K, NZ), lambda i: (0, 0, 0, 0)),
            pl.BlockSpec((NX, 1, K, NZ), lambda i: (0, NY - 1, 0, 0)),
            vm,
            vm,
            vm,
            vm,
        ],
        out_specs=(vm, vm),
        out_shape=(
            jax.ShapeDtypeStruct((SIDE, CHUNK, NZ), f32),
            jax.ShapeDtypeStruct((SIDE, CHUNK, NZ), bf16),
        ),
        scratch_shapes=[
            pltpu.VMEM((TALL, M), f32),
            pltpu.VMEM((NY, K, NZ), bf16),
            pltpu.VMEM((NY, M, NZ), bf16),
            pltpu.VMEM((ROWS, NZ), bf16),
        ],
        compiler_params=pltpu.CompilerParams(vmem_limit_bytes=56 << 20),
        name="edges",
    )(ids, acc, bt, bt, bt, bt, *infos)


def merge_body(own_ref, got_ref, out_ref):
    def add(i, _):
        out_ref[i, 0:BODY, :] = (own_ref[i, 0:BODY, :] + got_ref[i, 0:BODY, :].astype(f32)).astype(bf16)
        out_ref[i, BODY:CHUNK, :] = in_three(own_ref[i, BODY:CHUNK, :] + from_three(got_ref[i, BODY:CHUNK, :]))
        return 0

    lax.fori_loop(0, SIDE, add, 0)


def merge(own, got):
    return pl.pallas_call(
        merge_body,
        out_shape=jax.ShapeDtypeStruct((SIDE, CHUNK, NZ), bf16),
        name="merge",
    )(own, got)


def total_of(parts_ref, out_ref, count, copies):
    for at in range(0, BODY, 64):
        total = parts_ref[0, at:at + 64, :].astype(f32)
        for i in range(1, count):
            total = total + parts_ref[i, at:at + 64, :].astype(f32)
        total = total.astype(bf16)
        for i in range(copies):
            out_ref[i, at:at + 64, :] = total
    extra = from_three(parts_ref[0, BODY:CHUNK, :])
    for i in range(1, count):
        extra = extra + from_three(parts_ref[i, BODY:CHUNK, :])
    return extra


def first_body(ids_ref, params_ref, parts_ref, out_ref):
    extra = total_of(parts_ref, out_ref, SIDE, DEEP)
    lane = lax.broadcasted_iota(jnp.int32, (8, NZ), 1)
    row = lax.broadcasted_iota(jnp.int32, (8, NZ), 0)
    extra = jnp.where(row == 0, extra, 0.0)
    for q in range(TERMS):
        extra = jnp.where((row == 1) & (lane == q * DEEP + ids_ref[1]), params_ref[0, q], extra)
    extra = in_three(extra)
    for i in range(DEEP):
        out_ref[i, BODY:CHUNK, :] = extra


def first(ids, params, parts):
    sm = pl.BlockSpec(memory_space=pltpu.SMEM)
    return pl.pallas_call(
        first_body,
        in_specs=[sm, sm, pl.BlockSpec(memory_space=pltpu.VMEM)],
        out_shape=jax.ShapeDtypeStruct((DEEP, CHUNK, NZ), bf16),
        name="first",
    )(ids, params, parts)


def second_body(parts_ref, out_ref):
    extra = in_three(total_of(parts_ref, out_ref, DEEP, SIDE))
    for i in range(SIDE):
        out_ref[i, BODY:CHUNK, :] = extra


def second(parts):
    return pl.pallas_call(
        second_body,
        out_shape=jax.ShapeDtypeStruct((SIDE, CHUNK, NZ), bf16),
        name="second",
    )(parts)


def solve_body(ids_ref, own_ref, other_ref, order_ref, out_ref, st, high, low, extra, weight, wide, scale, xs, rs, ps):
    c = ids_ref[0]
    half = TERMS * K // 2

    def place(i, _):
        mine = pl.multiple_of(c * half + i * 16, 16)
        theirs = pl.multiple_of((1 - c) * half + i * 16, 16)
        for l in range(M // NZ):
            st[pl.ds(mine, 16), l * NZ:(l + 1) * NZ] = own_ref[i, l * 16:l * 16 + 16, :]
            st[pl.ds(theirs, 16), l * NZ:(l + 1) * NZ] = other_ref[i, l * 16:l * 16 + 16, :]
        return 0

    lax.fori_loop(0, SIDE, place, 0)
    extra[...] = jnp.zeros((NZ, NZ), f32)
    for ref, h in ((own_ref, c), (other_ref, 1 - c)):
        for i in range(SIDE):
            extra[i:i + 1, :] = from_three(ref[i, BODY:CHUNK, :])[1:2, :]
        columns = jnp.transpose(extra[...])
        for i in range(SIDE):
            at = pl.multiple_of(h * CHIPS + i * DEEP, DEEP)
            for q in range(TERMS):
                weight[q, pl.ds(at, DEEP), :] = jnp.broadcast_to(
                    columns[q * DEEP:(q + 1) * DEEP, i:i + 1], (DEEP, K)
                )
    source = jnp.concatenate([own_ref[i, BODY:CHUNK, :] for i in range(M // NZ)], axis=1)
    gram = nt(st[...], st[...])
    projected = nt(source, st[...])
    projected = projected[0:1, :] + (projected[2:3, :] + projected[4:5, :])
    top = gram.astype(bf16)
    high[...] = top
    low[...] = (gram - top.astype(f32)).astype(bf16)
    diagonal = lax.broadcasted_iota(jnp.int32, (K, K), 0) == lax.broadcasted_iota(jnp.int32, (K, K), 1)
    sizes = jnp.zeros((POINTS, K), f32)
    right = jnp.zeros((POINTS, K), f32)
    for q in range(TERMS):
        right = right + weight[q] * projected[:, q * K:(q + 1) * K]
        for r in range(TERMS):
            block = gram[q * K:(q + 1) * K, r * K:(r + 1) * K]
            entries = jnp.sum(jnp.where(diagonal, block, 0.0), axis=0, keepdims=True)
            sizes = sizes + (weight[q] * weight[r]) * entries
    scale[...] = 1.0 / sizes
    z0 = right * scale[...]
    xs[...] = jnp.zeros((POINTS, K), f32)
    rs[...] = right
    ps[...] = z0
    start = jnp.sum(right * z0, axis=1, keepdims=True)
    goal = start * TOL2

    def step(rz):
        p = ps[...]
        for q in range(TERMS):
            t = weight[q] * p
            t_high = t.astype(bf16)
            wide[0:POINTS, q * K:(q + 1) * K] = t_high
            wide[POINTS:2 * POINTS, q * K:(q + 1) * K] = (t - t_high.astype(f32)).astype(bf16)
        both = jnp.dot(wide[...], high[...], preferred_element_type=f32)
        image = both[:POINTS] + both[POINTS:] + jnp.dot(wide[0:POINTS, :], low[...], preferred_element_type=f32)
        ap = weight[0] * image[:, 0:K]
        for q in range(1, TERMS):
            ap = ap + weight[q] * image[:, q * K:(q + 1) * K]
        pap = jnp.sum(p * ap, axis=1, keepdims=True)
        alpha = jnp.where(pap > 0.0, rz / pap, 0.0)
        xs[...] += alpha * p
        r = rs[...] - alpha * ap
        rs[...] = r
        z = r * scale[...]
        new = jnp.sum(r * z, axis=1, keepdims=True)
        beta = jnp.where(rz > 0.0, new / rz, 0.0)
        ps[...] = z + beta * p
        return new

    def rounds(carry):
        n, rz, _ = carry
        rz = step(step(rz))
        return (n + 1, rz, jnp.max(jnp.where(rz > goal, 1.0, 0.0)))

    lax.while_loop(lambda s: (s[0] < MAX_ROUNDS) & (s[2] > 0.5), rounds, (jnp.int32(0), start, f32(1.0)))
    wanted = order_ref[...]
    wanted = (
        ((wanted & 1) << 7)
        + ((wanted >> 6) << 5)
        + (((wanted >> 3) & 3) << 3)
        + (((wanted >> 5) & 1) << 2)
        + ((wanted >> 1) & 3)
    )
    pick = jnp.where(lax.broadcasted_iota(jnp.int32, (POINTS, POINTS), 0) == wanted, 1.0, 0.0).astype(bf16)
    coef = xs[...].astype(bf16)
    picked = lax.dot_general(pick, coef, (((0,), (0,)), ((), ())), preferred_element_type=f32)
    out_ref[...] = picked.astype(bf16)


def solve(ids, own, other, order):
    vm = pl.BlockSpec(memory_space=pltpu.VMEM)
    wide = (POINTS, K)
    return pl.pallas_call(
        solve_body,
        in_specs=[pl.BlockSpec(memory_space=pltpu.SMEM), vm, vm, vm],
        out_shape=jax.ShapeDtypeStruct((POINTS, K), bf16),
        scratch_shapes=[
            pltpu.VMEM((TERMS * K, M), bf16),
            pltpu.VMEM((TERMS * K, TERMS * K), bf16),
            pltpu.VMEM((TERMS * K, TERMS * K), bf16),
            pltpu.VMEM((NZ, NZ), f32),
            pltpu.VMEM((TERMS, POINTS, K), f32),
            pltpu.VMEM((2 * POINTS, TERMS * K), bf16),
            pltpu.VMEM(wide, f32),
            pltpu.VMEM(wide, f32),
            pltpu.VMEM(wide, f32),
            pltpu.VMEM(wide, f32),
        ],
        compiler_params=pltpu.CompilerParams(vmem_limit_bytes=56 << 20),
        name="solve",
    )(ids, own, other, order)


def fields_body(picked_ref, bt_ref, out_ref, turned):
    picked = picked_ref[...]
    for y in range(0, NY, 2):
        pair = jnp.concatenate([bt_ref[0, y], bt_ref[0, y + 1]], axis=1)
        got = jnp.dot(picked, pair, preferred_element_type=f32)
        for d in range(2):
            turned[pl.ds(y + d, POINTS, stride=NY), :] = got[:, d * NZ:(d + 1) * NZ]
    out_ref[...] = turned[...].reshape(POINTS, 1, NY, NZ).astype(bf16)


def fields_of(picked, bt):
    return pl.pallas_call(
        fields_body,
        grid=(NX,),
        in_specs=[
            pl.BlockSpec((POINTS, K), lambda x: (0, 0)),
            pl.BlockSpec((1, NY, K, NZ), lambda x: (x, 0, 0, 0)),
        ],
        out_specs=pl.BlockSpec((POINTS, 1, NY, NZ), lambda x: (0, x, 0, 0)),
        out_shape=jax.ShapeDtypeStruct((POINTS, NX, NY, NZ), bf16),
        scratch_shapes=[pltpu.VMEM((POINTS * NY, NZ), f32)],
        compiler_params=pltpu.CompilerParams(
            dimension_semantics=("arbitrary",), vmem_limit_bytes=48 << 20
        ),
        name="fields",
    )(picked, bt)


NARROW = ("x", "zl")
WIDE = ("y", "zh", "core")
FACE = ("x", "y")
DEPTH = ("zl", "zh")


def per_device(basis, rhs, coeffs, rows, signs, params, order):
    x_low, x_high, y_low, y_high = planes(rows, signs, coeffs)
    infos = []
    for axes, count, low, high in ((NARROW, 8, x_low, x_high), (WIDE, 32, y_low, y_high)):
        infos.append(lax.ppermute(high, axes, [(i, i + 1) for i in range(count - 1)]))
        infos.append(lax.ppermute(low, axes, [(i + 1, i) for i in range(count - 1)]))
    core = lax.axis_index("core").astype(jnp.int32)
    ids = jnp.stack([core, (lax.axis_index("zl") * 4 + lax.axis_index("zh")).astype(jnp.int32)])
    acc, bt = sketch(basis, rhs, coeffs, rows, signs)
    own, other = edges(ids, acc, bt, infos)
    swap = [(0, 1), (1, 0)]
    parts = merge(own, lax.ppermute(other, "core", swap))
    parts = lax.all_to_all(parts, FACE, 0, 0, tiled=True)
    parts = lax.all_to_all(first(ids, params, parts), DEPTH, 0, 0, tiled=True)
    mine = lax.all_to_all(second(parts), FACE, 0, 0, tiled=True)
    theirs = lax.ppermute(mine, "core", swap)
    picked = solve(ids, mine, theirs, order.reshape(1, POINTS))
    return fields_of(picked, bt)


def solution(mesh):
    fine = Mesh(mesh.devices.reshape(4, 2, 4, 4, 2), ("x", "zl", "y", "zh", "core"))
    cells = P(None, NARROW, WIDE, None)
    in_specs = (
        cells,
        P(NARROW, WIDE, None),
        cells,
        cells,
        cells,
        P(NARROW + WIDE, None),
        P(),
    )
    return jax.shard_map(per_device, mesh=fine, in_specs=in_specs, out_specs=cells, check_vma=False)
```

time: 166 us -> 134 us (0.81)
  blocking collectives: 70.8 us -> 52.7 us
  Pallas kernels: 65.1 us -> 56.4 us
  local copies, waits for them, and re-layouts: 6.48 us -> 3.09 us
    all_to_all x2 -> x3, blocking collectives: 70.8 us -> 52.7 us  [the longest x1 22.7 us: per_device(): parts = lax.all_to_all(parts, FACE, 0, 0, tiled=True)]
    pallas_call x1, Pallas kernels: 31.5 us -> 21.9 us  [sketch(): pl.pallas_call(sketch_body, out_shape=(jax.ShapeDtypeStruct((TALL, M), f3...]
    slice x4 -> x0, local copies, waits for them, and re-layouts: 3.23 us -> none  [the longest x2 1.77 us: info(): take = lambda a: lax.index_in_dim(a, at, dim, keepdims=False).astype(f32)]
    pallas_call x3 -> x5, Pallas kernels: 15.9 us -> 17.2 us  [the longest x1 9.04 us: edges(): pl.pallas_call(edge_body, grid=(1,), in_specs=[pl.BlockSpec(memory_space=...]
  transfers between devices with their start and end apart: 6 -> 6, of which waited for: 2 -> 2; matrix products, arithmetic and copies ran while one was open for 1% -> 0% of each run, Pallas kernels for 19% -> 16%
where the time goes in v2:
time: 134 us; the launch traced here: 133 us
  Pallas kernels  56.4 us (42%)
  blocking collectives  52.7 us (39%)
  starting transfers between devices  16.5 us (12%)
  waiting for transfers between devices  3.76 us (3%)
  local copies, waits for them, and re-layouts  3.09 us (2%)
    all_to_all x1, blocking collectives, per_device(): parts = lax.all_to_all(parts, FACE, 0, 0, tiled=True)  22.7 us
    pallas_call x1, Pallas kernels, sketch(): pl.pallas_call(sketch_body, out_shape=(jax.ShapeDtypeStruct((TALL, M), f3...  21.9 us
    all_to_all x1, blocking collectives, per_device(): parts = lax.all_to_all(first(ids, params, parts), DEPTH, 0, 0, tiled=True)  17 us
    all_to_all x1, blocking collectives, per_device(): mine = lax.all_to_all(second(parts), FACE, 0, 0, tiled=True)  13 us
    pallas_call x1, Pallas kernels, solve(): pl.pallas_call(solve_body, in_specs=[pl.BlockSpec(memory_space=pltpu.SMEM...  12.7 us
    ppermute x2, starting transfers between devices, per_device(): lax.ppermute(high, axes, [(i, i + 1) for i in range(count - 1)])  9.81 us
    pallas_call x1, Pallas kernels, edges(): pl.pallas_call(edge_body, grid=(1,), in_specs=[pl.BlockSpec(memory_space=...  9.04 us
    pallas_call x1, Pallas kernels, fields_of(): pl.pallas_call(fields_body, grid=(NX,), in_specs=[pl.BlockSpec((POINTS, K...  4.68 us
  transfers between devices with their start and end apart: 6, of which 2 were waited for; matrix products, arithmetic and copies ran while one was open for 0% of the time, Pallas kernels for 16%

profile of v2, /device:TPU:1, one launch (start us, length us, event | category | flops | bytes accessed | tf_op | source)
XLA Modules:
  0.0 133.2 jit_solution(17698736692743922863)
XLA Ops:
  0.0 1.7 %planes.1 = (f32[9,16,128]{2,1,0:T(8,128)}, f32[9,16,128]{2,1,0:T(8,128)}, f32[9,4,128]{2,1,0:T(4,128)}, f32[9,4,128]{2,1,0:T(4,128)}) custom-call(s32[4,4,16,128]{3,2,1,0:T(8,128)} %rows_ref.3, s32[4,4,16,128]{3,2,1,0:T(8,128)} %signs_ref.3, f32[4,4,16,128]{3,2,1,0:T(8,128)} %co_ref.3), custom_call_target="tpu_custom_call" | custom-call | tf_op jit(solution)/shard_map/planes/pallas_call | solution.py:175
  1.7 6.3 %collective-permute-start.2 = (f32[9,4,128]{2,1,0:T(4,128)}, f32[9,4,128]{2,1,0:T(4,128)S(1)}, u32[]{:S(2)}, u32[]{:S(2)}) collective-permute-start(f32[9,4,128]{2,1,0:T(4,128)} %get-tuple-element.17), channel_id=1, source_target_pairs={{0,1},{1,2},{2,3},{3,4},{4,5},{5,6},{6,7},{7,8},{8,9},{9,10},{10,1... | collective-permute-start | bytes 55304 | tf_op jit(solution)/shard_map/ppermute | solution.py:481
  8.0 1.9 %collective-permute-start.3 = (f32[9,4,128]{2,1,0:T(4,128)}, f32[9,4,128]{2,1,0:T(4,128)S(1)}, u32[]{:S(2)}, u32[]{:S(2)}) collective-permute-start(f32[9,4,128]{2,1,0:T(4,128)} %get-tuple-element.18), channel_id=1, source_target_pairs={{1,0},{2,1},{3,2},{4,3},{5,4},{6,5},{7,6},{8,7},{9,8},{10,9},{11,1... | collective-permute-start | bytes 55304 | tf_op jit(solution)/shard_map/ppermute | solution.py:482
  9.9 3.5 %collective-permute-start = (f32[9,16,128]{2,1,0:T(8,128)}, f32[9,16,128]{2,1,0:T(8,128)S(1)}, u32[]{:S(2)}, u32[]{:S(2)}) collective-permute-start(f32[9,16,128]{2,1,0:T(8,128)} %get-tuple-element.15), channel_id=1, source_target_pairs={{0,32},{32,64},{64,96},{96,128},{128,160},{160,192},{192,224},{1,3... | collective-permute-start | bytes 221192 | tf_op jit(solution)/shard_map/ppermute | solution.py:481
  13.5 1.3 collective-permute-start.1
  14.8 0.6 pad_add_fusion.ids_ref
  15.4 21.9 %sketch.1 = (f32[528,1024]{1,0:T(8,128)}, bf16[4,16,128,128]{3,2,1,0:T(8,128)(2,1)}) custom-call(bf16[128,4,16,128]{3,2,1,0:T(8,128)(2,1)} %basis_ref.1, bf16[4,16,128]{2,1,0:T(8,128)(2,1)} %rhs_ref.1, f32[4,4,16,128]{3,2,1,0:T(8,128)} %co_ref.3, s32[4,4,16,128]{3,2,1,0:T(8,128)} %rows_ref.3, s32[4,4,16,128]{3,2,1,0:T(8,128)} %signs_ref.3), custom_call_target="tpu_custom_call" | custom-call | tf_op jit(solution)/shard_map/sketch/pallas_call | solution.py:141
  37.3 0.0 collective-permute-done.2.yl_ref
  37.3 0.0 copy-start.7
  37.3 0.0 collective-permute-done.3.yu_ref
  37.3 0.0 copy-start.8
  37.3 0.0 collective-permute-done.xl_ref
  37.3 0.0 copy-start.5
  37.3 0.0 collective-permute-done.1.xu_ref
  37.3 0.0 copy-start.6
  37.4 0.6 copy-done.7
  37.9 0.0 copy-done.8
  37.9 0.0 copy-done.5
  38.0 0.0 copy-done.6
  38.0 9.0 %edges.1 = (f32[16,136,128]{2,1,0:T(8,128)}, bf16[16,136,128]{2,1,0:T(8,128)(2,1)}) custom-call(s32[2]{0:T(128)} %pad_add_fusion.ids_ref, f32[528,1024]{1,0:T(8,128)} %get-tuple-element.13.acc_in, bf16[4,16,128,128]{3,2,1,0:T(8,128)(2,1)} %get-tuple-element.14.bxl_ref.bxu_ref.byl_ref.byu_ref.bt_ref, ...), custom_call_target="tpu_custom_call" | custom-call | tf_op jit(solution)/shard_map/edges/pallas_call | solution.py:230
  47.0 0.0 collective-permute-start.4
  47.0 2.2 %collective-permute-done.4.got_ref = bf16[16,136,128]{2,1,0:T(8,128)(2,1)S(1)} collective-permute-done((bf16[16,136,128]{2,1,0:T(8,128)(2,1)}, bf16[16,136,128]{2,1,0:T(8,128)(2,1)S(1)}, u32[]{:S(2)}, u32[]{:S(2)}) %collective-permute-start.4) | collective-permute-done | bytes 557088 | tf_op jit(solution)/shard_map/ppermute | solution.py:488
  49.2 0.0 copy-start.4
  49.2 0.8 copy-done.4
  50.0 2.6 %merge.1 = bf16[16,136,128]{2,1,0:T(8,128)(2,1)} custom-call(f32[16,136,128]{2,1,0:T(8,128)} %get-tuple-element.19.own_ref, bf16[16,136,128]{2,1,0:T(8,128)(2,1)} %copy-done.4), custom_call_target="tpu_custom_call" | custom-call | tf_op jit(solution)/shard_map/merge/pallas_call | solution.py:271
  52.6 22.7 %all_to_all.15.parts_ref = bf16[16,136,128]{2,1,0:T(8,128)(2,1)} all-to-all(bf16[16,136,128]{2,1,0:T(8,128)(2,1)} %merge.1), channel_id=1, replica_groups=mesh['x'=4,'zl'=2,'y'=4,'zh'=4,'core'=2] {'x','y'}, dimensions={0} | all-to-all | bytes 1114112 | tf_op jit(solution)/shard_map/all_to_all | solution.py:489
  75.3 0.0 copy-start
  75.3 2.0 %first.1 = bf16[8,136,128]{2,1,0:T(8,128)(2,1)} custom-call(s32[2]{0:T(128)} %pad_add_fusion.ids_ref, f32[1,4]{1,0:T(1,128)} %params_ref.1, bf16[16,136,128]{2,1,0:T(8,128)(2,1)} %all_to_all.15.parts_ref), custom_call_target="tpu_custom_call" | custom-call | tf_op jit(solution)/shard_map/first/pallas_call | solution.py:306
  77.3 17.0 %all_to_all.16.parts_ref = bf16[8,136,128]{2,1,0:T(8,128)(2,1)} all-to-all(bf16[8,136,128]{2,1,0:T(8,128)(2,1)} %first.1), channel_id=1, replica_groups=mesh['x'=4,'zl'=2,'y'=4,'zh'=4,'core'=2] {'zl','zh'}, dimensions={0} | all-to-all | bytes 557056 | tf_op jit(solution)/shard_map/all_to_all | solution.py:490
  94.3 1.8 %second.1 = bf16[16,136,128]{2,1,0:T(8,128)(2,1)} custom-call(bf16[8,136,128]{2,1,0:T(8,128)(2,1)} %all_to_all.16.parts_ref), custom_call_target="tpu_custom_call" | custom-call | tf_op jit(solution)/shard_map/second/pallas_call | solution.py:321
  96.2 13.0 %all_to_all.17.own_ref = bf16[16,136,128]{2,1,0:T(8,128)(2,1)S(1)} all-to-all(bf16[16,136,128]{2,1,0:T(8,128)(2,1)} %second.1), channel_id=1, replica_groups=mesh['x'=4,'zl'=2,'y'=4,'zh'=4,'core'=2] {'x','y'}, dimensions={0} | all-to-all | bytes 1114112 | tf_op jit(solution)/shard_map/all_to_all | solution.py:491
  109.1 0.0 copy-start.2
  109.1 3.5 %collective-permute-start.5 = (bf16[16,136,128]{2,1,0:T(8,128)(2,1)S(1)}, bf16[16,136,128]{2,1,0:T(8,128)(2,1)S(1)}, u32[]{:S(2)}, u32[]{:S(2)}) collective-permute-start(bf16[16,136,128]{2,1,0:T(8,128)(2,1)S(1)} %all_to_all.17.own_ref), channel_id=1, source_target_pairs={{0,1},{1,0},{2,3},{3,2},{4,5},{5,4},{6,7},{7,6},{8,9},{9,8},{10,11... | collective-permute-start | bytes 1671176 | tf_op jit(solution)/shard_map/ppermute | solution.py:492
  112.6 1.6 %collective-permute-done.5.other_ref = bf16[16,136,128]{2,1,0:T(8,128)(2,1)S(1)} collective-permute-done((bf16[16,136,128]{2,1,0:T(8,128)(2,1)S(1)}, bf16[16,136,128]{2,1,0:T(8,128)(2,1)S(1)}, u32[]{:S(2)}, u32[]{:S(2)}) %collective-permute-start.5) | collective-permute-done | bytes 557088 | tf_op jit(solution)/shard_map/ppermute | solution.py:492
  114.2 0.0 copy-start.3
  114.2 0.0 copy-done.2
  114.2 0.8 copy-done.3
  115.0 12.7 %solve.1.picked_ref = bf16[256,128]{1,0:T(8,128)(2,1)} custom-call(s32[2]{0:T(128)} %pad_add_fusion.ids_ref, bf16[16,136,128]{2,1,0:T(8,128)(2,1)} %copy-done.2, bf16[16,136,128]{2,1,0:T(8,128)(2,1)} %copy-done.3, s32[1,256]{1,0:T(1,128)} %bitcast.3), custom_call_target="tpu_custom_call" | custom-call | tf_op jit(solution)/shard_map/solve/pallas_call | solution.py:422
  127.7 0.0 copy-done
  127.7 0.0 copy-start.1
  127.7 0.8 copy-done.1
  128.6 4.7 %fields.1 = bf16[256,4,16,128]{3,2,1,0:T(8,128)(2,1)} custom-call(bf16[256,128]{1,0:T(8,128)(2,1)S(1)} %copy-done.1, bf16[4,16,128,128]{3,2,1,0:T(8,128)(2,1)S(1)} %copy-done), custom_call_target="tpu_custom_call" | custom-call | tf_op jit(solution)/shard_map/fields/pallas_call | solution.py:454
Async XLA Ops:
  1.7 35.6 %collective-permute-start.2 = (f32[9,4,128]{2,1,0:T(4,128)}, f32[9,4,128]{2,1,0:T(4,128)S(1)}, u32[]{:S(2)}, u32[]{:S(2)}) collective-permute-start(f32[9,4,128]{2,1,0:T(4,128)} %get-tuple-element.17), channel_id=1, source_target_pairs={{0,1},{1,2},{2,3},{3,4},{4,5},{5,6},{6,7},{7,8},{8,9},{9,10},{10,1... | collective-permute-start | bytes 55304 | tf_op jit(solution)/shard_map/ppermute | solution.py:481
  8.0 29.3 %collective-permute-start.3 = (f32[9,4,128]{2,1,0:T(4,128)}, f32[9,4,128]{2,1,0:T(4,128)S(1)}, u32[]{:S(2)}, u32[]{:S(2)}) collective-permute-start(f32[9,4,128]{2,1,0:T(4,128)} %get-tuple-element.18), channel_id=1, source_target_pairs={{1,0},{2,1},{3,2},{4,3},{5,4},{6,5},{7,6},{8,7},{9,8},{10,9},{11,1... | collective-permute-start | bytes 55304 | tf_op jit(solution)/shard_map/ppermute | solution.py:482
  9.9 27.4 %collective-permute-start = (f32[9,16,128]{2,1,0:T(8,128)}, f32[9,16,128]{2,1,0:T(8,128)S(1)}, u32[]{:S(2)}, u32[]{:S(2)}) collective-permute-start(f32[9,16,128]{2,1,0:T(8,128)} %get-tuple-element.15), channel_id=1, source_target_pairs={{0,32},{32,64},{64,96},{96,128},{128,160},{160,192},{192,224},{1,3... | collective-permute-start | bytes 221192 | tf_op jit(solution)/shard_map/ppermute | solution.py:481
  13.5 23.9 %collective-permute-start.1 = (f32[9,16,128]{2,1,0:T(8,128)}, f32[9,16,128]{2,1,0:T(8,128)S(1)}, u32[]{:S(2)}, u32[]{:S(2)}) collective-permute-start(f32[9,16,128]{2,1,0:T(8,128)} %get-tuple-element.16), channel_id=1, source_target_pairs={{32,0},{64,32},{96,64},{128,96},{160,128},{192,160},{224,192},{33,... | collective-permute-start | bytes 221192 | tf_op jit(solution)/shard_map/ppermute | solution.py:482
  37.3 0.6 copy-start.7
  37.3 0.6 copy-start.8
  37.3 0.6 copy-start.5
  37.3 0.6 copy-start.6
  47.0 2.2 %collective-permute-start.4 = (bf16[16,136,128]{2,1,0:T(8,128)(2,1)}, bf16[16,136,128]{2,1,0:T(8,128)(2,1)S(1)}, u32[]{:S(2)}, u32[]{:S(2)}) collective-permute-start(bf16[16,136,128]{2,1,0:T(8,128)(2,1)} %get-tuple-element.20), channel_id=1, source_target_pairs={{0,1},{1,0},{2,3},{3,2},{4,5},{5,4},{6,7},{7,6},{8,9},{9,8},{10,11... | collective-permute-start | bytes 1671176 | tf_op jit(solution)/shard_map/ppermute | solution.py:488
  49.2 0.8 copy-start.4
  75.3 52.4 %copy-start = (bf16[4,16,128,128]{3,2,1,0:T(8,128)(2,1)S(1)}, bf16[4,16,128,128]{3,2,1,0:T(8,128)(2,1)}, u32[]{:S(2)}) copy-start(bf16[4,16,128,128]{3,2,1,0:T(8,128)(2,1)} %get-tuple-element.14.bxl_ref.bxu_ref.byl_ref.byu_ref.bt_ref) | copy-start | bytes 6291460
  109.1 5.1 %copy-start.2 = (bf16[16,136,128]{2,1,0:T(8,128)(2,1)}, bf16[16,136,128]{2,1,0:T(8,128)(2,1)S(1)}, u32[]{:S(2)}) copy-start(bf16[16,136,128]{2,1,0:T(8,128)(2,1)S(1)} %all_to_all.17.own_ref) | copy-start | bytes 1671172
  109.1 5.1 %collective-permute-start.5 = (bf16[16,136,128]{2,1,0:T(8,128)(2,1)S(1)}, bf16[16,136,128]{2,1,0:T(8,128)(2,1)S(1)}, u32[]{:S(2)}, u32[]{:S(2)}) collective-permute-start(bf16[16,136,128]{2,1,0:T(8,128)(2,1)S(1)} %all_to_all.17.own_ref), channel_id=1, source_target_pairs={{0,1},{1,0},{2,3},{3,2},{4,5},{5,4},{6,7},{7,6},{8,9},{9,8},{10,11... | collective-permute-start | bytes 1671176 | tf_op jit(solution)/shard_map/ppermute | solution.py:492
  114.2 0.8 copy-start.3
  127.7 0.8 copy-start.1

commit v3 on v2

--- a/solution.py
+++ b/solution.py
@@ -24,6 +24,7 @@
 POINTS = 256
 TOL2 = 1e-10
 MAX_ROUNDS = 256
+PAIRS = tuple((q, r) for q in range(TERMS) for r in range(q, TERMS))
 
 f32 = jnp.float32
 bf16 = jnp.bfloat16
@@ -64,7 +65,16 @@
     return jnp.where(row < 2, coded + (pltpu.roll(coded, 6, 0) + pltpu.roll(coded, 4, 0)), 0.0)
 
 
-def sketch_body(basis_ref, rhs_ref, co_ref, rows_ref, signs_ref, acc_ref, bt_ref, pad, terms, hashes, source_ref, slots):
+def sketch_body(
+    basis_ref, rhs_ref, co_hbm, rows_hbm, signs_hbm, acc_ref, bt_hbm,
+    pad, terms, hashes, source_ref, slots, co_ref, rows_ref, signs_ref, bt_ref, sems,
+):
+    fetches = [
+        pltpu.make_async_copy(src, dst, sems.at[i])
+        for i, (src, dst) in enumerate(((co_hbm, co_ref), (rows_hbm, rows_ref), (signs_hbm, signs_ref)))
+    ]
+    for fetch in fetches:
+        fetch.start()
     put_slots(slots)
     none = jnp.zeros((NY + 2, K, NZ), f32)
     pad[0] = none
@@ -91,6 +101,10 @@
         return 0
 
     lax.fori_loop(0, K // 16, turned, 0)
+    give = pltpu.make_async_copy(bt_ref, bt_hbm, sems.at[3])
+    give.start()
+    for fetch in fetches:
+        fetch.wait()
     lane = lax.broadcasted_iota(jnp.int32, (1, NZ), 1)
 
     def plane(x, _):
@@ -135,11 +149,16 @@
         return 0
 
     lax.fori_loop(0, NX, plane, 0)
+    give.wait()
 
 
 def sketch(basis, rhs, coeffs, rows, signs):
+    vm = pl.BlockSpec(memory_space=pltpu.VMEM)
+    hbm = pl.BlockSpec(memory_space=pl.ANY)
     return pl.pallas_call(
         sketch_body,
+        in_specs=[vm, vm, hbm, hbm, hbm],
+        out_specs=(vm, hbm),
         out_shape=(
             jax.ShapeDtypeStruct((TALL, M), f32),
             jax.ShapeDtypeStruct((NX, NY, K, NZ), bf16),
@@ -150,36 +169,50 @@
             pltpu.VMEM((NY, M, NZ), bf16),
             pltpu.VMEM((NY, NZ), f32),
             pltpu.VMEM((ROWS, NZ), bf16),
+            pltpu.VMEM((TERMS, NX, NY, NZ), f32),
+            pltpu.VMEM((NNZ, NX, NY, NZ), jnp.int32),
+            pltpu.VMEM((NNZ, NX, NY, NZ), jnp.int32),
+            pltpu.VMEM((NX, NY, K, NZ), bf16),
+            pltpu.SemaphoreType.DMA((4,)),
         ],
         compiler_params=pltpu.CompilerParams(vmem_limit_bytes=56 << 20),
         name="sketch",
     )(basis, rhs, coeffs, rows, signs)
 
 
-def planes_body(rows_ref, signs_ref, co_ref, x_low, x_high, y_low, y_high):
-    for out, x in ((x_low, 0), (x_high, NX - 1)):
-        out[0:NNZ] = rows_ref[:, x].astype(f32)
-        out[NNZ:2 * NNZ] = signs_ref[:, x].astype(f32)
+def planes_body(ids_ref, rows_ref, signs_ref, co_ref, x_first, x_second, y_first, y_second):
+    for out, x in ((x_first, ids_ref[2]), (x_second, NX - 1 - ids_ref[2])):
+        for j in range(NNZ):
+            out[j] = rows_ref[j, x].astype(f32)
+            out[NNZ + j] = signs_ref[j, x].astype(f32)
         out[2 * NNZ] = co_ref[1, x]
-    for out, y in ((y_low, 0), (y_high, NY - 1)):
+    for out, y in ((y_first, ids_ref[3]), (y_second, NY - 1 - ids_ref[3])):
         for x in range(NX):
             for j in range(NNZ):
-                out[j, x:x + 1, :] = rows_ref[j, x, y:y + 1, :].astype(f32)
-                out[NNZ + j, x:x + 1, :] = signs_ref[j, x, y:y + 1, :].astype(f32)
-            out[2 * NNZ, x:x + 1, :] = co_ref[2, x, y:y + 1, :]
-
-
-def planes(rows, signs, coeffs):
+                out[j, x:x + 1, :] = rows_ref[j, x, pl.ds(y, 1), :].astype(f32)
+                out[NNZ + j, x:x + 1, :] = signs_ref[j, x, pl.ds(y, 1), :].astype(f32)
+            out[2 * NNZ, x:x + 1, :] = co_ref[2, x, pl.ds(y, 1), :]
+
+
+def planes(ids, rows, signs, coeffs):
+    vm = pl.BlockSpec(memory_space=pltpu.VMEM)
     along_x = jax.ShapeDtypeStruct((2 * NNZ + 1, NY, NZ), f32)
     along_y = jax.ShapeDtypeStruct((2 * NNZ + 1, NX, NZ), f32)
     return pl.pallas_call(
-        planes_body, out_shape=(along_x, along_x, along_y, along_y), name="planes"
-    )(rows, signs, coeffs)
-
-
-def edge_body(ids_ref, acc_in, bxl_ref, bxu_ref, byl_ref, byu_ref, xl_ref, xu_ref, yl_ref, yu_ref, own_ref, other_ref, acc, terms, hashes, slots):
+        planes_body,
+        in_specs=[pl.BlockSpec(memory_space=pltpu.SMEM), vm, vm, vm],
+        out_shape=(along_x, along_x, along_y, along_y),
+        name="planes",
+    )(ids, rows, signs, coeffs)
+
+
+def edge_body(
+    ids_ref, acc_hbm, bxl_ref, bxu_ref, byl_ref, byu_ref, xl_ref, xu_ref, yl_ref, yu_ref,
+    own_ref, other_ref, acc, terms, hashes, slots, sem,
+):
+    fetch = pltpu.make_async_copy(acc_hbm, acc, sem.at[0])
+    fetch.start()
     put_slots(slots)
-    acc[...] = acc_in[...]
 
     def one(info, v, y_info, place):
         terms[place] = (-info[2 * NNZ, pl.ds(y_info, 1), :] * v.astype(f32)).astype(bf16)
@@ -191,13 +224,16 @@
             lambda j: info[NNZ + j, pl.ds(y_info, 1), :] - 0.5,
         )
 
-    for info, values in ((xl_ref, bxl_ref), (xu_ref, bxu_ref)):
+    for n, (info, values) in enumerate(((xl_ref, bxl_ref), (xu_ref, bxu_ref))):
         def group(y, _):
             one(info, values[0, y], y, y)
             return 0
 
         lax.fori_loop(0, NY, group, 0, unroll=2)
-        acc[K:2 * K, :] += nt(side_by_side(terms, NY), side_by_side(hashes, NY))
+        got = nt(side_by_side(terms, NY), side_by_side(hashes, NY))
+        if n == 0:
+            fetch.wait()
+        acc[K:2 * K, :] += got
 
     def group(x, _):
         one(yl_ref, byl_ref[x, 0], x, x)
@@ -229,30 +265,33 @@
     vm = pl.BlockSpec(memory_space=pltpu.VMEM)
     return pl.pallas_call(
         edge_body,
+        grid_spec=pltpu.PrefetchScalarGridSpec(
+        num_scalar_prefetch=1,
         grid=(1,),
         in_specs=[
-            pl.BlockSpec(memory_space=pltpu.SMEM),
-            vm,
-            pl.BlockSpec((1, NY, K, NZ), lambda i: (0, 0, 0, 0)),
-            pl.BlockSpec((1, NY, K, NZ), lambda i: (NX - 1, 0, 0, 0)),
-            pl.BlockSpec((NX, 1, K, NZ), lambda i: (0, 0, 0, 0)),
-            pl.BlockSpec((NX, 1, K, NZ), lambda i: (0, NY - 1, 0, 0)),
+            pl.BlockSpec(memory_space=pl.ANY),
+            pl.BlockSpec((1, NY, K, NZ), lambda i, ids: (ids[2], 0, 0, 0)),
+            pl.BlockSpec((1, NY, K, NZ), lambda i, ids: (NX - 1 - ids[2], 0, 0, 0)),
+            pl.BlockSpec((NX, 1, K, NZ), lambda i, ids: (0, ids[3], 0, 0)),
+            pl.BlockSpec((NX, 1, K, NZ), lambda i, ids: (0, NY - 1 - ids[3], 0, 0)),
             vm,
             vm,
             vm,
             vm,
         ],
         out_specs=(vm, vm),
-        out_shape=(
-            jax.ShapeDtypeStruct((SIDE, CHUNK, NZ), f32),
-            jax.ShapeDtypeStruct((SIDE, CHUNK, NZ), bf16),
-        ),
         scratch_shapes=[
             pltpu.VMEM((TALL, M), f32),
             pltpu.VMEM((NY, K, NZ), bf16),
             pltpu.VMEM((NY, M, NZ), bf16),
             pltpu.VMEM((ROWS, NZ), bf16),
+            pltpu.SemaphoreType.DMA((1,)),
         ],
+        ),
+        out_shape=(
+            jax.ShapeDtypeStruct((SIDE, CHUNK, NZ), f32),
+            jax.ShapeDtypeStruct((SIDE, CHUNK, NZ), bf16),
+        ),
         compiler_params=pltpu.CompilerParams(vmem_limit_bytes=56 << 20),
         name="edges",
     )(ids, acc, bt, bt, bt, bt, *infos)
@@ -325,7 +364,12 @@
     )(parts)
 
 
-def solve_body(ids_ref, own_ref, other_ref, order_ref, out_ref, st, high, low, extra, weight, wide, scale, xs, rs, ps):
+def finish_body(
+    ids_ref, own_ref, other_ref, order_ref, bt_hbm, out_hbm,
+    st, table, extra, weight, pairs, scale, xs, rs, ps, bt_ref, turned, ready, sems,
+):
+    fetch = pltpu.make_async_copy(bt_hbm, bt_ref, sems.at[0])
+    fetch.start()
     c = ids_ref[0]
     half = TERMS * K // 2
 
@@ -353,18 +397,21 @@
     gram = nt(st[...], st[...])
     projected = nt(source, st[...])
     projected = projected[0:1, :] + (projected[2:3, :] + projected[4:5, :])
-    top = gram.astype(bf16)
-    high[...] = top
-    low[...] = (gram - top.astype(f32)).astype(bf16)
     diagonal = lax.broadcasted_iota(jnp.int32, (K, K), 0) == lax.broadcasted_iota(jnp.int32, (K, K), 1)
     sizes = jnp.zeros((POINTS, K), f32)
     right = jnp.zeros((POINTS, K), f32)
     for q in range(TERMS):
         right = right + weight[q] * projected[:, q * K:(q + 1) * K]
-        for r in range(TERMS):
-            block = gram[q * K:(q + 1) * K, r * K:(r + 1) * K]
-            entries = jnp.sum(jnp.where(diagonal, block, 0.0), axis=0, keepdims=True)
-            sizes = sizes + (weight[q] * weight[r]) * entries
+    for n, (q, r) in enumerate(PAIRS):
+        block = gram[q * K:(q + 1) * K, r * K:(r + 1) * K]
+        if q != r:
+            block = block + gram[r * K:(r + 1) * K, q * K:(q + 1) * K]
+        top = block.astype(bf16)
+        table[0:K, n * K:(n + 1) * K] = top
+        table[K:2 * K, n * K:(n + 1) * K] = (block - top.astype(f32)).astype(bf16)
+        both = weight[q] * weight[r]
+        pairs[n] = both
+        sizes = sizes + both * jnp.sum(jnp.where(diagonal, block, 0.0), axis=0, keepdims=True)
     scale[...] = 1.0 / sizes
     z0 = right * scale[...]
     xs[...] = jnp.zeros((POINTS, K), f32)
@@ -374,17 +421,13 @@
     goal = start * TOL2
 
     def step(rz):
-        p = ps[...]
-        for q in range(TERMS):
-            t = weight[q] * p
-            t_high = t.astype(bf16)
-            wide[0:POINTS, q * K:(q + 1) * K] = t_high
-            wide[POINTS:2 * POINTS, q * K:(q + 1) * K] = (t - t_high.astype(f32)).astype(bf16)
-        both = jnp.dot(wide[...], high[...], preferred_element_type=f32)
-        image = both[:POINTS] + both[POINTS:] + jnp.dot(wide[0:POINTS, :], low[...], preferred_element_type=f32)
-        ap = weight[0] * image[:, 0:K]
-        for q in range(1, TERMS):
-            ap = ap + weight[q] * image[:, q * K:(q + 1) * K]
+        whole = ps[...]
+        short = whole.astype(bf16)
+        p = short.astype(f32)
+        images = jnp.dot(jnp.concatenate([short, short], axis=1), table[...], preferred_element_type=f32)
+        ap = pairs[0] * images[:, 0:K]
+        for n in range(1, len(PAIRS)):
+            ap = ap + pairs[n] * images[:, n * K:(n + 1) * K]
         pap = jnp.sum(p * ap, axis=1, keepdims=True)
         alpha = jnp.where(pap > 0.0, rz / pap, 0.0)
         xs[...] += alpha * p
@@ -393,7 +436,7 @@
         z = r * scale[...]
         new = jnp.sum(r * z, axis=1, keepdims=True)
         beta = jnp.where(rz > 0.0, new / rz, 0.0)
-        ps[...] = z + beta * p
+        ps[...] = z + beta * whole
         return new
 
     def rounds(carry):
@@ -413,59 +456,53 @@
     pick = jnp.where(lax.broadcasted_iota(jnp.int32, (POINTS, POINTS), 0) == wanted, 1.0, 0.0).astype(bf16)
     coef = xs[...].astype(bf16)
     picked = lax.dot_general(pick, coef, (((0,), (0,)), ((), ())), preferred_element_type=f32)
-    out_ref[...] = picked.astype(bf16)
-
-
-def solve(ids, own, other, order):
+    picked = picked.astype(bf16)
+    fetch.wait()
+    gives = []
+    for x in range(NX):
+        slot = x % 2
+        for y in range(0, NY, 2):
+            pair = jnp.concatenate([bt_ref[x, y], bt_ref[x, y + 1]], axis=1)
+            got = jnp.dot(picked, pair, preferred_element_type=f32)
+            for d in range(2):
+                turned[pl.ds(y + d, POINTS, stride=NY), :] = got[:, d * NZ:(d + 1) * NZ]
+        if x >= 2:
+            gives[x - 2].wait()
+        ready[slot] = turned[...].reshape(POINTS, NY, NZ).astype(bf16)
+        give = pltpu.make_async_copy(ready.at[slot], out_hbm.at[:, x], sems.at[1 + slot])
+        give.start()
+        gives.append(give)
+    gives[NX - 2].wait()
+    gives[NX - 1].wait()
+
+
+def finish(ids, own, other, order, bt):
     vm = pl.BlockSpec(memory_space=pltpu.VMEM)
-    wide = (POINTS, K)
-    return pl.pallas_call(
-        solve_body,
-        in_specs=[pl.BlockSpec(memory_space=pltpu.SMEM), vm, vm, vm],
-        out_shape=jax.ShapeDtypeStruct((POINTS, K), bf16),
+    hbm = pl.BlockSpec(memory_space=pl.ANY)
+    each = pltpu.VMEM((POINTS, K), f32)
+    return pl.pallas_call(
+        finish_body,
+        in_specs=[pl.BlockSpec(memory_space=pltpu.SMEM), vm, vm, vm, hbm],
+        out_specs=hbm,
+        out_shape=jax.ShapeDtypeStruct((POINTS, NX, NY, NZ), bf16),
         scratch_shapes=[
             pltpu.VMEM((TERMS * K, M), bf16),
-            pltpu.VMEM((TERMS * K, TERMS * K), bf16),
-            pltpu.VMEM((TERMS * K, TERMS * K), bf16),
+            pltpu.VMEM((2 * K, len(PAIRS) * K), bf16),
             pltpu.VMEM((NZ, NZ), f32),
             pltpu.VMEM((TERMS, POINTS, K), f32),
-            pltpu.VMEM((2 * POINTS, TERMS * K), bf16),
-            pltpu.VMEM(wide, f32),
-            pltpu.VMEM(wide, f32),
-            pltpu.VMEM(wide, f32),
-            pltpu.VMEM(wide, f32),
+            pltpu.VMEM((len(PAIRS), POINTS, K), f32),
+            each,
+            each,
+            each,
+            each,
+            pltpu.VMEM((NX, NY, K, NZ), bf16),
+            pltpu.VMEM((POINTS * NY, NZ), f32),
+            pltpu.VMEM((2, POINTS, NY, NZ), bf16),
+            pltpu.SemaphoreType.DMA((3,)),
         ],
         compiler_params=pltpu.CompilerParams(vmem_limit_bytes=56 << 20),
-        name="solve",
-    )(ids, own, other, order)
-
-
-def fields_body(picked_ref, bt_ref, out_ref, turned):
-    picked = picked_ref[...]
-    for y in range(0, NY, 2):
-        pair = jnp.concatenate([bt_ref[0, y], bt_ref[0, y + 1]], axis=1)
-        got = jnp.dot(picked, pair, preferred_element_type=f32)
-        for d in range(2):
-            turned[pl.ds(y + d, POINTS, stride=NY), :] = got[:, d * NZ:(d + 1) * NZ]
-    out_ref[...] = turned[...].reshape(POINTS, 1, NY, NZ).astype(bf16)
-
-
-def fields_of(picked, bt):
-    return pl.pallas_call(
-        fields_body,
-        grid=(NX,),
-        in_specs=[
-            pl.BlockSpec((POINTS, K), lambda x: (0, 0)),
-            pl.BlockSpec((1, NY, K, NZ), lambda x: (x, 0, 0, 0)),
-        ],
-        out_specs=pl.BlockSpec((POINTS, 1, NY, NZ), lambda x: (0, x, 0, 0)),
-        out_shape=jax.ShapeDtypeStruct((POINTS, NX, NY, NZ), bf16),
-        scratch_shapes=[pltpu.VMEM((POINTS * NY, NZ), f32)],
-        compiler_params=pltpu.CompilerParams(
-            dimension_semantics=("arbitrary",), vmem_limit_bytes=48 << 20
-        ),
-        name="fields",
-    )(picked, bt)
+        name="finish",
+    )(ids, own, other, order, bt)
 
 
 NARROW = ("x", "zl")
@@ -474,24 +511,30 @@
 DEPTH = ("zl", "zh")
 
 
+def swapped(value, axes, pairs):
+    return lax.ppermute(value, axes, pairs + [(j, i) for i, j in pairs])
+
+
 def per_device(basis, rhs, coeffs, rows, signs, params, order):
-    x_low, x_high, y_low, y_high = planes(rows, signs, coeffs)
-    infos = []
-    for axes, count, low, high in ((NARROW, 8, x_low, x_high), (WIDE, 32, y_low, y_high)):
-        infos.append(lax.ppermute(high, axes, [(i, i + 1) for i in range(count - 1)]))
-        infos.append(lax.ppermute(low, axes, [(i + 1, i) for i in range(count - 1)]))
-    core = lax.axis_index("core").astype(jnp.int32)
-    ids = jnp.stack([core, (lax.axis_index("zl") * 4 + lax.axis_index("zh")).astype(jnp.int32)])
+    at = [lax.axis_index(name).astype(jnp.int32) for name in ("zl", "zh", "core")]
+    zl, zh, core = at
+    ids = jnp.stack([core, zl * 4 + zh, (1 - zl) * (NX - 1), (1 - core) * (NY - 1)])
+    x_first, x_second, y_first, y_second = planes(ids, rows, signs, coeffs)
+    pair = [(0, 1)]
+    infos = [
+        swapped(x_first, "zl", pair),
+        swapped(x_second, NARROW, [(i, i + 1) for i in range(1, 7, 2)]),
+        swapped(y_first, "core", pair),
+        swapped(y_second, WIDE, [(i, i + 1) for i in range(1, 31, 2)]),
+    ]
     acc, bt = sketch(basis, rhs, coeffs, rows, signs)
     own, other = edges(ids, acc, bt, infos)
-    swap = [(0, 1), (1, 0)]
-    parts = merge(own, lax.ppermute(other, "core", swap))
+    parts = merge(own, swapped(other, "core", pair))
     parts = lax.all_to_all(parts, FACE, 0, 0, tiled=True)
     parts = lax.all_to_all(first(ids, params, parts), DEPTH, 0, 0, tiled=True)
     mine = lax.all_to_all(second(parts), FACE, 0, 0, tiled=True)
-    theirs = lax.ppermute(mine, "core", swap)
-    picked = solve(ids, mine, theirs, order.reshape(1, POINTS))
-    return fields_of(picked, bt)
+    theirs = swapped(mine, "core", pair)
+    return finish(ids, mine, theirs, order.reshape(1, POINTS), bt)
 
 
 def solution(mesh):

time: 134 us -> 122 us (0.910)
  Pallas kernels: 56.4 us -> 51.7 us
  starting transfers between devices: 16.5 us -> 12.8 us
  blocking collectives: 52.7 us -> 50.1 us
    pallas_call x5 -> x4, Pallas kernels: 50 us -> 45.4 us  [the longest x1 21.1 us: sketch(): pl.pallas_call(sketch_body, in_specs=[vm, vm, hbm, hbm, hbm], out_specs=(...]
    ppermute x6, starting transfers between devices: 16.5 us -> 12.8 us  [swapped(): return lax.ppermute(value, axes, pairs + [(j, i) for i, j in pairs])]
    all_to_all x1, blocking collectives: 17 us -> 14.4 us  [per_device(): parts = lax.all_to_all(first(ids, params, parts), DEPTH, 0, 0, tiled=True)]
    unnamed x18 -> x14, local copies, waits for them, and re-layouts: 3.09 us -> 2.26 us
  transfers between devices with their start and end apart: 6 -> 6, of which waited for: 2 -> 2; matrix products, arithmetic and copies ran while one was open for 0% -> 0% of each run, Pallas kernels for 16% -> 17%
where the time goes in v3:
time: 122 us; the launch traced here: 121 us
  Pallas kernels  51.7 us (42%)
  blocking collectives  50.1 us (41%)
  starting transfers between devices  12.8 us (10%)
  waiting for transfers between devices  3.75 us (3%)
  local copies, waits for them, and re-layouts  2.26 us (2%)
    all_to_all x1, blocking collectives, per_device(): parts = lax.all_to_all(parts, FACE, 0, 0, tiled=True)  22.8 us
    pallas_call x1, Pallas kernels, sketch(): pl.pallas_call(sketch_body, in_specs=[vm, vm, hbm, hbm, hbm], out_specs=(...  21.1 us
    all_to_all x1, blocking collectives, per_device(): parts = lax.all_to_all(first(ids, params, parts), DEPTH, 0, 0, tiled=True)  14.4 us
    pallas_call x1, Pallas kernels, finish(): pl.pallas_call(finish_body, in_specs=[pl.BlockSpec(memory_space=pltpu.SME...  13.7 us
    all_to_all x1, blocking collectives, per_device(): mine = lax.all_to_all(second(parts), FACE, 0, 0, tiled=True)  12.9 us
    ppermute x6, starting transfers between devices, swapped(): return lax.ppermute(value, axes, pairs + [(j, i) for i, j in pairs])  12.8 us
    pallas_call x1, Pallas kernels, edges(): pl.pallas_call(edge_body, grid_spec=pltpu.PrefetchScalarGridSpec(num_scal...  8.9 us
    ppermute x6, waiting for transfers between devices, swapped(): return lax.ppermute(value, axes, pairs + [(j, i) for i, j in pairs])  3.75 us
  transfers between devices with their start and end apart: 6, of which 2 were waited for; matrix products, arithmetic and copies ran while one was open for 0% of the time, Pallas kernels for 17%

profile of v3, /device:TPU:1, one launch (start us, length us, event | category | flops | bytes accessed | tf_op | source)
XLA Modules:
  0.0 121.5 jit_solution(4801709212219468690)
XLA Ops:
  0.0 0.6 pad_add_fusion.ids_ref
  0.6 1.8 %planes.1 = (f32[9,16,128]{2,1,0:T(8,128)}, f32[9,16,128]{2,1,0:T(8,128)}, f32[9,4,128]{2,1,0:T(4,128)}, f32[9,4,128]{2,1,0:T(4,128)}) custom-call(s32[4]{0:T(128)} %pad_add_fusion.ids_ref, s32[4,4,16,128]{3,2,1,0:T(8,128)} %rows_ref.1, s32[4,4,16,128]{3,2,1,0:T(8,128)} %signs_ref.1, f32[4,4,16,128]{3,2,1,0:T(8,128)} %co_ref.1), custom_call_target="tpu_custom_call" | custom-call | tf_op jit(solution)/shard_map/planes/pallas_call | solution.py:201
  2.3 2.5 %collective-permute-start = (f32[9,16,128]{2,1,0:T(8,128)}, f32[9,16,128]{2,1,0:T(8,128)S(1)}, u32[]{:S(2)}, u32[]{:S(2)}) collective-permute-start(f32[9,16,128]{2,1,0:T(8,128)} %get-tuple-element.15), channel_id=1, source_target_pairs={{0,32},{32,0},{1,33},{33,1},{2,34},{34,2},{3,35},{35,3},{4,36},{36... | collective-permute-start | bytes 221192 | tf_op jit(solution)/shard_map/ppermute | solution.py:515
  4.8 0.7 collective-permute-start.1
  5.5 1.0 collective-permute-start.2
  6.5 4.8 %collective-permute-start.3 = (f32[9,4,128]{2,1,0:T(4,128)}, f32[9,4,128]{2,1,0:T(4,128)S(1)}, u32[]{:S(2)}, u32[]{:S(2)}) collective-permute-start(f32[9,4,128]{2,1,0:T(4,128)} %get-tuple-element.18), channel_id=1, source_target_pairs={{1,2},{3,4},{5,6},{7,8},{9,10},{11,12},{13,14},{15,16},{17,18},{19... | collective-permute-start | bytes 55304 | tf_op jit(solution)/shard_map/ppermute | solution.py:515
  11.3 21.1 %sketch.1 = (f32[528,1024]{1,0:T(8,128)}, bf16[4,16,128,128]{3,2,1,0:T(8,128)(2,1)}) custom-call(bf16[128,4,16,128]{3,2,1,0:T(8,128)(2,1)} %basis_ref.1, bf16[4,16,128]{2,1,0:T(8,128)(2,1)} %rhs_ref.1, f32[4,4,16,128]{3,2,1,0:T(8,128)} %co_ref.1, s32[4,4,16,128]{3,2,1,0:T(8,128)} %rows_ref.1, s32[4,4,16,128]{3,2,1,0:T(8,128)} %signs_ref.1), custom_call_target="tpu_custom_call" | custom-call | tf_op jit(solution)/shard_map/sketch/pallas_call | solution.py:158
  32.4 0.0 collective-permute-done.2.yl_ref
  32.4 0.0 copy-start.5
  32.4 0.0 collective-permute-done.3.yu_ref
  32.4 0.0 copy-start.6
  32.4 0.0 collective-permute-done.xl_ref
  32.5 0.0 copy-start.3
  32.5 0.0 collective-permute-done.1.xu_ref
  32.5 0.0 copy-start.4
  32.5 0.5 copy-done.5
  33.0 0.0 copy-done.6
  33.0 0.0 copy-done.3
  33.1 0.0 copy-done.4
  33.1 8.9 %edges.1 = (f32[16,136,128]{2,1,0:T(8,128)}, bf16[16,136,128]{2,1,0:T(8,128)(2,1)}) custom-call(s32[4]{0:T(128)} %pad_add_fusion.ids_ref, f32[528,1024]{1,0:T(8,128)} %get-tuple-element.13.acc_hbm, bf16[4,16,128,128]{3,2,1,0:T(8,128)(2,1)} %get-tuple-element.14.bxl_ref.bxu_ref.byl_ref.byu_ref.bt_hbm, ...), custom_call_target="tpu_custom_call" | custom-call | tf_op jit(solution)/shard_map/edges/pallas_call | solution.py:266
  42.0 0.1 collective-permute-start.4
  42.1 2.2 %collective-permute-done.4.got_ref = bf16[16,136,128]{2,1,0:T(8,128)(2,1)S(1)} collective-permute-done((bf16[16,136,128]{2,1,0:T(8,128)(2,1)}, bf16[16,136,128]{2,1,0:T(8,128)(2,1)S(1)}, u32[]{:S(2)}, u32[]{:S(2)}) %collective-permute-start.4) | collective-permute-done | bytes 557088 | tf_op jit(solution)/shard_map/ppermute | solution.py:515
  44.3 0.0 copy-start.1
  44.3 0.8 copy-done.1
  45.1 2.6 %merge.1 = bf16[16,136,128]{2,1,0:T(8,128)(2,1)} custom-call(f32[16,136,128]{2,1,0:T(8,128)} %get-tuple-element.19.own_ref, bf16[16,136,128]{2,1,0:T(8,128)(2,1)} %copy-done.1), custom_call_target="tpu_custom_call" | custom-call | tf_op jit(solution)/shard_map/merge/pallas_call | solution.py:310
  47.7 22.8 %all_to_all.15.parts_ref = bf16[16,136,128]{2,1,0:T(8,128)(2,1)} all-to-all(bf16[16,136,128]{2,1,0:T(8,128)(2,1)} %merge.1), channel_id=1, replica_groups=mesh['x'=4,'zl'=2,'y'=4,'zh'=4,'core'=2] {'x','y'}, dimensions={0} | all-to-all | bytes 1114112 | tf_op jit(solution)/shard_map/all_to_all | solution.py:533
  70.5 1.9 %first.1 = bf16[8,136,128]{2,1,0:T(8,128)(2,1)} custom-call(s32[4]{0:T(128)} %pad_add_fusion.ids_ref, f32[1,4]{1,0:T(1,128)} %params_ref.1, bf16[16,136,128]{2,1,0:T(8,128)(2,1)} %all_to_all.15.parts_ref), custom_call_target="tpu_custom_call" | custom-call | tf_op jit(solution)/shard_map/first/pallas_call | solution.py:345
  72.3 14.4 %all_to_all.16.parts_ref = bf16[8,136,128]{2,1,0:T(8,128)(2,1)} all-to-all(bf16[8,136,128]{2,1,0:T(8,128)(2,1)} %first.1), channel_id=1, replica_groups=mesh['x'=4,'zl'=2,'y'=4,'zh'=4,'core'=2] {'zl','zh'}, dimensions={0} | all-to-all | bytes 557056 | tf_op jit(solution)/shard_map/all_to_all | solution.py:534
  86.7 1.8 %second.1 = bf16[16,136,128]{2,1,0:T(8,128)(2,1)} custom-call(bf16[8,136,128]{2,1,0:T(8,128)(2,1)} %all_to_all.16.parts_ref), custom_call_target="tpu_custom_call" | custom-call | tf_op jit(solution)/shard_map/second/pallas_call | solution.py:360
  88.6 12.9 %all_to_all.17.own_ref = bf16[16,136,128]{2,1,0:T(8,128)(2,1)S(1)} all-to-all(bf16[16,136,128]{2,1,0:T(8,128)(2,1)} %second.1), channel_id=1, replica_groups=mesh['x'=4,'zl'=2,'y'=4,'zh'=4,'core'=2] {'x','y'}, dimensions={0} | all-to-all | bytes 1114112 | tf_op jit(solution)/shard_map/all_to_all | solution.py:535
  101.5 0.0 copy-start
  101.5 3.8 %collective-permute-start.5 = (bf16[16,136,128]{2,1,0:T(8,128)(2,1)S(1)}, bf16[16,136,128]{2,1,0:T(8,128)(2,1)S(1)}, u32[]{:S(2)}, u32[]{:S(2)}) collective-permute-start(bf16[16,136,128]{2,1,0:T(8,128)(2,1)S(1)} %all_to_all.17.own_ref), channel_id=1, source_target_pairs={{0,1},{1,0},{2,3},{3,2},{4,5},{5,4},{6,7},{7,6},{8,9},{9,8},{10,11... | collective-permute-start | bytes 1671176 | tf_op jit(solution)/shard_map/ppermute | solution.py:515
  105.2 1.6 %collective-permute-done.5.other_ref = bf16[16,136,128]{2,1,0:T(8,128)(2,1)S(1)} collective-permute-done((bf16[16,136,128]{2,1,0:T(8,128)(2,1)S(1)}, bf16[16,136,128]{2,1,0:T(8,128)(2,1)S(1)}, u32[]{:S(2)}, u32[]{:S(2)}) %collective-permute-start.5) | collective-permute-done | bytes 557088 | tf_op jit(solution)/shard_map/ppermute | solution.py:515
  106.8 0.0 copy-start.2
  106.8 0.0 copy-done
  106.8 0.8 copy-done.2
  107.6 13.7 %finish.1 = bf16[256,4,16,128]{3,2,1,0:T(8,128)(2,1)} custom-call(s32[4]{0:T(128)} %pad_add_fusion.ids_ref, bf16[16,136,128]{2,1,0:T(8,128)(2,1)} %copy-done, bf16[16,136,128]{2,1,0:T(8,128)(2,1)} %copy-done.2, s32[1,256]{1,0:T(1,128)} %bitcast.5, bf16[4,16,128,128]{3,2,1,0:T(8,128)(2,1)} %get-tuple-element.14.bxl_ref.bxu_ref.byl_ref.byu_ref.bt_hbm), custom_call_target="tpu_custom_call" | custom-call | tf_op jit(solution)/shard_map/finish/pallas_call | solution.py:483
Async XLA Ops:
  2.3 30.1 %collective-permute-start = (f32[9,16,128]{2,1,0:T(8,128)}, f32[9,16,128]{2,1,0:T(8,128)S(1)}, u32[]{:S(2)}, u32[]{:S(2)}) collective-permute-start(f32[9,16,128]{2,1,0:T(8,128)} %get-tuple-element.15), channel_id=1, source_target_pairs={{0,32},{32,0},{1,33},{33,1},{2,34},{34,2},{3,35},{35,3},{4,36},{36... | collective-permute-start | bytes 221192 | tf_op jit(solution)/shard_map/ppermute | solution.py:515
  4.8 27.7 %collective-permute-start.1 = (f32[9,16,128]{2,1,0:T(8,128)}, f32[9,16,128]{2,1,0:T(8,128)S(1)}, u32[]{:S(2)}, u32[]{:S(2)}) collective-permute-start(f32[9,16,128]{2,1,0:T(8,128)} %get-tuple-element.16), channel_id=1, source_target_pairs={{32,64},{96,128},{160,192},{64,32},{128,96},{192,160},{33,65},{97,... | collective-permute-start | bytes 221192 | tf_op jit(solution)/shard_map/ppermute | solution.py:515
  5.5 26.9 %collective-permute-start.2 = (f32[9,4,128]{2,1,0:T(4,128)}, f32[9,4,128]{2,1,0:T(4,128)S(1)}, u32[]{:S(2)}, u32[]{:S(2)}) collective-permute-start(f32[9,4,128]{2,1,0:T(4,128)} %get-tuple-element.17), channel_id=1, source_target_pairs={{0,1},{1,0},{2,3},{3,2},{4,5},{5,4},{6,7},{7,6},{8,9},{9,8},{10,11... | collective-permute-start | bytes 55304 | tf_op jit(solution)/shard_map/ppermute | solution.py:515
  6.5 25.9 %collective-permute-start.3 = (f32[9,4,128]{2,1,0:T(4,128)}, f32[9,4,128]{2,1,0:T(4,128)S(1)}, u32[]{:S(2)}, u32[]{:S(2)}) collective-permute-start(f32[9,4,128]{2,1,0:T(4,128)} %get-tuple-element.18), channel_id=1, source_target_pairs={{1,2},{3,4},{5,6},{7,8},{9,10},{11,12},{13,14},{15,16},{17,18},{19... | collective-permute-start | bytes 55304 | tf_op jit(solution)/shard_map/ppermute | solution.py:515
  32.4 0.6 copy-start.5
  32.4 0.6 copy-start.6
  32.5 0.6 copy-start.3
  32.5 0.7 copy-start.4
  42.0 2.3 %collective-permute-start.4 = (bf16[16,136,128]{2,1,0:T(8,128)(2,1)}, bf16[16,136,128]{2,1,0:T(8,128)(2,1)S(1)}, u32[]{:S(2)}, u32[]{:S(2)}) collective-permute-start(bf16[16,136,128]{2,1,0:T(8,128)(2,1)} %get-tuple-element.20), channel_id=1, source_target_pairs={{0,1},{1,0},{2,3},{3,2},{4,5},{5,4},{6,7},{7,6},{8,9},{9,8},{10,11... | collective-permute-start | bytes 1671176 | tf_op jit(solution)/shard_map/ppermute | solution.py:515
  44.3 0.8 copy-start.1
  101.5 5.4 %copy-start = (bf16[16,136,128]{2,1,0:T(8,128)(2,1)}, bf16[16,136,128]{2,1,0:T(8,128)(2,1)S(1)}, u32[]{:S(2)}) copy-start(bf16[16,136,128]{2,1,0:T(8,128)(2,1)S(1)} %all_to_all.17.own_ref) | copy-start | bytes 1671172
  101.5 5.4 %collective-permute-start.5 = (bf16[16,136,128]{2,1,0:T(8,128)(2,1)S(1)}, bf16[16,136,128]{2,1,0:T(8,128)(2,1)S(1)}, u32[]{:S(2)}, u32[]{:S(2)}) collective-permute-start(bf16[16,136,128]{2,1,0:T(8,128)(2,1)S(1)} %all_to_all.17.own_ref), channel_id=1, source_target_pairs={{0,1},{1,0},{2,3},{3,2},{4,5},{5,4},{6,7},{7,6},{8,9},{9,8},{10,11... | collective-permute-start | bytes 1671176 | tf_op jit(solution)/shard_map/ppermute | solution.py:515
  106.8 0.8 copy-start.2

commit v4 on v3

--- a/solution.py
+++ b/solution.py
@@ -16,13 +16,14 @@
 NZ = 128
 CELLS = NY * NZ
 TALL = TERMS * K + 16
+PART = 256
 CHIPS = 128
 SIDE = 16
 DEEP = 8
 BODY = 128
 CHUNK = BODY + 8
 POINTS = 256
-TOL2 = 1e-10
+TOL2 = 1e-9
 MAX_ROUNDS = 256
 PAIRS = tuple((q, r) for q in range(TERMS) for r in range(q, TERMS))
 
@@ -52,6 +53,12 @@
     return jnp.concatenate([ref[y] for y in range(count)], axis=1)
 
 
+def turning():
+    out = lax.broadcasted_iota(jnp.int32, (16 * NY, 16 * NY), 0)
+    src = lax.broadcasted_iota(jnp.int32, (16 * NY, 16 * NY), 1)
+    return jnp.where((out // 16 == src % 16) & (out % 16 == src // 16), 1.0, 0.0).astype(bf16)
+
+
 def in_three(extra):
     high = extra.astype(bf16).astype(f32)
     rest = extra - high
@@ -66,12 +73,15 @@
 
 
 def sketch_body(
-    basis_ref, rhs_ref, co_hbm, rows_hbm, signs_hbm, acc_ref, bt_hbm,
-    pad, terms, hashes, source_ref, slots, co_ref, rows_ref, signs_ref, bt_ref, sems,
+    basis_hbm, rhs_ref, co_hbm, rows_hbm, signs_hbm, acc_hbm, bt_hbm,
+    pad, terms, hashes, terms_b, hashes_b, source_ref, slots, basis_ref, co_ref, rows_ref, signs_ref, bt_ref, acc_ref,
+    sems, out_sems,
 ):
     fetches = [
         pltpu.make_async_copy(src, dst, sems.at[i])
-        for i, (src, dst) in enumerate(((co_hbm, co_ref), (rows_hbm, rows_ref), (signs_hbm, signs_ref)))
+        for i, (src, dst) in enumerate(
+            ((basis_hbm, basis_ref), (co_hbm, co_ref), (rows_hbm, rows_ref), (signs_hbm, signs_ref))
+        )
     ]
     for fetch in fetches:
         fetch.start()
@@ -82,9 +92,9 @@
     for x in range(NX):
         pad[x + 1, 0] = jnp.zeros((K, NZ), f32)
         pad[x + 1, NY + 1] = jnp.zeros((K, NZ), f32)
-    out = lax.broadcasted_iota(jnp.int32, (16 * NY, 16 * NY), 0)
-    src = lax.broadcasted_iota(jnp.int32, (16 * NY, 16 * NY), 1)
-    turn = jnp.where((out // 16 == src % 16) & (out % 16 == src // 16), 1.0, 0.0).astype(bf16)
+    turn = turning()
+    source_ref[...] = rhs_ref[...].astype(f32)
+    fetches[0].wait()
 
     def turned(i, _):
         k = pl.multiple_of(i * 16, 16)
@@ -101,54 +111,63 @@
         return 0
 
     lax.fori_loop(0, K // 16, turned, 0)
-    give = pltpu.make_async_copy(bt_ref, bt_hbm, sems.at[3])
+    give = pltpu.make_async_copy(bt_ref, bt_hbm, sems.at[4])
     give.start()
-    for fetch in fetches:
+    for fetch in fetches[1:]:
         fetch.wait()
     lane = lax.broadcasted_iota(jnp.int32, (1, NZ), 1)
-
-    def plane(x, _):
-        source_ref[...] = rhs_ref[x].astype(f32)
-
-        def group(y, _):
-            c0, c1, c2, c3 = (co_ref[q, x, pl.ds(y, 1), :] for q in range(TERMS))
-            low3 = jnp.where(lane == 0, 0.0, c3)
-            up3 = jnp.where(lane == NZ - 1, 0.0, c3)
-            for k in range(0, K, 16):
-                at = slice(k, k + 16)
-                v = pad[x + 1, y + 1, at, :]
-                v2 = v + v
-                along_x = v2 - pad[x, y + 1, at, :] - pad[x + 2, y + 1, at, :]
-                along_y = v2 - pad[x + 1, y, at, :] - pad[x + 1, y + 2, at, :]
-                t3 = c3 * v2 - low3 * pltpu.roll(v, 1, 1) - up3 * pltpu.roll(v, NZ - 1, 1)
-                for q, t in enumerate((c0 * v, c1 * along_x, c2 * along_y, t3)):
-                    terms[y, q * K + k:q * K + k + 16, :] = t.astype(bf16)
-            top = lax.broadcasted_iota(jnp.int32, (16, NZ), 0) == 0
-            source = source_ref[pl.ds(y, 1), :]
-            terms[y, TERMS * K:TALL, :] = jnp.where(top, source, 0.0).astype(bf16)
-            put_hash(
-                hashes,
-                slots,
-                y,
-                lambda j: rows_ref[j, x, pl.ds(y, 1), :].astype(f32),
-                lambda j: signs_ref[j, x, pl.ds(y, 1), :].astype(f32) - 0.5,
+    top = lax.broadcasted_iota(jnp.int32, (16, NZ), 0) == 0
+
+    def build(x, y, terms, hashes):
+        c0, c1, c2, c3 = (co_ref[q, x, pl.ds(y, 1), :] for q in range(TERMS))
+        low3 = jnp.where(lane == 0, 0.0, c3)
+        up3 = jnp.where(lane == NZ - 1, 0.0, c3)
+        for k in range(0, K, 16):
+            at = slice(k, k + 16)
+            v = pad[x + 1, y + 1, at, :]
+            v2 = v + v
+            along_x = v2 - pad[x, y + 1, at, :] - pad[x + 2, y + 1, at, :]
+            along_y = v2 - pad[x + 1, y, at, :] - pad[x + 1, y + 2, at, :]
+            t3 = c3 * v2 - low3 * pltpu.roll(v, 1, 1) - up3 * pltpu.roll(v, NZ - 1, 1)
+            for q, t in enumerate((c0 * v, c1 * along_x, c2 * along_y, t3)):
+                terms[y, q * K + k:q * K + k + 16, :] = t.astype(bf16)
+        source = source_ref[x, pl.ds(y, 1), :]
+        terms[y, TERMS * K:TALL, :] = jnp.where(top, source, 0.0).astype(bf16)
+        put_hash(
+            hashes,
+            slots,
+            y,
+            lambda j: rows_ref[j, x, pl.ds(y, 1), :].astype(f32),
+            lambda j: signs_ref[j, x, pl.ds(y, 1), :].astype(f32) - 0.5,
+        )
+
+    buffers = ((terms, hashes), (terms_b, hashes_b))
+
+    def opening(y, _):
+        build(0, y, *buffers[0])
+        return 0
+
+    lax.fori_loop(0, NY, opening, 0, unroll=2)
+    for x in range(NX):
+        t, h = buffers[x % 2]
+
+        def block(i, _):
+            cols = pl.multiple_of(i * PART, PART)
+            got = nt(
+                side_by_side(t, NY),
+                jnp.concatenate([h[y, pl.ds(cols, PART), :] for y in range(NY)], axis=1),
             )
+            acc_ref[i] = got if x == 0 else acc_ref[i] + got
+            if x + 1 < NX:
+                for d in range(4):
+                    build(x + 1, i * 4 + d, *buffers[(x + 1) % 2])
+            else:
+                pltpu.make_async_copy(acc_ref.at[i], acc_hbm.at[i], out_sems.at[i]).start()
             return 0
 
-        lax.fori_loop(0, NY, group, 0, unroll=2)
-        got = nt(side_by_side(terms, NY), side_by_side(hashes, NY))
-
-        @pl.when(x == 0)
-        def _():
-            acc_ref[...] = got
-
-        @pl.when(x > 0)
-        def _():
-            acc_ref[...] += got
-
-        return 0
-
-    lax.fori_loop(0, NX, plane, 0)
+        lax.fori_loop(0, M // PART, block, 0)
+    for i in range(M // PART):
+        pltpu.make_async_copy(acc_ref.at[i], acc_hbm.at[i], out_sems.at[i]).wait()
     give.wait()
 
 
@@ -157,36 +176,46 @@
     hbm = pl.BlockSpec(memory_space=pl.ANY)
     return pl.pallas_call(
         sketch_body,
-        in_specs=[vm, vm, hbm, hbm, hbm],
-        out_specs=(vm, hbm),
+        in_specs=[hbm, vm, hbm, hbm, hbm],
+        out_specs=(hbm, hbm),
         out_shape=(
-            jax.ShapeDtypeStruct((TALL, M), f32),
+            jax.ShapeDtypeStruct((M // PART, TALL, PART), f32),
             jax.ShapeDtypeStruct((NX, NY, K, NZ), bf16),
         ),
         scratch_shapes=[
             pltpu.VMEM((NX + 2, NY + 2, K, NZ), f32),
             pltpu.VMEM((NY, TALL, NZ), bf16),
             pltpu.VMEM((NY, M, NZ), bf16),
-            pltpu.VMEM((NY, NZ), f32),
+            pltpu.VMEM((NY, TALL, NZ), bf16),
+            pltpu.VMEM((NY, M, NZ), bf16),
+            pltpu.VMEM((NX, NY, NZ), f32),
             pltpu.VMEM((ROWS, NZ), bf16),
+            pltpu.VMEM((K, NX, NY, NZ), bf16),
             pltpu.VMEM((TERMS, NX, NY, NZ), f32),
             pltpu.VMEM((NNZ, NX, NY, NZ), jnp.int32),
             pltpu.VMEM((NNZ, NX, NY, NZ), jnp.int32),
             pltpu.VMEM((NX, NY, K, NZ), bf16),
-            pltpu.SemaphoreType.DMA((4,)),
+            pltpu.VMEM((M // PART, TALL, PART), f32),
+            pltpu.SemaphoreType.DMA((5,)),
+            pltpu.SemaphoreType.DMA((M // PART,)),
         ],
         compiler_params=pltpu.CompilerParams(vmem_limit_bytes=56 << 20),
         name="sketch",
     )(basis, rhs, coeffs, rows, signs)
 
 
-def planes_body(ids_ref, rows_ref, signs_ref, co_ref, x_first, x_second, y_first, y_second):
-    for out, x in ((x_first, ids_ref[2]), (x_second, NX - 1 - ids_ref[2])):
+def planes_body(rows_ref, signs_ref, co_ref, x_first, x_second, y_first, y_second, ids_ref):
+    zl, zh, core = (lax.axis_index(name).astype(jnp.int32) for name in ("zl", "zh", "core"))
+    plane = (1 - zl) * (NX - 1)
+    line = (1 - core) * (NY - 1)
+    for n, value in enumerate((core, zl * 4 + zh, plane, line)):
+        ids_ref[n] = value
+    for out, x in ((x_first, plane), (x_second, NX - 1 - plane)):
         for j in range(NNZ):
             out[j] = rows_ref[j, x].astype(f32)
             out[NNZ + j] = signs_ref[j, x].astype(f32)
         out[2 * NNZ] = co_ref[1, x]
-    for out, y in ((y_first, ids_ref[3]), (y_second, NY - 1 - ids_ref[3])):
+    for out, y in ((y_first, line), (y_second, NY - 1 - line)):
         for x in range(NX):
             for j in range(NNZ):
                 out[j, x:x + 1, :] = rows_ref[j, x, pl.ds(y, 1), :].astype(f32)
@@ -194,16 +223,17 @@
             out[2 * NNZ, x:x + 1, :] = co_ref[2, x, pl.ds(y, 1), :]
 
 
-def planes(ids, rows, signs, coeffs):
+def planes(rows, signs, coeffs):
     vm = pl.BlockSpec(memory_space=pltpu.VMEM)
     along_x = jax.ShapeDtypeStruct((2 * NNZ + 1, NY, NZ), f32)
     along_y = jax.ShapeDtypeStruct((2 * NNZ + 1, NX, NZ), f32)
     return pl.pallas_call(
         planes_body,
-        in_specs=[pl.BlockSpec(memory_space=pltpu.SMEM), vm, vm, vm],
-        out_shape=(along_x, along_x, along_y, along_y),
+        in_specs=[vm, vm, vm],
+        out_specs=(vm, vm, vm, vm, pl.BlockSpec(memory_space=pltpu.SMEM)),
+        out_shape=(along_x, along_x, along_y, along_y, jax.ShapeDtypeStruct((4,), jnp.int32)),
         name="planes",
-    )(ids, rows, signs, coeffs)
+    )(rows, signs, coeffs)
 
 
 def edge_body(
@@ -233,7 +263,8 @@
         got = nt(side_by_side(terms, NY), side_by_side(hashes, NY))
         if n == 0:
             fetch.wait()
-        acc[K:2 * K, :] += got
+        for n in range(M // PART):
+            acc[n, K:2 * K, :] += got[:, n * PART:(n + 1) * PART]
 
     def group(x, _):
         one(yl_ref, byl_ref[x, 0], x, x)
@@ -241,7 +272,9 @@
         return 0
 
     lax.fori_loop(0, NX, group, 0)
-    acc[2 * K:3 * K, :] += nt(side_by_side(terms, 2 * NX), side_by_side(hashes, 2 * NX))
+    got = nt(side_by_side(terms, 2 * NX), side_by_side(hashes, 2 * NX))
+    for n in range(M // PART):
+        acc[n, 2 * K:3 * K, :] += got[:, n * PART:(n + 1) * PART]
     c = ids_ref[0]
     row = lax.broadcasted_iota(jnp.int32, (8, NZ), 0)
 
@@ -249,10 +282,11 @@
         mine = pl.multiple_of(c * 2 * K + i * 16, 16)
         theirs = pl.multiple_of((1 - c) * 2 * K + i * 16, 16)
         for l in range(M // NZ):
-            own_ref[i, l * 16:l * 16 + 16, :] = acc[pl.ds(mine, 16), l * NZ:(l + 1) * NZ]
-            other_ref[i, l * 16:l * 16 + 16, :] = acc[pl.ds(theirs, 16), l * NZ:(l + 1) * NZ].astype(bf16)
-        lane = pl.multiple_of(jnp.minimum(i, M // NZ - 1) * NZ, NZ)
-        source = acc[TERMS * K:TERMS * K + 8, pl.ds(lane, NZ)]
+            n, lanes = l // 2, slice((l % 2) * NZ, (l % 2 + 1) * NZ)
+            own_ref[i, l * 16:l * 16 + 16, :] = acc[n, pl.ds(mine, 16), lanes]
+            other_ref[i, l * 16:l * 16 + 16, :] = acc[n, pl.ds(theirs, 16), lanes].astype(bf16)
+        part = jnp.minimum(i, M // NZ - 1)
+        source = acc[part // 2, TERMS * K:TERMS * K + 8, pl.ds(pl.multiple_of((part % 2) * NZ, NZ), NZ)]
         source = jnp.where((row == 0) & (i < M // NZ), source, 0.0)
         own_ref[i, BODY:CHUNK, :] = source
         other_ref[i, BODY:CHUNK, :] = in_three(source)
@@ -281,7 +315,7 @@
         ],
         out_specs=(vm, vm),
         scratch_shapes=[
-            pltpu.VMEM((TALL, M), f32),
+            pltpu.VMEM((M // PART, TALL, PART), f32),
             pltpu.VMEM((NY, K, NZ), bf16),
             pltpu.VMEM((NY, M, NZ), bf16),
             pltpu.VMEM((ROWS, NZ), bf16),
@@ -297,19 +331,50 @@
     )(ids, acc, bt, bt, bt, bt, *infos)
 
 
-def merge_body(own_ref, got_ref, out_ref):
-    def add(i, _):
-        out_ref[i, 0:BODY, :] = (own_ref[i, 0:BODY, :] + got_ref[i, 0:BODY, :].astype(f32)).astype(bf16)
-        out_ref[i, BODY:CHUNK, :] = in_three(own_ref[i, BODY:CHUNK, :] + from_three(got_ref[i, BODY:CHUNK, :]))
-        return 0
-
-    lax.fori_loop(0, SIDE, add, 0)
+def merge_body(own_hbm, got_hbm, out_hbm, own_ref, got_ref, out_ref, sems):
+    size = SIDE // 4
+    fetches = [
+        [
+            pltpu.make_async_copy(src.at[pl.ds(g * size, size)], dst.at[pl.ds(g * size, size)], sems.at[n, g])
+            for n, (src, dst) in enumerate(((own_hbm, own_ref), (got_hbm, got_ref)))
+        ]
+        for g in range(4)
+    ]
+    for pair in fetches:
+        for fetch in pair:
+            fetch.start()
+    gives = []
+    for g in range(4):
+        for fetch in fetches[g]:
+            fetch.wait()
+
+        def add(i, _):
+            out_ref[i, 0:BODY, :] = (own_ref[i, 0:BODY, :] + got_ref[i, 0:BODY, :].astype(f32)).astype(bf16)
+            out_ref[i, BODY:CHUNK, :] = in_three(own_ref[i, BODY:CHUNK, :] + from_three(got_ref[i, BODY:CHUNK, :]))
+            return 0
+
+        lax.fori_loop(g * size, (g + 1) * size, add, 0)
+        part = pl.ds(g * size, size)
+        give = pltpu.make_async_copy(out_ref.at[part], out_hbm.at[part], sems.at[2, g])
+        give.start()
+        gives.append(give)
+    for give in gives:
+        give.wait()
 
 
 def merge(own, got):
+    hbm = pl.BlockSpec(memory_space=pl.ANY)
     return pl.pallas_call(
         merge_body,
+        in_specs=[hbm, hbm],
+        out_specs=hbm,
         out_shape=jax.ShapeDtypeStruct((SIDE, CHUNK, NZ), bf16),
+        scratch_shapes=[
+            pltpu.VMEM((SIDE, CHUNK, NZ), f32),
+            pltpu.VMEM((SIDE, CHUNK, NZ), bf16),
+            pltpu.VMEM((SIDE, CHUNK, NZ), bf16),
+            pltpu.SemaphoreType.DMA((3, 4)),
+        ],
         name="merge",
     )(own, got)
 
@@ -365,11 +430,19 @@
 
 
 def finish_body(
-    ids_ref, own_ref, other_ref, order_ref, bt_hbm, out_hbm,
-    st, table, extra, weight, pairs, scale, xs, rs, ps, bt_ref, turned, ready, sems,
+    ids_ref, own_hbm, other_hbm, order_ref, bt_hbm, out_hbm, own_ref, other_ref,
+    st, table, extra, weight, pairs, scale, xs, rs, ps, bt_ref, lines, ready, sems,
 ):
+    halves = [
+        pltpu.make_async_copy(own_hbm, own_ref, sems.at[3]),
+        pltpu.make_async_copy(other_hbm, other_ref, sems.at[4]),
+    ]
+    for half in halves:
+        half.start()
     fetch = pltpu.make_async_copy(bt_hbm, bt_ref, sems.at[0])
     fetch.start()
+    for half in halves:
+        half.wait()
     c = ids_ref[0]
     half = TERMS * K // 2
 
@@ -458,17 +531,28 @@
     picked = lax.dot_general(pick, coef, (((0,), (0,)), ((), ())), preferred_element_type=f32)
     picked = picked.astype(bf16)
     fetch.wait()
+    turn = turning()
     gives = []
     for x in range(NX):
         slot = x % 2
         for y in range(0, NY, 2):
             pair = jnp.concatenate([bt_ref[x, y], bt_ref[x, y + 1]], axis=1)
-            got = jnp.dot(picked, pair, preferred_element_type=f32)
+            got = jnp.dot(picked, pair, preferred_element_type=f32).astype(bf16)
             for d in range(2):
-                turned[pl.ds(y + d, POINTS, stride=NY), :] = got[:, d * NZ:(d + 1) * NZ]
+                lines[y + d] = got[:, d * NZ:(d + 1) * NZ]
         if x >= 2:
             gives[x - 2].wait()
-        ready[slot] = turned[...].reshape(POINTS, NY, NZ).astype(bf16)
+        for j in range(0, POINTS, 32):
+            stack = jnp.concatenate(
+                [
+                    jnp.concatenate([lines[y, j + d * 16:j + d * 16 + 16, :] for y in range(NY)], axis=0)
+                    for d in range(2)
+                ],
+                axis=1,
+            )
+            got = jnp.dot(turn, stack, preferred_element_type=f32).astype(bf16)
+            for d in range(2):
+                ready[slot, j + d * 16:j + d * 16 + 16] = got[:, d * NZ:(d + 1) * NZ].reshape(16, NY, NZ)
         give = pltpu.make_async_copy(ready.at[slot], out_hbm.at[:, x], sems.at[1 + slot])
         give.start()
         gives.append(give)
@@ -482,10 +566,12 @@
     each = pltpu.VMEM((POINTS, K), f32)
     return pl.pallas_call(
         finish_body,
-        in_specs=[pl.BlockSpec(memory_space=pltpu.SMEM), vm, vm, vm, hbm],
+        in_specs=[pl.BlockSpec(memory_space=pltpu.SMEM), hbm, hbm, vm, hbm],
         out_specs=hbm,
         out_shape=jax.ShapeDtypeStruct((POINTS, NX, NY, NZ), bf16),
         scratch_shapes=[
+            pltpu.VMEM((SIDE, CHUNK, NZ), bf16),
+            pltpu.VMEM((SIDE, CHUNK, NZ), bf16),
             pltpu.VMEM((TERMS * K, M), bf16),
             pltpu.VMEM((2 * K, len(PAIRS) * K), bf16),
             pltpu.VMEM((NZ, NZ), f32),
@@ -496,9 +582,9 @@
             each,
             each,
             pltpu.VMEM((NX, NY, K, NZ), bf16),
-            pltpu.VMEM((POINTS * NY, NZ), f32),
+            pltpu.VMEM((NY, POINTS, NZ), bf16),
             pltpu.VMEM((2, POINTS, NY, NZ), bf16),
-            pltpu.SemaphoreType.DMA((3,)),
+            pltpu.SemaphoreType.DMA((5,)),
         ],
         compiler_params=pltpu.CompilerParams(vmem_limit_bytes=56 << 20),
         name="finish",
@@ -516,10 +602,7 @@
 
 
 def per_device(basis, rhs, coeffs, rows, signs, params, order):
-    at = [lax.axis_index(name).astype(jnp.int32) for name in ("zl", "zh", "core")]
-    zl, zh, core = at
-    ids = jnp.stack([core, zl * 4 + zh, (1 - zl) * (NX - 1), (1 - core) * (NY - 1)])
-    x_first, x_second, y_first, y_second = planes(ids, rows, signs, coeffs)
+    x_first, x_second, y_first, y_second, ids = planes(rows, signs, coeffs)
     pair = [(0, 1)]
     infos = [
         swapped(x_first, "zl", pair),

time: 122 us -> 120 us (0.984)
  Pallas kernels: 51.7 us -> 49.6 us
    pallas_call x3, Pallas kernels: 25.4 us -> 24.1 us  [the longest x1 20.1 us: sketch(): pl.pallas_call(sketch_body, in_specs=[hbm, vm, hbm, hbm, hbm], out_specs=...]
where the time goes in v4:
time: 120 us; the launch traced here: 119 us
  blocking collectives  50.1 us (42%)
  Pallas kernels  49.6 us (41%)
  starting transfers between devices  12.9 us (11%)
  waiting for transfers between devices  3.75 us (3%)
  local copies, waits for them, and re-layouts  2.26 us (2%)
    all_to_all x1, blocking collectives, per_device(): parts = lax.all_to_all(parts, FACE, 0, 0, tiled=True)  22.8 us
    pallas_call x1, Pallas kernels, sketch(): pl.pallas_call(sketch_body, in_specs=[hbm, vm, hbm, hbm, hbm], out_specs=...  20.1 us
    all_to_all x1, blocking collectives, per_device(): parts = lax.all_to_all(first(ids, params, parts), DEPTH, 0, 0, tiled=True)  14.4 us
    ppermute x6, starting transfers between devices, swapped(): return lax.ppermute(value, axes, pairs + [(j, i) for i, j in pairs])  12.9 us
    all_to_all x1, blocking collectives, per_device(): mine = lax.all_to_all(second(parts), FACE, 0, 0, tiled=True)  12.9 us
    pallas_call x1, Pallas kernels, finish(): pl.pallas_call(finish_body, in_specs=[pl.BlockSpec(memory_space=pltpu.SME...  12.9 us
    pallas_call x1, Pallas kernels, edges(): pl.pallas_call(edge_body, grid_spec=pltpu.PrefetchScalarGridSpec(num_scal...  8.94 us
    ppermute x6, waiting for transfers between devices, swapped(): return lax.ppermute(value, axes, pairs + [(j, i) for i, j in pairs])  3.75 us
  transfers between devices with their start and end apart: 6, of which 2 were waited for; matrix products, arithmetic and copies ran while one was open for 0% of the time, Pallas kernels for 17%

profile of v4, /device:TPU:1, one launch (start us, length us, event | category | flops | bytes accessed | tf_op | source)
XLA Modules:
  0.0 118.9 jit_solution(13317892405866637307)
XLA Ops:
  0.0 1.8 %planes.1 = (f32[9,16,128]{2,1,0:T(8,128)}, f32[9,16,128]{2,1,0:T(8,128)}, f32[9,4,128]{2,1,0:T(4,128)}, f32[9,4,128]{2,1,0:T(4,128)}, s32[4]{0:T(128)}) custom-call(s32[4,4,16,128]{3,2,1,0:T(8,128)} %rows_hbm.1, s32[4,4,16,128]{3,2,1,0:T(8,128)} %signs_hbm.1, f32[4,4,16,128]{3,2,1,0:T(8,128)} %co_hbm.1), custom_call_target="tpu_custom_call" | custom-call | tf_op jit(solution)/shard_map/planes/pallas_call | solution.py:230
  1.8 2.5 %collective-permute-start = (f32[9,16,128]{2,1,0:T(8,128)}, f32[9,16,128]{2,1,0:T(8,128)S(1)}, u32[]{:S(2)}, u32[]{:S(2)}) collective-permute-start(f32[9,16,128]{2,1,0:T(8,128)} %get-tuple-element.17), channel_id=1, source_target_pairs={{0,32},{32,0},{1,33},{33,1},{2,34},{34,2},{3,35},{35,3},{4,36},{36... | collective-permute-start | bytes 221192 | tf_op jit(solution)/shard_map/ppermute | solution.py:601
  4.3 0.7 collective-permute-start.1
  5.0 1.0 collective-permute-start.2
  6.0 4.8 %collective-permute-start.3 = (f32[9,4,128]{2,1,0:T(4,128)}, f32[9,4,128]{2,1,0:T(4,128)S(1)}, u32[]{:S(2)}, u32[]{:S(2)}) collective-permute-start(f32[9,4,128]{2,1,0:T(4,128)} %get-tuple-element.20), channel_id=1, source_target_pairs={{1,2},{3,4},{5,6},{7,8},{9,10},{11,12},{13,14},{15,16},{17,18},{19... | collective-permute-start | bytes 55304 | tf_op jit(solution)/shard_map/ppermute | solution.py:601
  10.8 20.1 %sketch.1 = (f32[4,528,256]{2,1,0:T(8,128)}, bf16[4,16,128,128]{3,2,1,0:T(8,128)(2,1)}) custom-call(bf16[128,4,16,128]{3,2,1,0:T(8,128)(2,1)} %basis_hbm.1, bf16[4,16,128]{2,1,0:T(8,128)(2,1)} %rhs_ref.1, f32[4,4,16,128]{3,2,1,0:T(8,128)} %co_hbm.1, s32[4,4,16,128]{3,2,1,0:T(8,128)} %rows_hbm.1, s32[4,4,16,128]{3,2,1,0:T(8,128)} %signs_hbm.1), custom_call_target="tpu_custom_call" | custom-call | tf_op jit(solution)/shard_map/sketch/pallas_call | solution.py:177
  30.9 0.0 collective-permute-done.2.yl_ref
  31.0 0.0 copy-start.5
  31.0 0.0 collective-permute-done.3.yu_ref
  31.0 0.0 copy-start.6
  31.0 0.0 collective-permute-done.xl_ref
  31.0 0.0 copy-start.3
  31.0 0.0 collective-permute-done.1.xu_ref
  31.0 0.0 copy-start.4
  31.0 0.5 copy-done.5
  31.5 0.0 copy-done.6
  31.6 0.0 copy-done.3
  31.6 0.0 copy-done.4
  31.7 8.9 %edges.1 = (f32[16,136,128]{2,1,0:T(8,128)}, bf16[16,136,128]{2,1,0:T(8,128)(2,1)}) custom-call(s32[4]{0:T(128)} %get-tuple-element.14.ids_ref, f32[4,528,256]{2,1,0:T(8,128)} %get-tuple-element.15.acc_hbm, bf16[4,16,128,128]{3,2,1,0:T(8,128)(2,1)} %get-tuple-element.16.bxl_ref.bxu_ref.byl_ref.byu_ref.bt_hbm, ...), custom_call_target="tpu_custom_call" | custom-call | tf_op jit(solution)/shard_map/edges/pallas_call | solution.py:300
  40.6 0.1 collective-permute-start.4
  40.7 2.2 %collective-permute-done.4.got_hbm = bf16[16,136,128]{2,1,0:T(8,128)(2,1)S(1)} collective-permute-done((bf16[16,136,128]{2,1,0:T(8,128)(2,1)}, bf16[16,136,128]{2,1,0:T(8,128)(2,1)S(1)}, u32[]{:S(2)}, u32[]{:S(2)}) %collective-permute-start.4) | collective-permute-done | bytes 557088 | tf_op jit(solution)/shard_map/ppermute | solution.py:601
  42.9 0.0 copy-start.1
  42.9 0.8 copy-done.1
  43.7 2.2 %merge.1 = bf16[16,136,128]{2,1,0:T(8,128)(2,1)} custom-call(f32[16,136,128]{2,1,0:T(8,128)} %get-tuple-element.21.own_hbm, bf16[16,136,128]{2,1,0:T(8,128)(2,1)} %copy-done.1), custom_call_target="tpu_custom_call" | custom-call | tf_op jit(solution)/shard_map/merge/pallas_call | solution.py:367
  45.9 22.8 %all_to_all.15.parts_ref = bf16[16,136,128]{2,1,0:T(8,128)(2,1)} all-to-all(bf16[16,136,128]{2,1,0:T(8,128)(2,1)} %merge.1), channel_id=1, replica_groups=mesh['x'=4,'zl'=2,'y'=4,'zh'=4,'core'=2] {'x','y'}, dimensions={0} | all-to-all | bytes 1114112 | tf_op jit(solution)/shard_map/all_to_all | solution.py:616
  68.7 1.9 %first.1 = bf16[8,136,128]{2,1,0:T(8,128)(2,1)} custom-call(s32[4]{0:T(128)} %get-tuple-element.14.ids_ref, f32[1,4]{1,0:T(1,128)} %params_ref.1, bf16[16,136,128]{2,1,0:T(8,128)(2,1)} %all_to_all.15.parts_ref), custom_call_target="tpu_custom_call" | custom-call | tf_op jit(solution)/shard_map/first/pallas_call | solution.py:410
  70.6 14.4 %all_to_all.16.parts_ref = bf16[8,136,128]{2,1,0:T(8,128)(2,1)} all-to-all(bf16[8,136,128]{2,1,0:T(8,128)(2,1)} %first.1), channel_id=1, replica_groups=mesh['x'=4,'zl'=2,'y'=4,'zh'=4,'core'=2] {'zl','zh'}, dimensions={0} | all-to-all | bytes 557056 | tf_op jit(solution)/shard_map/all_to_all | solution.py:617
  85.0 1.8 %second.1 = bf16[16,136,128]{2,1,0:T(8,128)(2,1)} custom-call(bf16[8,136,128]{2,1,0:T(8,128)(2,1)} %all_to_all.16.parts_ref), custom_call_target="tpu_custom_call" | custom-call | tf_op jit(solution)/shard_map/second/pallas_call | solution.py:425
  86.8 12.9 %all_to_all.17.own_hbm = bf16[16,136,128]{2,1,0:T(8,128)(2,1)S(1)} all-to-all(bf16[16,136,128]{2,1,0:T(8,128)(2,1)} %second.1), channel_id=1, replica_groups=mesh['x'=4,'zl'=2,'y'=4,'zh'=4,'core'=2] {'x','y'}, dimensions={0} | all-to-all | bytes 1114112 | tf_op jit(solution)/shard_map/all_to_all | solution.py:618
  99.7 0.0 copy-start
  99.7 3.8 %collective-permute-start.5 = (bf16[16,136,128]{2,1,0:T(8,128)(2,1)S(1)}, bf16[16,136,128]{2,1,0:T(8,128)(2,1)S(1)}, u32[]{:S(2)}, u32[]{:S(2)}) collective-permute-start(bf16[16,136,128]{2,1,0:T(8,128)(2,1)S(1)} %all_to_all.17.own_hbm), channel_id=1, source_target_pairs={{0,1},{1,0},{2,3},{3,2},{4,5},{5,4},{6,7},{7,6},{8,9},{9,8},{10,11... | collective-permute-start | bytes 1671176 | tf_op jit(solution)/shard_map/ppermute | solution.py:601
  103.5 1.6 %collective-permute-done.5.other_hbm = bf16[16,136,128]{2,1,0:T(8,128)(2,1)S(1)} collective-permute-done((bf16[16,136,128]{2,1,0:T(8,128)(2,1)S(1)}, bf16[16,136,128]{2,1,0:T(8,128)(2,1)S(1)}, u32[]{:S(2)}, u32[]{:S(2)}) %collective-permute-start.5) | collective-permute-done | bytes 557088 | tf_op jit(solution)/shard_map/ppermute | solution.py:601
  105.1 0.0 copy-start.2
  105.1 0.0 copy-done
  105.1 0.8 copy-done.2
  105.9 12.9 %finish.1 = bf16[256,4,16,128]{3,2,1,0:T(8,128)(2,1)} custom-call(s32[4]{0:T(128)} %get-tuple-element.14.ids_ref, bf16[16,136,128]{2,1,0:T(8,128)(2,1)} %copy-done, bf16[16,136,128]{2,1,0:T(8,128)(2,1)} %copy-done.2, s32[1,256]{1,0:T(1,128)} %bitcast.1, bf16[4,16,128,128]{3,2,1,0:T(8,128)(2,1)} %get-tuple-element.16.bxl_ref.bxu_ref.byl_ref.byu_ref.bt_hbm), custom_call_target="tpu_custom_call" | custom-call | tf_op jit(solution)/shard_map/finish/pallas_call | solution.py:567
Async XLA Ops:
  1.8 29.2 %collective-permute-start = (f32[9,16,128]{2,1,0:T(8,128)}, f32[9,16,128]{2,1,0:T(8,128)S(1)}, u32[]{:S(2)}, u32[]{:S(2)}) collective-permute-start(f32[9,16,128]{2,1,0:T(8,128)} %get-tuple-element.17), channel_id=1, source_target_pairs={{0,32},{32,0},{1,33},{33,1},{2,34},{34,2},{3,35},{35,3},{4,36},{36... | collective-permute-start | bytes 221192 | tf_op jit(solution)/shard_map/ppermute | solution.py:601
  4.3 26.7 %collective-permute-start.1 = (f32[9,16,128]{2,1,0:T(8,128)}, f32[9,16,128]{2,1,0:T(8,128)S(1)}, u32[]{:S(2)}, u32[]{:S(2)}) collective-permute-start(f32[9,16,128]{2,1,0:T(8,128)} %get-tuple-element.18), channel_id=1, source_target_pairs={{32,64},{96,128},{160,192},{64,32},{128,96},{192,160},{33,65},{97,... | collective-permute-start | bytes 221192 | tf_op jit(solution)/shard_map/ppermute | solution.py:601
  5.0 26.0 %collective-permute-start.2 = (f32[9,4,128]{2,1,0:T(4,128)}, f32[9,4,128]{2,1,0:T(4,128)S(1)}, u32[]{:S(2)}, u32[]{:S(2)}) collective-permute-start(f32[9,4,128]{2,1,0:T(4,128)} %get-tuple-element.19), channel_id=1, source_target_pairs={{0,1},{1,0},{2,3},{3,2},{4,5},{5,4},{6,7},{7,6},{8,9},{9,8},{10,11... | collective-permute-start | bytes 55304 | tf_op jit(solution)/shard_map/ppermute | solution.py:601
  6.0 25.0 %collective-permute-start.3 = (f32[9,4,128]{2,1,0:T(4,128)}, f32[9,4,128]{2,1,0:T(4,128)S(1)}, u32[]{:S(2)}, u32[]{:S(2)}) collective-permute-start(f32[9,4,128]{2,1,0:T(4,128)} %get-tuple-element.20), channel_id=1, source_target_pairs={{1,2},{3,4},{5,6},{7,8},{9,10},{11,12},{13,14},{15,16},{17,18},{19... | collective-permute-start | bytes 55304 | tf_op jit(solution)/shard_map/ppermute | solution.py:601
  31.0 0.6 copy-start.5
  31.0 0.6 copy-start.6
  31.0 0.6 copy-start.3
  31.0 0.7 copy-start.4
  40.6 2.3 %collective-permute-start.4 = (bf16[16,136,128]{2,1,0:T(8,128)(2,1)}, bf16[16,136,128]{2,1,0:T(8,128)(2,1)S(1)}, u32[]{:S(2)}, u32[]{:S(2)}) collective-permute-start(bf16[16,136,128]{2,1,0:T(8,128)(2,1)} %get-tuple-element.22), channel_id=1, source_target_pairs={{0,1},{1,0},{2,3},{3,2},{4,5},{5,4},{6,7},{7,6},{8,9},{9,8},{10,11... | collective-permute-start | bytes 1671176 | tf_op jit(solution)/shard_map/ppermute | solution.py:601
  42.9 0.8 copy-start.1
  99.7 5.4 %copy-start = (bf16[16,136,128]{2,1,0:T(8,128)(2,1)}, bf16[16,136,128]{2,1,0:T(8,128)(2,1)S(1)}, u32[]{:S(2)}) copy-start(bf16[16,136,128]{2,1,0:T(8,128)(2,1)S(1)} %all_to_all.17.own_hbm) | copy-start | bytes 1671172
  99.7 5.4 %collective-permute-start.5 = (bf16[16,136,128]{2,1,0:T(8,128)(2,1)S(1)}, bf16[16,136,128]{2,1,0:T(8,128)(2,1)S(1)}, u32[]{:S(2)}, u32[]{:S(2)}) collective-permute-start(bf16[16,136,128]{2,1,0:T(8,128)(2,1)S(1)} %all_to_all.17.own_hbm), channel_id=1, source_target_pairs={{0,1},{1,0},{2,3},{3,2},{4,5},{5,4},{6,7},{7,6},{8,9},{9,8},{10,11... | collective-permute-start | bytes 1671176 | tf_op jit(solution)/shard_map/ppermute | solution.py:601
  105.1 0.8 copy-start.2

commit v5 on v4

--- a/solution.py
+++ b/solution.py
@@ -75,14 +75,21 @@
 def sketch_body(
     basis_hbm, rhs_ref, co_hbm, rows_hbm, signs_hbm, acc_hbm, bt_hbm,
     pad, terms, hashes, terms_b, hashes_b, source_ref, slots, basis_ref, co_ref, rows_ref, signs_ref, bt_ref, acc_ref,
-    sems, out_sems,
+    sems, out_sems, slab_sems,
 ):
     fetches = [
         pltpu.make_async_copy(src, dst, sems.at[i])
         for i, (src, dst) in enumerate(
-            ((basis_hbm, basis_ref), (co_hbm, co_ref), (rows_hbm, rows_ref), (signs_hbm, signs_ref))
+            ((co_hbm, co_ref), (rows_hbm, rows_ref), (signs_hbm, signs_ref))
         )
     ]
+
+    def slab(i):
+        at = pl.ds(pl.multiple_of(i * 16, 16), 16)
+        return pltpu.make_async_copy(basis_hbm.at[at], basis_ref.at[at], slab_sems.at[i])
+
+    for i in range(K // 16):
+        slab(i).start()
     for fetch in fetches:
         fetch.start()
     put_slots(slots)
@@ -94,9 +101,9 @@
         pad[x + 1, NY + 1] = jnp.zeros((K, NZ), f32)
     turn = turning()
     source_ref[...] = rhs_ref[...].astype(f32)
-    fetches[0].wait()
 
     def turned(i, _):
+        slab(i).wait()
         k = pl.multiple_of(i * 16, 16)
         for x in range(0, NX, 2):
             both = jnp.concatenate(
@@ -113,7 +120,7 @@
     lax.fori_loop(0, K // 16, turned, 0)
     give = pltpu.make_async_copy(bt_ref, bt_hbm, sems.at[4])
     give.start()
-    for fetch in fetches[1:]:
+    for fetch in fetches:
         fetch.wait()
     lane = lax.broadcasted_iota(jnp.int32, (1, NZ), 1)
     top = lax.broadcasted_iota(jnp.int32, (16, NZ), 0) == 0
@@ -198,6 +205,7 @@
             pltpu.VMEM((M // PART, TALL, PART), f32),
             pltpu.SemaphoreType.DMA((5,)),
             pltpu.SemaphoreType.DMA((M // PART,)),
+            pltpu.SemaphoreType.DMA((K // 16,)),
         ],
         compiler_params=pltpu.CompilerParams(vmem_limit_bytes=56 << 20),
         name="sketch",
@@ -331,22 +339,17 @@
     )(ids, acc, bt, bt, bt, bt, *infos)
 
 
-def merge_body(own_hbm, got_hbm, out_hbm, own_ref, got_ref, out_ref, sems):
+def merge_body(own_hbm, got_ref, out_hbm, own_ref, out_ref, sems):
     size = SIDE // 4
     fetches = [
-        [
-            pltpu.make_async_copy(src.at[pl.ds(g * size, size)], dst.at[pl.ds(g * size, size)], sems.at[n, g])
-            for n, (src, dst) in enumerate(((own_hbm, own_ref), (got_hbm, got_ref)))
-        ]
+        pltpu.make_async_copy(own_hbm.at[pl.ds(g * size, size)], own_ref.at[pl.ds(g * size, size)], sems.at[0, g])
         for g in range(4)
     ]
-    for pair in fetches:
-        for fetch in pair:
-            fetch.start()
+    for fetch in fetches:
+        fetch.start()
     gives = []
     for g in range(4):
-        for fetch in fetches[g]:
-            fetch.wait()
+        fetches[g].wait()
 
         def add(i, _):
             out_ref[i, 0:BODY, :] = (own_ref[i, 0:BODY, :] + got_ref[i, 0:BODY, :].astype(f32)).astype(bf16)
@@ -355,7 +358,7 @@
 
         lax.fori_loop(g * size, (g + 1) * size, add, 0)
         part = pl.ds(g * size, size)
-        give = pltpu.make_async_copy(out_ref.at[part], out_hbm.at[part], sems.at[2, g])
+        give = pltpu.make_async_copy(out_ref.at[part], out_hbm.at[part], sems.at[1, g])
         give.start()
         gives.append(give)
     for give in gives:
@@ -366,14 +369,13 @@
     hbm = pl.BlockSpec(memory_space=pl.ANY)
     return pl.pallas_call(
         merge_body,
-        in_specs=[hbm, hbm],
+        in_specs=[hbm, pl.BlockSpec(memory_space=pltpu.VMEM)],
         out_specs=hbm,
         out_shape=jax.ShapeDtypeStruct((SIDE, CHUNK, NZ), bf16),
         scratch_shapes=[
             pltpu.VMEM((SIDE, CHUNK, NZ), f32),
             pltpu.VMEM((SIDE, CHUNK, NZ), bf16),
-            pltpu.VMEM((SIDE, CHUNK, NZ), bf16),
-            pltpu.SemaphoreType.DMA((3, 4)),
+            pltpu.SemaphoreType.DMA((2, 4)),
         ],
         name="merge",
     )(own, got)
@@ -430,19 +432,12 @@
 
 
 def finish_body(
-    ids_ref, own_hbm, other_hbm, order_ref, bt_hbm, out_hbm, own_ref, other_ref,
+    ids_ref, own_ref, other_ref, order_ref, bt_hbm, out_hbm,
     st, table, extra, weight, pairs, scale, xs, rs, ps, bt_ref, lines, ready, sems,
 ):
-    halves = [
-        pltpu.make_async_copy(own_hbm, own_ref, sems.at[3]),
-        pltpu.make_async_copy(other_hbm, other_ref, sems.at[4]),
-    ]
-    for half in halves:
-        half.start()
     fetch = pltpu.make_async_copy(bt_hbm, bt_ref, sems.at[0])
     fetch.start()
-    for half in halves:
-        half.wait()
+
     c = ids_ref[0]
     half = TERMS * K // 2
 
@@ -566,12 +561,10 @@
     each = pltpu.VMEM((POINTS, K), f32)
     return pl.pallas_call(
         finish_body,
-        in_specs=[pl.BlockSpec(memory_space=pltpu.SMEM), hbm, hbm, vm, hbm],
+        in_specs=[pl.BlockSpec(memory_space=pltpu.SMEM), vm, vm, vm, hbm],
         out_specs=hbm,
         out_shape=jax.ShapeDtypeStruct((POINTS, NX, NY, NZ), bf16),
         scratch_shapes=[
-            pltpu.VMEM((SIDE, CHUNK, NZ), bf16),
-            pltpu.VMEM((SIDE, CHUNK, NZ), bf16),
             pltpu.VMEM((TERMS * K, M), bf16),
             pltpu.VMEM((2 * K, len(PAIRS) * K), bf16),
             pltpu.VMEM((NZ, NZ), f32),
@@ -584,7 +577,7 @@
             pltpu.VMEM((NX, NY, K, NZ), bf16),
             pltpu.VMEM((NY, POINTS, NZ), bf16),
             pltpu.VMEM((2, POINTS, NY, NZ), bf16),
-            pltpu.SemaphoreType.DMA((5,)),
+            pltpu.SemaphoreType.DMA((3,)),
         ],
         compiler_params=pltpu.CompilerParams(vmem_limit_bytes=56 << 20),
         name="finish",
@@ -597,8 +590,12 @@
 DEPTH = ("zl", "zh")
 
 
+def near(value):
+    return pltpu.with_memory_space_constraint(value, pltpu.MemorySpace.VMEM)
+
+
 def swapped(value, axes, pairs):
-    return lax.ppermute(value, axes, pairs + [(j, i) for i, j in pairs])
+    return near(lax.ppermute(value, axes, pairs + [(j, i) for i, j in pairs]))
 
 
 def per_device(basis, rhs, coeffs, rows, signs, params, order):
@@ -617,7 +614,7 @@
     parts = lax.all_to_all(first(ids, params, parts), DEPTH, 0, 0, tiled=True)
     mine = lax.all_to_all(second(parts), FACE, 0, 0, tiled=True)
     theirs = swapped(mine, "core", pair)
-    return finish(ids, mine, theirs, order.reshape(1, POINTS), bt)
+    return finish(ids, near(mine), theirs, order.reshape(1, POINTS), bt)
 
 
 def solution(mesh):

time: 120 us -> 115 us (0.958)
  local copies, waits for them, and re-layouts: 2.26 us -> 0 us
  Pallas kernels: 49.6 us -> 47.6 us
    unnamed x14 -> x0, local copies, waits for them, and re-layouts: 2.26 us -> none
    pallas_call x1, Pallas kernels: 12.9 us -> 11.6 us  [finish(): pl.pallas_call(finish_body, in_specs=[pl.BlockSpec(memory_space=pltpu.SME...]
where the time goes in v5:
time: 115 us
  blocking collectives  50.1 us (44%)
  Pallas kernels  47.6 us (41%)
  starting transfers between devices  12.9 us (11%)
  waiting for transfers between devices  3.75 us (3%)
    all_to_all x1, blocking collectives, per_device(): parts = lax.all_to_all(parts, FACE, 0, 0, tiled=True)  22.8 us
    pallas_call x1, Pallas kernels, sketch(): pl.pallas_call(sketch_body, in_specs=[hbm, vm, hbm, hbm, hbm], out_specs=...  19.5 us
    all_to_all x1, blocking collectives, per_device(): parts = lax.all_to_all(first(ids, params, parts), DEPTH, 0, 0, tiled=True)  14.4 us
    ppermute x6, starting transfers between devices, swapped(): return near(lax.ppermute(value, axes, pairs + [(j, i) for i, j in pairs]))  12.9 us
    all_to_all x1, blocking collectives, per_device(): mine = lax.all_to_all(second(parts), FACE, 0, 0, tiled=True)  12.9 us
    pallas_call x1, Pallas kernels, finish(): pl.pallas_call(finish_body, in_specs=[pl.BlockSpec(memory_space=pltpu.SME...  11.6 us
    pallas_call x1, Pallas kernels, edges(): pl.pallas_call(edge_body, grid_spec=pltpu.PrefetchScalarGridSpec(num_scal...  8.94 us
    ppermute x6, waiting for transfers between devices, swapped(): return near(lax.ppermute(value, axes, pairs + [(j, i) for i, j in pairs]))  3.75 us
  transfers between devices with their start and end apart: 6, of which 2 were waited for; matrix products, arithmetic and copies ran while one was open for 0% of the time, Pallas kernels for 17%

profile of v5, /device:TPU:1, one launch (start us, length us, event | category | flops | bytes accessed | tf_op | source)
XLA Modules:
  0.0 114.7 jit_solution(16544947696817950262)
XLA Ops:
  0.0 1.7 %planes.1 = (f32[9,16,128]{2,1,0:T(8,128)}, f32[9,16,128]{2,1,0:T(8,128)}, f32[9,4,128]{2,1,0:T(4,128)}, f32[9,4,128]{2,1,0:T(4,128)}, s32[4]{0:T(128)}) custom-call(s32[4,4,16,128]{3,2,1,0:T(8,128)} %rows_hbm.1, s32[4,4,16,128]{3,2,1,0:T(8,128)} %signs_hbm.1, f32[4,4,16,128]{3,2,1,0:T(8,128)} %co_hbm.1), custom_call_target="tpu_custom_call" | custom-call | tf_op jit(solution)/shard_map/planes/pallas_call | solution.py:238
  1.8 2.5 %collective-permute-start = (f32[9,16,128]{2,1,0:T(8,128)}, f32[9,16,128]{2,1,0:T(8,128)S(1)}, u32[]{:S(2)}, u32[]{:S(2)}) collective-permute-start(f32[9,16,128]{2,1,0:T(8,128)} %get-tuple-element.17), channel_id=1, source_target_pairs={{0,32},{32,0},{1,33},{33,1},{2,34},{34,2},{3,35},{35,3},{4,36},{36... | collective-permute-start | bytes 221192 | tf_op jit(solution)/shard_map/ppermute | solution.py:598
  4.3 0.7 collective-permute-start.1
  5.0 1.0 collective-permute-start.2
  6.0 4.8 %collective-permute-start.3 = (f32[9,4,128]{2,1,0:T(4,128)}, f32[9,4,128]{2,1,0:T(4,128)S(1)}, u32[]{:S(2)}, u32[]{:S(2)}) collective-permute-start(f32[9,4,128]{2,1,0:T(4,128)} %get-tuple-element.20), channel_id=1, source_target_pairs={{1,2},{3,4},{5,6},{7,8},{9,10},{11,12},{13,14},{15,16},{17,18},{19... | collective-permute-start | bytes 55304 | tf_op jit(solution)/shard_map/ppermute | solution.py:598
  10.8 19.5 %sketch.1 = (f32[4,528,256]{2,1,0:T(8,128)}, bf16[4,16,128,128]{3,2,1,0:T(8,128)(2,1)}) custom-call(bf16[128,4,16,128]{3,2,1,0:T(8,128)(2,1)} %basis_hbm.1, bf16[4,16,128]{2,1,0:T(8,128)(2,1)} %rhs_ref.1, f32[4,4,16,128]{3,2,1,0:T(8,128)} %co_hbm.1, s32[4,4,16,128]{3,2,1,0:T(8,128)} %rows_hbm.1, s32[4,4,16,128]{3,2,1,0:T(8,128)} %signs_hbm.1), custom_call_target="tpu_custom_call" | custom-call | tf_op jit(solution)/shard_map/sketch/pallas_call | solution.py:184
  30.3 0.0 collective-permute-done.2.yl_ref
  30.4 0.0 collective-permute-done.3.yu_ref
  30.4 0.0 collective-permute-done.xl_ref
  30.4 0.0 collective-permute-done.1.xu_ref
  30.4 8.9 %edges.1 = (f32[16,136,128]{2,1,0:T(8,128)}, bf16[16,136,128]{2,1,0:T(8,128)(2,1)}) custom-call(s32[4]{0:T(128)} %get-tuple-element.14.ids_ref, f32[4,528,256]{2,1,0:T(8,128)} %get-tuple-element.15.acc_hbm, bf16[4,16,128,128]{3,2,1,0:T(8,128)(2,1)} %get-tuple-element.16.bxl_ref.bxu_ref.byl_ref.byu_ref.bt_hbm, ...), custom_call_target="tpu_custom_call" | custom-call | tf_op jit(solution)/shard_map/edges/pallas_call | solution.py:308
  39.3 0.1 collective-permute-start.4
  39.4 2.2 %collective-permute-done.4.got_ref = bf16[16,136,128]{2,1,0:T(8,128)(2,1)S(1)} collective-permute-done((bf16[16,136,128]{2,1,0:T(8,128)(2,1)}, bf16[16,136,128]{2,1,0:T(8,128)(2,1)S(1)}, u32[]{:S(2)}, u32[]{:S(2)}) %collective-permute-start.4) | collective-permute-done | bytes 557088 | tf_op jit(solution)/shard_map/ppermute | solution.py:598
  41.6 2.1 %merge.1 = bf16[16,136,128]{2,1,0:T(8,128)(2,1)} custom-call(f32[16,136,128]{2,1,0:T(8,128)} %get-tuple-element.21.own_hbm, bf16[16,136,128]{2,1,0:T(8,128)(2,1)S(1)} %collective-permute-done.4.got_ref), custom_call_target="tpu_custom_call" | custom-call | tf_op jit(solution)/shard_map/merge/pallas_call | solution.py:370
  43.7 22.8 %all_to_all.15.parts_ref = bf16[16,136,128]{2,1,0:T(8,128)(2,1)} all-to-all(bf16[16,136,128]{2,1,0:T(8,128)(2,1)} %merge.1), channel_id=1, replica_groups=mesh['x'=4,'zl'=2,'y'=4,'zh'=4,'core'=2] {'x','y'}, dimensions={0} | all-to-all | bytes 1114112 | tf_op jit(solution)/shard_map/all_to_all | solution.py:613
  66.5 1.9 %first.1 = bf16[8,136,128]{2,1,0:T(8,128)(2,1)} custom-call(s32[4]{0:T(128)} %get-tuple-element.14.ids_ref, f32[1,4]{1,0:T(1,128)} %params_ref.1, bf16[16,136,128]{2,1,0:T(8,128)(2,1)} %all_to_all.15.parts_ref), custom_call_target="tpu_custom_call" | custom-call | tf_op jit(solution)/shard_map/first/pallas_call | solution.py:412
  68.4 14.4 %all_to_all.16.parts_ref = bf16[8,136,128]{2,1,0:T(8,128)(2,1)} all-to-all(bf16[8,136,128]{2,1,0:T(8,128)(2,1)} %first.1), channel_id=1, replica_groups=mesh['x'=4,'zl'=2,'y'=4,'zh'=4,'core'=2] {'zl','zh'}, dimensions={0} | all-to-all | bytes 557056 | tf_op jit(solution)/shard_map/all_to_all | solution.py:614
  82.8 1.8 %second.1 = bf16[16,136,128]{2,1,0:T(8,128)(2,1)} custom-call(bf16[8,136,128]{2,1,0:T(8,128)(2,1)} %all_to_all.16.parts_ref), custom_call_target="tpu_custom_call" | custom-call | tf_op jit(solution)/shard_map/second/pallas_call | solution.py:427
  84.6 12.9 %all_to_all.17.own_ref = bf16[16,136,128]{2,1,0:T(8,128)(2,1)S(1)} all-to-all(bf16[16,136,128]{2,1,0:T(8,128)(2,1)} %second.1), channel_id=1, replica_groups=mesh['x'=4,'zl'=2,'y'=4,'zh'=4,'core'=2] {'x','y'}, dimensions={0} | all-to-all | bytes 1114112 | tf_op jit(solution)/shard_map/all_to_all | solution.py:615
  97.5 3.8 %collective-permute-start.5 = (bf16[16,136,128]{2,1,0:T(8,128)(2,1)S(1)}, bf16[16,136,128]{2,1,0:T(8,128)(2,1)S(1)}, u32[]{:S(2)}, u32[]{:S(2)}) collective-permute-start(bf16[16,136,128]{2,1,0:T(8,128)(2,1)S(1)} %all_to_all.17.own_ref), channel_id=1, source_target_pairs={{0,1},{1,0},{2,3},{3,2},{4,5},{5,4},{6,7},{7,6},{8,9},{9,8},{10,11... | collective-permute-start | bytes 1671176 | tf_op jit(solution)/shard_map/ppermute | solution.py:598
  101.3 1.6 %collective-permute-done.5.other_ref = bf16[16,136,128]{2,1,0:T(8,128)(2,1)S(1)} collective-permute-done((bf16[16,136,128]{2,1,0:T(8,128)(2,1)S(1)}, bf16[16,136,128]{2,1,0:T(8,128)(2,1)S(1)}, u32[]{:S(2)}, u32[]{:S(2)}) %collective-permute-start.5) | collective-permute-done | bytes 557088 | tf_op jit(solution)/shard_map/ppermute | solution.py:598
  102.9 11.6 %finish.1 = bf16[256,4,16,128]{3,2,1,0:T(8,128)(2,1)} custom-call(s32[4]{0:T(128)} %get-tuple-element.14.ids_ref, bf16[16,136,128]{2,1,0:T(8,128)(2,1)S(1)} %all_to_all.17.own_ref, bf16[16,136,128]{2,1,0:T(8,128)(2,1)S(1)} %collective-permute-done.5.other_ref, s32[1,256]{1,0:T(1,128)} %bitcast.1, ...), custom_call_target="tpu_custom_call" | custom-call | tf_op jit(solution)/shard_map/finish/pallas_call | solution.py:562
Async XLA Ops:
  1.8 28.6 %collective-permute-start = (f32[9,16,128]{2,1,0:T(8,128)}, f32[9,16,128]{2,1,0:T(8,128)S(1)}, u32[]{:S(2)}, u32[]{:S(2)}) collective-permute-start(f32[9,16,128]{2,1,0:T(8,128)} %get-tuple-element.17), channel_id=1, source_target_pairs={{0,32},{32,0},{1,33},{33,1},{2,34},{34,2},{3,35},{35,3},{4,36},{36... | collective-permute-start | bytes 221192 | tf_op jit(solution)/shard_map/ppermute | solution.py:598
  4.3 26.1 %collective-permute-start.1 = (f32[9,16,128]{2,1,0:T(8,128)}, f32[9,16,128]{2,1,0:T(8,128)S(1)}, u32[]{:S(2)}, u32[]{:S(2)}) collective-permute-start(f32[9,16,128]{2,1,0:T(8,128)} %get-tuple-element.18), channel_id=1, source_target_pairs={{32,64},{96,128},{160,192},{64,32},{128,96},{192,160},{33,65},{97,... | collective-permute-start | bytes 221192 | tf_op jit(solution)/shard_map/ppermute | solution.py:598
  5.0 25.4 %collective-permute-start.2 = (f32[9,4,128]{2,1,0:T(4,128)}, f32[9,4,128]{2,1,0:T(4,128)S(1)}, u32[]{:S(2)}, u32[]{:S(2)}) collective-permute-start(f32[9,4,128]{2,1,0:T(4,128)} %get-tuple-element.19), channel_id=1, source_target_pairs={{0,1},{1,0},{2,3},{3,2},{4,5},{5,4},{6,7},{7,6},{8,9},{9,8},{10,11... | collective-permute-start | bytes 55304 | tf_op jit(solution)/shard_map/ppermute | solution.py:598
  6.0 24.4 %collective-permute-start.3 = (f32[9,4,128]{2,1,0:T(4,128)}, f32[9,4,128]{2,1,0:T(4,128)S(1)}, u32[]{:S(2)}, u32[]{:S(2)}) collective-permute-start(f32[9,4,128]{2,1,0:T(4,128)} %get-tuple-element.20), channel_id=1, source_target_pairs={{1,2},{3,4},{5,6},{7,8},{9,10},{11,12},{13,14},{15,16},{17,18},{19... | collective-permute-start | bytes 55304 | tf_op jit(solution)/shard_map/ppermute | solution.py:598
  39.3 2.3 %collective-permute-start.4 = (bf16[16,136,128]{2,1,0:T(8,128)(2,1)}, bf16[16,136,128]{2,1,0:T(8,128)(2,1)S(1)}, u32[]{:S(2)}, u32[]{:S(2)}) collective-permute-start(bf16[16,136,128]{2,1,0:T(8,128)(2,1)} %get-tuple-element.22), channel_id=1, source_target_pairs={{0,1},{1,0},{2,3},{3,2},{4,5},{5,4},{6,7},{7,6},{8,9},{9,8},{10,11... | collective-permute-start | bytes 1671176 | tf_op jit(solution)/shard_map/ppermute | solution.py:598
  97.5 5.4 %collective-permute-start.5 = (bf16[16,136,128]{2,1,0:T(8,128)(2,1)S(1)}, bf16[16,136,128]{2,1,0:T(8,128)(2,1)S(1)}, u32[]{:S(2)}, u32[]{:S(2)}) collective-permute-start(bf16[16,136,128]{2,1,0:T(8,128)(2,1)S(1)} %all_to_all.17.own_ref), channel_id=1, source_target_pairs={{0,1},{1,0},{2,3},{3,2},{4,5},{5,4},{6,7},{7,6},{8,9},{9,8},{10,11... | collective-permute-start | bytes 1671176 | tf_op jit(solution)/shard_map/ppermute | solution.py:598

commit v6 on v5

--- a/solution.py
+++ b/solution.py
@@ -331,52 +331,30 @@
         ],
         ),
         out_shape=(
-            jax.ShapeDtypeStruct((SIDE, CHUNK, NZ), f32),
-            jax.ShapeDtypeStruct((SIDE, CHUNK, NZ), bf16),
+            pltpu.VMEM((SIDE, CHUNK, NZ), f32),
+            pltpu.VMEM((SIDE, CHUNK, NZ), bf16),
         ),
         compiler_params=pltpu.CompilerParams(vmem_limit_bytes=56 << 20),
         name="edges",
     )(ids, acc, bt, bt, bt, bt, *infos)
 
 
-def merge_body(own_hbm, got_ref, out_hbm, own_ref, out_ref, sems):
-    size = SIDE // 4
-    fetches = [
-        pltpu.make_async_copy(own_hbm.at[pl.ds(g * size, size)], own_ref.at[pl.ds(g * size, size)], sems.at[0, g])
-        for g in range(4)
-    ]
-    for fetch in fetches:
-        fetch.start()
-    gives = []
-    for g in range(4):
-        fetches[g].wait()
-
-        def add(i, _):
-            out_ref[i, 0:BODY, :] = (own_ref[i, 0:BODY, :] + got_ref[i, 0:BODY, :].astype(f32)).astype(bf16)
-            out_ref[i, BODY:CHUNK, :] = in_three(own_ref[i, BODY:CHUNK, :] + from_three(got_ref[i, BODY:CHUNK, :]))
-            return 0
-
-        lax.fori_loop(g * size, (g + 1) * size, add, 0)
-        part = pl.ds(g * size, size)
-        give = pltpu.make_async_copy(out_ref.at[part], out_hbm.at[part], sems.at[1, g])
-        give.start()
-        gives.append(give)
-    for give in gives:
-        give.wait()
+def merge_body(own_ref, got_ref, out_ref):
+    def add(i, _):
+        out_ref[i, 0:BODY, :] = (own_ref[i, 0:BODY, :] + got_ref[i, 0:BODY, :].astype(f32)).astype(bf16)
+        out_ref[i, BODY:CHUNK, :] = in_three(own_ref[i, BODY:CHUNK, :] + from_three(got_ref[i, BODY:CHUNK, :]))
+        return 0
+
+    lax.fori_loop(0, SIDE, add, 0)
 
 
 def merge(own, got):
-    hbm = pl.BlockSpec(memory_space=pl.ANY)
+    vm = pl.BlockSpec(memory_space=pltpu.VMEM)
     return pl.pallas_call(
         merge_body,
-        in_specs=[hbm, pl.BlockSpec(memory_space=pltpu.VMEM)],
-        out_specs=hbm,
-        out_shape=jax.ShapeDtypeStruct((SIDE, CHUNK, NZ), bf16),
-        scratch_shapes=[
-            pltpu.VMEM((SIDE, CHUNK, NZ), f32),
-            pltpu.VMEM((SIDE, CHUNK, NZ), bf16),
-            pltpu.SemaphoreType.DMA((2, 4)),
-        ],
+        in_specs=[vm, vm],
+        out_specs=vm,
+        out_shape=pltpu.VMEM((SIDE, CHUNK, NZ), bf16),
         name="merge",
     )(own, got)
 
@@ -412,7 +390,7 @@
     return pl.pallas_call(
         first_body,
         in_specs=[sm, sm, pl.BlockSpec(memory_space=pltpu.VMEM)],
-        out_shape=jax.ShapeDtypeStruct((DEEP, CHUNK, NZ), bf16),
+        out_shape=pltpu.VMEM((DEEP, CHUNK, NZ), bf16),
         name="first",
     )(ids, params, parts)
 
@@ -426,7 +404,8 @@
 def second(parts):
     return pl.pallas_call(
         second_body,
-        out_shape=jax.ShapeDtypeStruct((SIDE, CHUNK, NZ), bf16),
+        in_specs=[pl.BlockSpec(memory_space=pltpu.VMEM)],
+        out_shape=pltpu.VMEM((SIDE, CHUNK, NZ), bf16),
         name="second",
     )(parts)
 
@@ -609,9 +588,9 @@
     ]
     acc, bt = sketch(basis, rhs, coeffs, rows, signs)
     own, other = edges(ids, acc, bt, infos)
-    parts = merge(own, swapped(other, "core", pair))
-    parts = lax.all_to_all(parts, FACE, 0, 0, tiled=True)
-    parts = lax.all_to_all(first(ids, params, parts), DEPTH, 0, 0, tiled=True)
+    parts = merge(near(own), swapped(other, "core", pair))
+    parts = near(lax.all_to_all(parts, FACE, 0, 0, tiled=True))
+    parts = near(lax.all_to_all(first(ids, params, parts), DEPTH, 0, 0, tiled=True))
     mine = lax.all_to_all(second(parts), FACE, 0, 0, tiled=True)
     theirs = swapped(mine, "core", pair)
     return finish(ids, near(mine), theirs, order.reshape(1, POINTS), bt)

time: 115 us -> 108 us (0.939)
  Pallas kernels: 47.6 us -> 41.9 us
  blocking collectives: 50.1 us -> 48.7 us
    pallas_call x2, Pallas kernels: 3.89 us -> 0.45 us  [the longest x1 0.38 us: merge(): pl.pallas_call(merge_body, in_specs=[vm, vm], out_specs=vm, out_shape=plt...]
    pallas_call x1, Pallas kernels: 8.94 us -> 7.75 us  [edges(): pl.pallas_call(edge_body, grid_spec=pltpu.PrefetchScalarGridSpec(num_scal...]
  transfers between devices with their start and end apart: 6 -> 6, of which waited for: 2 -> 2; matrix products, arithmetic and copies ran while one was open for 0% -> 0% of each run, Pallas kernels for 17% -> 18%
where the time goes in v6:
time: 108 us; the launch traced here: 107 us
  blocking collectives  48.7 us (45%)
  Pallas kernels  41.9 us (39%)
  starting transfers between devices  13 us (12%)
  waiting for transfers between devices  3.54 us (3%)
    all_to_all x1, blocking collectives, per_device(): parts = near(lax.all_to_all(parts, FACE, 0, 0, tiled=True))  22.5 us
    pallas_call x1, Pallas kernels, sketch(): pl.pallas_call(sketch_body, in_specs=[hbm, vm, hbm, hbm, hbm], out_specs=...  19.5 us
    all_to_all x1, blocking collectives, per_device(): lax.all_to_all(first(ids, params, parts), DEPTH, 0, 0, tiled=True)  14 us
    ppermute x6, starting transfers between devices, swapped(): return near(lax.ppermute(value, axes, pairs + [(j, i) for i, j in pairs]))  13 us
    all_to_all x1, blocking collectives, per_device(): mine = lax.all_to_all(second(parts), FACE, 0, 0, tiled=True)  12.2 us
    pallas_call x1, Pallas kernels, finish(): pl.pallas_call(finish_body, in_specs=[pl.BlockSpec(memory_space=pltpu.SME...  11.6 us
    pallas_call x1, Pallas kernels, edges(): pl.pallas_call(edge_body, grid_spec=pltpu.PrefetchScalarGridSpec(num_scal...  7.75 us
    ppermute x6, waiting for transfers between devices, swapped(): return near(lax.ppermute(value, axes, pairs + [(j, i) for i, j in pairs]))  3.54 us
  transfers between devices with their start and end apart: 6, of which 2 were waited for; matrix products, arithmetic and copies ran while one was open for 0% of the time, Pallas kernels for 18%

profile of v6, /device:TPU:1, one launch (start us, length us, event | category | flops | bytes accessed | tf_op | source)
XLA Modules:
  0.0 107.4 jit_solution(12451223272578809306)
XLA Ops:
  0.0 1.7 %planes.1 = (f32[9,16,128]{2,1,0:T(8,128)}, f32[9,16,128]{2,1,0:T(8,128)}, f32[9,4,128]{2,1,0:T(4,128)}, f32[9,4,128]{2,1,0:T(4,128)}, s32[4]{0:T(128)}) custom-call(s32[4,4,16,128]{3,2,1,0:T(8,128)} %rows_hbm.1, s32[4,4,16,128]{3,2,1,0:T(8,128)} %signs_hbm.1, f32[4,4,16,128]{3,2,1,0:T(8,128)} %co_hbm.1), custom_call_target="tpu_custom_call" | custom-call | tf_op jit(solution)/shard_map/planes/pallas_call | solution.py:238
  1.8 2.5 %collective-permute-start = (f32[9,16,128]{2,1,0:T(8,128)}, f32[9,16,128]{2,1,0:T(8,128)S(1)}, u32[]{:S(2)}, u32[]{:S(2)}) collective-permute-start(f32[9,16,128]{2,1,0:T(8,128)} %get-tuple-element.17), channel_id=1, source_target_pairs={{0,32},{32,0},{1,33},{33,1},{2,34},{34,2},{3,35},{35,3},{4,36},{36... | collective-permute-start | bytes 221192 | tf_op jit(solution)/shard_map/ppermute | solution.py:577
  4.3 0.7 collective-permute-start.1
  5.0 1.0 collective-permute-start.2
  6.0 4.8 %collective-permute-start.3 = (f32[9,4,128]{2,1,0:T(4,128)}, f32[9,4,128]{2,1,0:T(4,128)S(1)}, u32[]{:S(2)}, u32[]{:S(2)}) collective-permute-start(f32[9,4,128]{2,1,0:T(4,128)} %get-tuple-element.20), channel_id=1, source_target_pairs={{1,2},{3,4},{5,6},{7,8},{9,10},{11,12},{13,14},{15,16},{17,18},{19... | collective-permute-start | bytes 55304 | tf_op jit(solution)/shard_map/ppermute | solution.py:577
  10.8 19.5 %sketch.1 = (f32[4,528,256]{2,1,0:T(8,128)}, bf16[4,16,128,128]{3,2,1,0:T(8,128)(2,1)}) custom-call(bf16[128,4,16,128]{3,2,1,0:T(8,128)(2,1)} %basis_hbm.1, bf16[4,16,128]{2,1,0:T(8,128)(2,1)} %rhs_ref.1, f32[4,4,16,128]{3,2,1,0:T(8,128)} %co_hbm.1, s32[4,4,16,128]{3,2,1,0:T(8,128)} %rows_hbm.1, s32[4,4,16,128]{3,2,1,0:T(8,128)} %signs_hbm.1), custom_call_target="tpu_custom_call" | custom-call | tf_op jit(solution)/shard_map/sketch/pallas_call | solution.py:184
  30.3 0.0 collective-permute-done.2.yl_ref
  30.4 0.0 collective-permute-done.3.yu_ref
  30.4 0.0 collective-permute-done.xl_ref
  30.4 0.0 collective-permute-done.1.xu_ref
  30.4 7.8 %edges.1 = (f32[16,136,128]{2,1,0:T(8,128)S(1)}, bf16[16,136,128]{2,1,0:T(8,128)(2,1)S(1)}) custom-call(s32[4]{0:T(128)} %get-tuple-element.14.ids_ref, f32[4,528,256]{2,1,0:T(8,128)} %get-tuple-element.15.acc_hbm, bf16[4,16,128,128]{3,2,1,0:T(8,128)(2,1)} %get-tuple-element.16.bxl_ref.bxu_ref.byl_ref.byu_ref.bt_hbm, ...), custom_call_target="tpu_custom_call" | custom-call | tf_op jit(solution)/shard_map/edges/pallas_call | solution.py:308
  38.1 0.1 collective-permute-start.4
  38.2 1.9 %collective-permute-done.4.got_ref = bf16[16,136,128]{2,1,0:T(8,128)(2,1)S(1)} collective-permute-done((bf16[16,136,128]{2,1,0:T(8,128)(2,1)S(1)}, bf16[16,136,128]{2,1,0:T(8,128)(2,1)S(1)}, u32[]{:S(2)}, u32[]{:S(2)}) %collective-permute-start.4) | collective-permute-done | bytes 557088 | tf_op jit(solution)/shard_map/ppermute | solution.py:577
  40.2 0.4 merge.1
  40.6 22.5 %all_to_all.15.parts_ref = bf16[16,136,128]{2,1,0:T(8,128)(2,1)S(1)} all-to-all(bf16[16,136,128]{2,1,0:T(8,128)(2,1)S(1)} %merge.1), channel_id=1, replica_groups=mesh['x'=4,'zl'=2,'y'=4,'zh'=4,'core'=2] {'x','y'}, dimensions={0} | all-to-all | bytes 1114112 | tf_op jit(solution)/shard_map/all_to_all | solution.py:592
  63.1 0.8 first.1
  63.9 14.0 %all_to_all.16.parts_ref = bf16[8,136,128]{2,1,0:T(8,128)(2,1)S(1)} all-to-all(bf16[8,136,128]{2,1,0:T(8,128)(2,1)S(1)} %first.1), channel_id=1, replica_groups=mesh['x'=4,'zl'=2,'y'=4,'zh'=4,'core'=2] {'zl','zh'}, dimensions={0} | all-to-all | bytes 557056 | tf_op jit(solution)/shard_map/all_to_all | solution.py:593
  77.8 0.1 second.1
  77.9 12.2 %all_to_all.17.own_ref = bf16[16,136,128]{2,1,0:T(8,128)(2,1)S(1)} all-to-all(bf16[16,136,128]{2,1,0:T(8,128)(2,1)S(1)} %second.1), channel_id=1, replica_groups=mesh['x'=4,'zl'=2,'y'=4,'zh'=4,'core'=2] {'x','y'}, dimensions={0} | all-to-all | bytes 1114112 | tf_op jit(solution)/shard_map/all_to_all | solution.py:594
  90.1 3.9 %collective-permute-start.5 = (bf16[16,136,128]{2,1,0:T(8,128)(2,1)S(1)}, bf16[16,136,128]{2,1,0:T(8,128)(2,1)S(1)}, u32[]{:S(2)}, u32[]{:S(2)}) collective-permute-start(bf16[16,136,128]{2,1,0:T(8,128)(2,1)S(1)} %all_to_all.17.own_ref), channel_id=1, source_target_pairs={{0,1},{1,0},{2,3},{3,2},{4,5},{5,4},{6,7},{7,6},{8,9},{9,8},{10,11... | collective-permute-start | bytes 1671176 | tf_op jit(solution)/shard_map/ppermute | solution.py:577
  94.0 1.6 %collective-permute-done.5.other_ref = bf16[16,136,128]{2,1,0:T(8,128)(2,1)S(1)} collective-permute-done((bf16[16,136,128]{2,1,0:T(8,128)(2,1)S(1)}, bf16[16,136,128]{2,1,0:T(8,128)(2,1)S(1)}, u32[]{:S(2)}, u32[]{:S(2)}) %collective-permute-start.5) | collective-permute-done | bytes 557088 | tf_op jit(solution)/shard_map/ppermute | solution.py:577
  95.6 11.6 %finish.1 = bf16[256,4,16,128]{3,2,1,0:T(8,128)(2,1)} custom-call(s32[4]{0:T(128)} %get-tuple-element.14.ids_ref, bf16[16,136,128]{2,1,0:T(8,128)(2,1)S(1)} %all_to_all.17.own_ref, bf16[16,136,128]{2,1,0:T(8,128)(2,1)S(1)} %collective-permute-done.5.other_ref, s32[1,256]{1,0:T(1,128)} %bitcast.1, ...), custom_call_target="tpu_custom_call" | custom-call | tf_op jit(solution)/shard_map/finish/pallas_call | solution.py:541
Async XLA Ops:
  1.8 28.6 %collective-permute-start = (f32[9,16,128]{2,1,0:T(8,128)}, f32[9,16,128]{2,1,0:T(8,128)S(1)}, u32[]{:S(2)}, u32[]{:S(2)}) collective-permute-start(f32[9,16,128]{2,1,0:T(8,128)} %get-tuple-element.17), channel_id=1, source_target_pairs={{0,32},{32,0},{1,33},{33,1},{2,34},{34,2},{3,35},{35,3},{4,36},{36... | collective-permute-start | bytes 221192 | tf_op jit(solution)/shard_map/ppermute | solution.py:577
  4.3 26.1 %collective-permute-start.1 = (f32[9,16,128]{2,1,0:T(8,128)}, f32[9,16,128]{2,1,0:T(8,128)S(1)}, u32[]{:S(2)}, u32[]{:S(2)}) collective-permute-start(f32[9,16,128]{2,1,0:T(8,128)} %get-tuple-element.18), channel_id=1, source_target_pairs={{32,64},{96,128},{160,192},{64,32},{128,96},{192,160},{33,65},{97,... | collective-permute-start | bytes 221192 | tf_op jit(solution)/shard_map/ppermute | solution.py:577
  5.0 25.4 %collective-permute-start.2 = (f32[9,4,128]{2,1,0:T(4,128)}, f32[9,4,128]{2,1,0:T(4,128)S(1)}, u32[]{:S(2)}, u32[]{:S(2)}) collective-permute-start(f32[9,4,128]{2,1,0:T(4,128)} %get-tuple-element.19), channel_id=1, source_target_pairs={{0,1},{1,0},{2,3},{3,2},{4,5},{5,4},{6,7},{7,6},{8,9},{9,8},{10,11... | collective-permute-start | bytes 55304 | tf_op jit(solution)/shard_map/ppermute | solution.py:577
  6.0 24.4 %collective-permute-start.3 = (f32[9,4,128]{2,1,0:T(4,128)}, f32[9,4,128]{2,1,0:T(4,128)S(1)}, u32[]{:S(2)}, u32[]{:S(2)}) collective-permute-start(f32[9,4,128]{2,1,0:T(4,128)} %get-tuple-element.20), channel_id=1, source_target_pairs={{1,2},{3,4},{5,6},{7,8},{9,10},{11,12},{13,14},{15,16},{17,18},{19... | collective-permute-start | bytes 55304 | tf_op jit(solution)/shard_map/ppermute | solution.py:577
  38.1 2.0 %collective-permute-start.4 = (bf16[16,136,128]{2,1,0:T(8,128)(2,1)S(1)}, bf16[16,136,128]{2,1,0:T(8,128)(2,1)S(1)}, u32[]{:S(2)}, u32[]{:S(2)}) collective-permute-start(bf16[16,136,128]{2,1,0:T(8,128)(2,1)S(1)} %get-tuple-element.22), channel_id=1, source_target_pairs={{0,1},{1,0},{2,3},{3,2},{4,5},{5,4},{6,7},{7,6},{8,9},{9,8},{10,11... | collective-permute-start | bytes 1671176 | tf_op jit(solution)/shard_map/ppermute | solution.py:577
  90.1 5.5 %collective-permute-start.5 = (bf16[16,136,128]{2,1,0:T(8,128)(2,1)S(1)}, bf16[16,136,128]{2,1,0:T(8,128)(2,1)S(1)}, u32[]{:S(2)}, u32[]{:S(2)}) collective-permute-start(bf16[16,136,128]{2,1,0:T(8,128)(2,1)S(1)} %all_to_all.17.own_ref), channel_id=1, source_target_pairs={{0,1},{1,0},{2,3},{3,2},{4,5},{5,4},{6,7},{7,6},{8,9},{9,8},{10,11... | collective-permute-start | bytes 1671176 | tf_op jit(solution)/shard_map/ppermute | solution.py:577

commit v7 on v6

--- a/solution.py
+++ b/solution.py
@@ -73,9 +73,9 @@
 
 
 def sketch_body(
-    basis_hbm, rhs_ref, co_hbm, rows_hbm, signs_hbm, acc_hbm, bt_hbm,
-    pad, terms, hashes, terms_b, hashes_b, source_ref, slots, basis_ref, co_ref, rows_ref, signs_ref, bt_ref, acc_ref,
-    sems, out_sems, slab_sems,
+    basis_hbm, rhs_ref, co_hbm, rows_hbm, signs_hbm, acc_ref, bt_hbm,
+    pad, terms, hashes, terms_b, hashes_b, source_ref, slots, basis_ref, co_ref, rows_ref, signs_ref, bt_ref,
+    sems, slab_sems,
 ):
     fetches = [
         pltpu.make_async_copy(src, dst, sems.at[i])
@@ -168,13 +168,9 @@
             if x + 1 < NX:
                 for d in range(4):
                     build(x + 1, i * 4 + d, *buffers[(x + 1) % 2])
-            else:
-                pltpu.make_async_copy(acc_ref.at[i], acc_hbm.at[i], out_sems.at[i]).start()
             return 0
 
         lax.fori_loop(0, M // PART, block, 0)
-    for i in range(M // PART):
-        pltpu.make_async_copy(acc_ref.at[i], acc_hbm.at[i], out_sems.at[i]).wait()
     give.wait()
 
 
@@ -184,9 +180,9 @@
     return pl.pallas_call(
         sketch_body,
         in_specs=[hbm, vm, hbm, hbm, hbm],
-        out_specs=(hbm, hbm),
+        out_specs=(vm, hbm),
         out_shape=(
-            jax.ShapeDtypeStruct((M // PART, TALL, PART), f32),
+            pltpu.VMEM((M // PART, TALL, PART), f32),
             jax.ShapeDtypeStruct((NX, NY, K, NZ), bf16),
         ),
         scratch_shapes=[
@@ -202,9 +198,7 @@
             pltpu.VMEM((NNZ, NX, NY, NZ), jnp.int32),
             pltpu.VMEM((NNZ, NX, NY, NZ), jnp.int32),
             pltpu.VMEM((NX, NY, K, NZ), bf16),
-            pltpu.VMEM((M // PART, TALL, PART), f32),
             pltpu.SemaphoreType.DMA((5,)),
-            pltpu.SemaphoreType.DMA((M // PART,)),
             pltpu.SemaphoreType.DMA((K // 16,)),
         ],
         compiler_params=pltpu.CompilerParams(vmem_limit_bytes=56 << 20),
@@ -245,12 +239,11 @@
 
 
 def edge_body(
-    ids_ref, acc_hbm, bxl_ref, bxu_ref, byl_ref, byu_ref, xl_ref, xu_ref, yl_ref, yu_ref,
-    own_ref, other_ref, acc, terms, hashes, slots, sem,
+    ids_ref, acc_in, bxl_ref, bxu_ref, byl_ref, byu_ref, xl_ref, xu_ref, yl_ref, yu_ref,
+    own_ref, other_ref, acc, terms, hashes, slots,
 ):
-    fetch = pltpu.make_async_copy(acc_hbm, acc, sem.at[0])
-    fetch.start()
     put_slots(slots)
+    acc[...] = acc_in[...]
 
     def one(info, v, y_info, place):
         terms[place] = (-info[2 * NNZ, pl.ds(y_info, 1), :] * v.astype(f32)).astype(bf16)
@@ -269,8 +262,6 @@
 
         lax.fori_loop(0, NY, group, 0, unroll=2)
         got = nt(side_by_side(terms, NY), side_by_side(hashes, NY))
-        if n == 0:
-            fetch.wait()
         for n in range(M // PART):
             acc[n, K:2 * K, :] += got[:, n * PART:(n + 1) * PART]
 
@@ -311,7 +302,7 @@
         num_scalar_prefetch=1,
         grid=(1,),
         in_specs=[
-            pl.BlockSpec(memory_space=pl.ANY),
+            vm,
             pl.BlockSpec((1, NY, K, NZ), lambda i, ids: (ids[2], 0, 0, 0)),
             pl.BlockSpec((1, NY, K, NZ), lambda i, ids: (NX - 1 - ids[2], 0, 0, 0)),
             pl.BlockSpec((NX, 1, K, NZ), lambda i, ids: (0, ids[3], 0, 0)),
@@ -327,7 +318,6 @@
             pltpu.VMEM((NY, K, NZ), bf16),
             pltpu.VMEM((NY, M, NZ), bf16),
             pltpu.VMEM((ROWS, NZ), bf16),
-            pltpu.SemaphoreType.DMA((1,)),
         ],
         ),
         out_shape=(
@@ -587,7 +577,7 @@
         swapped(y_second, WIDE, [(i, i + 1) for i in range(1, 31, 2)]),
     ]
     acc, bt = sketch(basis, rhs, coeffs, rows, signs)
-    own, other = edges(ids, acc, bt, infos)
+    own, other = edges(ids, near(acc), bt, infos)
     parts = merge(near(own), swapped(other, "core", pair))
     parts = near(lax.all_to_all(parts, FACE, 0, 0, tiled=True))
     parts = near(lax.all_to_all(first(ids, params, parts), DEPTH, 0, 0, tiled=True))

time: 108 us -> 107 us (level)
  no operation moved by 1% of the time
where the time goes in v7:
time: 107 us
  blocking collectives  48.7 us (46%)
  Pallas kernels  41.2 us (39%)
  starting transfers between devices  13 us (12%)
  waiting for transfers between devices  3.54 us (3%)
    all_to_all x1, blocking collectives, per_device(): parts = near(lax.all_to_all(parts, FACE, 0, 0, tiled=True))  22.5 us
    pallas_call x1, Pallas kernels, sketch(): pl.pallas_call(sketch_body, in_specs=[hbm, vm, hbm, hbm, hbm], out_specs=...  18.7 us
    all_to_all x1, blocking collectives, per_device(): lax.all_to_all(first(ids, params, parts), DEPTH, 0, 0, tiled=True)  14 us
    ppermute x6, starting transfers between devices, swapped(): return near(lax.ppermute(value, axes, pairs + [(j, i) for i, j in pairs]))  13 us
    all_to_all x1, blocking collectives, per_device(): mine = lax.all_to_all(second(parts), FACE, 0, 0, tiled=True)  12.2 us
    pallas_call x1, Pallas kernels, finish(): pl.pallas_call(finish_body, in_specs=[pl.BlockSpec(memory_space=pltpu.SME...  11.6 us
    pallas_call x1, Pallas kernels, edges(): pl.pallas_call(edge_body, grid_spec=pltpu.PrefetchScalarGridSpec(num_scal...  7.87 us
    ppermute x6, waiting for transfers between devices, swapped(): return near(lax.ppermute(value, axes, pairs + [(j, i) for i, j in pairs]))  3.54 us
  transfers between devices with their start and end apart: 6, of which 2 were waited for; matrix products, arithmetic and copies ran while one was open for 0% of the time, Pallas kernels for 18%

profile of v7, /device:TPU:1, one launch (start us, length us, event | category | flops | bytes accessed | tf_op | source)
XLA Modules:
  0.0 106.7 jit_solution(6192951176807812542)
XLA Ops:
  0.0 1.7 %planes.1 = (f32[9,16,128]{2,1,0:T(8,128)}, f32[9,16,128]{2,1,0:T(8,128)}, f32[9,4,128]{2,1,0:T(4,128)}, f32[9,4,128]{2,1,0:T(4,128)}, s32[4]{0:T(128)}) custom-call(s32[4,4,16,128]{3,2,1,0:T(8,128)} %rows_hbm.1, s32[4,4,16,128]{3,2,1,0:T(8,128)} %signs_hbm.1, f32[4,4,16,128]{3,2,1,0:T(8,128)} %co_hbm.1), custom_call_target="tpu_custom_call" | custom-call | tf_op jit(solution)/shard_map/planes/pallas_call | solution.py:232
  1.7 2.5 %collective-permute-start = (f32[9,16,128]{2,1,0:T(8,128)}, f32[9,16,128]{2,1,0:T(8,128)S(1)}, u32[]{:S(2)}, u32[]{:S(2)}) collective-permute-start(f32[9,16,128]{2,1,0:T(8,128)} %get-tuple-element.17), channel_id=1, source_target_pairs={{0,32},{32,0},{1,33},{33,1},{2,34},{34,2},{3,35},{35,3},{4,36},{36... | collective-permute-start | bytes 221192 | tf_op jit(solution)/shard_map/ppermute | solution.py:567
  4.3 0.7 collective-permute-start.1
  4.9 1.0 collective-permute-start.2
  6.0 4.8 %collective-permute-start.3 = (f32[9,4,128]{2,1,0:T(4,128)}, f32[9,4,128]{2,1,0:T(4,128)S(1)}, u32[]{:S(2)}, u32[]{:S(2)}) collective-permute-start(f32[9,4,128]{2,1,0:T(4,128)} %get-tuple-element.20), channel_id=1, source_target_pairs={{1,2},{3,4},{5,6},{7,8},{9,10},{11,12},{13,14},{15,16},{17,18},{19... | collective-permute-start | bytes 55304 | tf_op jit(solution)/shard_map/ppermute | solution.py:567
  10.8 18.7 %sketch.1 = (f32[4,528,256]{2,1,0:T(8,128)S(1)}, bf16[4,16,128,128]{3,2,1,0:T(8,128)(2,1)}) custom-call(bf16[128,4,16,128]{3,2,1,0:T(8,128)(2,1)} %basis_hbm.1, bf16[4,16,128]{2,1,0:T(8,128)(2,1)} %rhs_ref.1, f32[4,4,16,128]{3,2,1,0:T(8,128)} %co_hbm.1, s32[4,4,16,128]{3,2,1,0:T(8,128)} %rows_hbm.1, s32[4,4,16,128]{3,2,1,0:T(8,128)} %signs_hbm.1), custom_call_target="tpu_custom_call" | custom-call | tf_op jit(solution)/shard_map/sketch/pallas_call | solution.py:180
  29.5 0.0 collective-permute-done.2.yl_ref
  29.5 0.0 collective-permute-done.3.yu_ref
  29.5 0.0 collective-permute-done.xl_ref
  29.5 0.0 collective-permute-done.1.xu_ref
  29.6 7.9 %edges.1 = (f32[16,136,128]{2,1,0:T(8,128)S(1)}, bf16[16,136,128]{2,1,0:T(8,128)(2,1)S(1)}) custom-call(s32[4]{0:T(128)} %get-tuple-element.14.ids_ref, f32[4,528,256]{2,1,0:T(8,128)S(1)} %get-tuple-element.15.acc_in, bf16[4,16,128,128]{3,2,1,0:T(8,128)(2,1)} %get-tuple-element.16.bxl_ref.bxu_ref.byl_ref.byu_ref.bt_hbm, ...), custom_call_target="tpu_custom_call" | custom-call | tf_op jit(solution)/shard_map/edges/pallas_call | solution.py:299
  37.4 0.1 collective-permute-start.4
  37.5 1.9 %collective-permute-done.4.got_ref = bf16[16,136,128]{2,1,0:T(8,128)(2,1)S(1)} collective-permute-done((bf16[16,136,128]{2,1,0:T(8,128)(2,1)S(1)}, bf16[16,136,128]{2,1,0:T(8,128)(2,1)S(1)}, u32[]{:S(2)}, u32[]{:S(2)}) %collective-permute-start.4) | collective-permute-done | bytes 557088 | tf_op jit(solution)/shard_map/ppermute | solution.py:567
  39.5 0.4 merge.1
  39.9 22.5 %all_to_all.15.parts_ref = bf16[16,136,128]{2,1,0:T(8,128)(2,1)S(1)} all-to-all(bf16[16,136,128]{2,1,0:T(8,128)(2,1)S(1)} %merge.1), channel_id=1, replica_groups=mesh['x'=4,'zl'=2,'y'=4,'zh'=4,'core'=2] {'x','y'}, dimensions={0} | all-to-all | bytes 1114112 | tf_op jit(solution)/shard_map/all_to_all | solution.py:582
  62.4 0.8 first.1
  63.1 14.0 %all_to_all.16.parts_ref = bf16[8,136,128]{2,1,0:T(8,128)(2,1)S(1)} all-to-all(bf16[8,136,128]{2,1,0:T(8,128)(2,1)S(1)} %first.1), channel_id=1, replica_groups=mesh['x'=4,'zl'=2,'y'=4,'zh'=4,'core'=2] {'zl','zh'}, dimensions={0} | all-to-all | bytes 557056 | tf_op jit(solution)/shard_map/all_to_all | solution.py:583
  77.1 0.1 second.1
  77.2 12.2 %all_to_all.17.own_ref = bf16[16,136,128]{2,1,0:T(8,128)(2,1)S(1)} all-to-all(bf16[16,136,128]{2,1,0:T(8,128)(2,1)S(1)} %second.1), channel_id=1, replica_groups=mesh['x'=4,'zl'=2,'y'=4,'zh'=4,'core'=2] {'x','y'}, dimensions={0} | all-to-all | bytes 1114112 | tf_op jit(solution)/shard_map/all_to_all | solution.py:584
  89.4 3.9 %collective-permute-start.5 = (bf16[16,136,128]{2,1,0:T(8,128)(2,1)S(1)}, bf16[16,136,128]{2,1,0:T(8,128)(2,1)S(1)}, u32[]{:S(2)}, u32[]{:S(2)}) collective-permute-start(bf16[16,136,128]{2,1,0:T(8,128)(2,1)S(1)} %all_to_all.17.own_ref), channel_id=1, source_target_pairs={{0,1},{1,0},{2,3},{3,2},{4,5},{5,4},{6,7},{7,6},{8,9},{9,8},{10,11... | collective-permute-start | bytes 1671176 | tf_op jit(solution)/shard_map/ppermute | solution.py:567
  93.3 1.6 %collective-permute-done.5.other_ref = bf16[16,136,128]{2,1,0:T(8,128)(2,1)S(1)} collective-permute-done((bf16[16,136,128]{2,1,0:T(8,128)(2,1)S(1)}, bf16[16,136,128]{2,1,0:T(8,128)(2,1)S(1)}, u32[]{:S(2)}, u32[]{:S(2)}) %collective-permute-start.5) | collective-permute-done | bytes 557088 | tf_op jit(solution)/shard_map/ppermute | solution.py:567
  94.9 11.6 %finish.1 = bf16[256,4,16,128]{3,2,1,0:T(8,128)(2,1)} custom-call(s32[4]{0:T(128)} %get-tuple-element.14.ids_ref, bf16[16,136,128]{2,1,0:T(8,128)(2,1)S(1)} %all_to_all.17.own_ref, bf16[16,136,128]{2,1,0:T(8,128)(2,1)S(1)} %collective-permute-done.5.other_ref, s32[1,256]{1,0:T(1,128)} %bitcast.1, ...), custom_call_target="tpu_custom_call" | custom-call | tf_op jit(solution)/shard_map/finish/pallas_call | solution.py:531
Async XLA Ops:
  1.7 27.8 %collective-permute-start = (f32[9,16,128]{2,1,0:T(8,128)}, f32[9,16,128]{2,1,0:T(8,128)S(1)}, u32[]{:S(2)}, u32[]{:S(2)}) collective-permute-start(f32[9,16,128]{2,1,0:T(8,128)} %get-tuple-element.17), channel_id=1, source_target_pairs={{0,32},{32,0},{1,33},{33,1},{2,34},{34,2},{3,35},{35,3},{4,36},{36... | collective-permute-start | bytes 221192 | tf_op jit(solution)/shard_map/ppermute | solution.py:567
  4.3 25.3 %collective-permute-start.1 = (f32[9,16,128]{2,1,0:T(8,128)}, f32[9,16,128]{2,1,0:T(8,128)S(1)}, u32[]{:S(2)}, u32[]{:S(2)}) collective-permute-start(f32[9,16,128]{2,1,0:T(8,128)} %get-tuple-element.18), channel_id=1, source_target_pairs={{32,64},{96,128},{160,192},{64,32},{128,96},{192,160},{33,65},{97,... | collective-permute-start | bytes 221192 | tf_op jit(solution)/shard_map/ppermute | solution.py:567
  4.9 24.6 %collective-permute-start.2 = (f32[9,4,128]{2,1,0:T(4,128)}, f32[9,4,128]{2,1,0:T(4,128)S(1)}, u32[]{:S(2)}, u32[]{:S(2)}) collective-permute-start(f32[9,4,128]{2,1,0:T(4,128)} %get-tuple-element.19), channel_id=1, source_target_pairs={{0,1},{1,0},{2,3},{3,2},{4,5},{5,4},{6,7},{7,6},{8,9},{9,8},{10,11... | collective-permute-start | bytes 55304 | tf_op jit(solution)/shard_map/ppermute | solution.py:567
  6.0 23.5 %collective-permute-start.3 = (f32[9,4,128]{2,1,0:T(4,128)}, f32[9,4,128]{2,1,0:T(4,128)S(1)}, u32[]{:S(2)}, u32[]{:S(2)}) collective-permute-start(f32[9,4,128]{2,1,0:T(4,128)} %get-tuple-element.20), channel_id=1, source_target_pairs={{1,2},{3,4},{5,6},{7,8},{9,10},{11,12},{13,14},{15,16},{17,18},{19... | collective-permute-start | bytes 55304 | tf_op jit(solution)/shard_map/ppermute | solution.py:567
  37.4 2.0 %collective-permute-start.4 = (bf16[16,136,128]{2,1,0:T(8,128)(2,1)S(1)}, bf16[16,136,128]{2,1,0:T(8,128)(2,1)S(1)}, u32[]{:S(2)}, u32[]{:S(2)}) collective-permute-start(bf16[16,136,128]{2,1,0:T(8,128)(2,1)S(1)} %get-tuple-element.22), channel_id=1, source_target_pairs={{0,1},{1,0},{2,3},{3,2},{4,5},{5,4},{6,7},{7,6},{8,9},{9,8},{10,11... | collective-permute-start | bytes 1671176 | tf_op jit(solution)/shard_map/ppermute | solution.py:567
  89.4 5.5 %collective-permute-start.5 = (bf16[16,136,128]{2,1,0:T(8,128)(2,1)S(1)}, bf16[16,136,128]{2,1,0:T(8,128)(2,1)S(1)}, u32[]{:S(2)}, u32[]{:S(2)}) collective-permute-start(bf16[16,136,128]{2,1,0:T(8,128)(2,1)S(1)} %all_to_all.17.own_ref), channel_id=1, source_target_pairs={{0,1},{1,0},{2,3},{3,2},{4,5},{5,4},{6,7},{7,6},{8,9},{9,8},{10,11... | collective-permute-start | bytes 1671176 | tf_op jit(solution)/shard_map/ppermute | solution.py:567
